TPU v7x, 32 devices: a whole 2x2x4 slice. The times are simulated.
32 devices in a mesh: row: 8 (over z, y), col: 4 (over x, core).
Axes of the slice: x: 2, y: 2, z: 4, core: 2. Of those that a mesh axis runs over, the one named last changes fastest.
Arguments:
- panel_col: float32 [16384, 256], P('row', 'col'), may hold values from -6 to 6
- look_cols: float32 [16384, 2048], P('row', 'col'), may hold values from -6 to 6
- sketch_map: float32 [256, 16384], P(None, 'row'), may hold values from -0.046875 to 0.046875
- upper_inv: float32 [256, 256], replicated, may hold values from -0.09375 to 0.09375
- lower_inv: float32 [256, 256], replicated, may hold values from -0.375 to 0.375
- pivots: int32 [256], replicated, may hold values from 256 to 16383, as said below
Outputs:
- l_panel: float32 [16384, 256], P('row', 'col')
- updated: float32 [16384, 2048], P('row', 'col')
- sketch: float32 [256, 256], P(None, 'col')
Inputs may be any that keep to these rules, and one draw needn't show every extreme that they name: `pivots`: distinct rows, none of them among the first 256.
All inputs are finite; a program needn't handle non-finite values.
Results may differ from a plain program's by a relative error of at most 0.000073.
Values sent between devices are 32-bit elements; how exact they have to be, the bound alone decides.
No kernel may reach another device: no remote copies, remote signals or barrier semaphores. Data moves between devices by JAX's collectives and lax.ppermute only.
A program may use at most 64 MiB of HBM per device.

v0:
```python
import jax
import jax.numpy as jnp
from jax import lax
from jax.sharding import PartitionSpec as P

high_prec = lax.Precision.HIGHEST


def on_device(panel_col, look_cols, sketch_map, upper_inv, lower_inv, pivots):
    row_count = panel_col.shape[0]
    col_width = panel_col.shape[1]
    block_size = upper_inv.shape[0]
    col_index = lax.axis_index("col")
    row_index = lax.axis_index("row")
    first_row = row_index * row_count
    owned = (pivots >= first_row) & (pivots < first_row + row_count)
    local_idx = jnp.where(owned, pivots - first_row, 0)
    owned_mask = owned[:, None]
    panel_pick = jnp.where(owned_mask, panel_col[local_idx], 0.0)
    look_pick = jnp.where(owned_mask, look_cols[local_idx], 0.0)
    sketch_part = jnp.dot(
        sketch_map, panel_col, precision=high_prec, preferred_element_type=jnp.float32
    )
    on_root = row_index == 0
    panel_head = jnp.where(on_root, panel_col[:block_size], 0.0)
    look_head = jnp.where(on_root, look_cols[:block_size], 0.0)
    sketch, panel_piv, look_piv, panel_orig, look_orig = lax.psum(
        (sketch_part, panel_pick, look_pick, panel_head, look_head), "row"
    )
    target = jnp.where(owned, pivots - first_row, row_count)
    swapped_panel = panel_col.at[target].set(panel_orig, mode="drop")
    swapped_look = look_cols.at[target].set(look_orig, mode="drop")
    swapped_panel = jnp.where(on_root, swapped_panel.at[:block_size].set(panel_piv), swapped_panel)
    swapped_look = jnp.where(on_root, swapped_look.at[:block_size].set(look_piv), swapped_look)
    upper_tri = jnp.triu(upper_inv)
    lower_tri = jnp.tril(lower_inv, -1) + jnp.eye(block_size, dtype=jnp.float32)
    factor = jnp.dot(
        lax.all_gather(swapped_panel, "col", axis=1, tiled=True),
        upper_tri,
        precision=high_prec,
        preferred_element_type=jnp.float32,
    )
    global_row = first_row + jnp.arange(row_count, dtype=jnp.int32)
    is_top = (global_row < block_size)[:, None]
    my_factor = lax.dynamic_slice_in_dim(factor, col_index * col_width, col_width, 1)
    l_panel = jnp.where(is_top, swapped_panel, my_factor)
    u_rows = jnp.dot(lower_tri, look_piv, precision=high_prec, preferred_element_type=jnp.float32)
    updated = swapped_look - jnp.dot(
        factor, u_rows, precision=high_prec, preferred_element_type=jnp.float32
    )
    updated = jnp.where(on_root, updated.at[:block_size].set(u_rows), updated)
    return (l_panel, updated, sketch)


def solution(mesh):
    placed = (P("row", "col"), P("row", "col"), P(None, "row"), P(), P(), P())
    return jax.shard_map(
        on_device,
        mesh=mesh,
        in_specs=placed,
        out_specs=(P("row", "col"), P("row", "col"), P(None, "col")),
        check_vma=False,
    )
```

profile of v0, /device:TPU:0, one launch (start us, length us, event | category | flops | bytes accessed | tf_op | source)
XLA Modules:
  0.0 155.1 jit_solution(2442636134449940187)
XLA Ops:
  7.2 0.0 copy-start
  7.2 0.0 all-reduce.3.cloned.1.call-start
  7.2 4.8 %copy.28 = f32[2048,512]{1,0:T(8,128)} copy(f32[2048,512]{1,0:T(8,128)} %param.13) | data formatting | bytes 8388608
  12.1 1.4 copy.11
  13.5 3.7 %fusion.15 = f32[256,64]{0,1:T(8,128)} fusion(f32[256,2048]{1,0:T(8,128)S(1)} %copy-done, f32[2048,64]{0,1:T(8,128)} %param.12), kind=kOutput, calls=%fused_computation.36 | convolution fusion | flops 402653184 | bytes 2686976 | tf_op jit(solution)/shard_map/dot_general | solution.py:21
  17.2 0.7 gather_fusion
  17.9 0.1 copy.14
  18.0 4.2 %gather_fusion.1 = f32[256,512]{1,0:T(8,128)} fusion(f32[2048,512]{1,0:T(8,128)} %copy.28, s32[1024]{0:T(1024)S(1)} %pad_clamp_fusion), kind=kCustom, calls=%fused_computation.1 | custom fusion | bytes 1049600 | tf_op jit(solution)/shard_map/gather | solution.py:20
  22.2 1.5 slice_select_fusion.4
  23.6 2.2 %slice_select_fusion.2 = (f32[256,512]{1,0:T(8,128)}, f32[256,512]{1,0:T(8,128)}) fusion(f32[2048,512]{1,0:T(8,128)} %copy.28, pred[]{:T(512)S(6)} %eq.6, f32[256,512]{1,0:T(8,128)} %gather_fusion.1, pred[256]{0:T(512)(128)(4,1)S(1)} %compare_and_fusion), kind=kLoop, calls=%fused_computation.9 | loop fusion | flops 262144 | bytes 2097409 | tf_op jit(solution)/shard_map/jit(_where)/select_n | solution.py:26
  25.9 0.0 all-reduce.3.cloned.1.call-update
  25.9 0.0 all-gather.2.cloned.1.call-start
  25.9 85.5 %all-reduce.3.cloned.1.call-done = (f32[256,64]{0,1:T(8,128)}, f32[256,64]{0,1:T(8,128)}, f32[256,512]{1,0:T(8,128)}, f32[256,512]{1,0:T(8,128)}, f32[256,64]{0,1:T(8,128)}) async-done(((f32[256,64]{0,1:T(8,128)}, f32[256,64]{0,1:T(8,128)}, f32[256,512]{1,0:T(8,128)}, f32[256,512]{1,0:T(8,128)}, f32[256,64]{0,1:T(8,128)}), (f32[256,64]{0,1:T(8,128)}, f32[256,64]{0,1:T(8,128)}, f32[256,512]{1,0:T(8,128)}, ...) | async-done | bytes 1245200 | tf_op jit(solution)/shard_map/psum | solution.py:27
  111.5 0.9 copy.12
  112.4 1.6 %scatter_fusion = f32[2048,64]{1,0:T(8,128)S(1)} fusion(f32[2048,64]{1,0:T(8,128)S(1)} %copy.11, s32[256]{0:T(256)S(1)} %get-tuple-element.45, f32[256,64]{1,0:T(8,128)S(1)} %copy.12), kind=kCustom, calls=%fused_computation.2 | custom fusion | bytes 197632 | tf_op jit(solution)/shard_map/scatter | solution.py:31
  114.0 1.1 copy.16
  115.1 1.5 fusion.12
  116.6 0.0 all-gather.2.cloned.1.call-update
  116.7 0.0 copy-start.5
  116.7 6.1 %scatter_fusion.1 = f32[2048,512]{1,0:T(8,128)} fusion(f32[2048,512]{1,0:T(8,128)} %copy.28, s32[256]{0:T(256)S(1)} %get-tuple-element.45, f32[256,512]{1,0:T(8,128)} %get-tuple-element.41), kind=kCustom, calls=%fused_computation.3 | custom fusion | bytes 1573888 | tf_op jit(solution)/shard_map/scatter | solution.py:32
  122.8 1.6 %fusion.2 = f32[256,512]{1,0:T(8,128)S(1)} fusion(f32[256,512]{1,0:T(8,128)S(1)} %copy-done.4, f32[256,256]{1,0:T(8,128)} %param.16, s32[256]{0:T(256)S(1)} %iota_add_fusion), kind=kOutput, calls=%fused_computation.11 | convolution fusion | flops 402980864 | bytes 1311744 | tf_op jit(solution)/shard_map/dot_general | solution.py:47
  124.4 1.9 %fusion.1 = f32[2048,512]{1,0:T(8,128)} fusion(f32[2048,512]{1,0:T(8,128)} %scatter_fusion.1, f32[256,512]{1,0:T(8,128)S(1)} %copy-done.4, pred[]{:T(512)S(6)} %eq.6), kind=kLoop, calls=%fused_computation.8 | loop fusion | flops 131072 | bytes 1572865 | tf_op jit(solution)/shard_map/jit(_where)/select_n | solution.py:34
  126.4 12.0 %all-gather.2.cloned.1.call-done = f32[2048,256]{0,1:T(8,128)} async-done(((f32[2048,64]{0,1:T(8,128)}), f32[2048,256]{0,1:T(8,128)}) %all-gather.2.cloned.1.call-update) | async-done | bytes 2097168 | tf_op jit(solution)/shard_map/all_gather | solution.py:38
  138.4 3.8 %fusion.6 = f32[2048,256]{0,1:T(8,128)S(1)} fusion(f32[2048,256]{0,1:T(8,128)} %all-gather.2.cloned.1.call-done, f32[256,256]{1,0:T(8,128)S(1)} %copy-done.5, s32[256]{0:T(256)S(1)} %iota_add_fusion), kind=kOutput, calls=%fused_computation.17 | convolution fusion | flops 1610743808 | bytes 4457472 | tf_op jit(solution)/shard_map/dot_general | solution.py:37
  142.2 0.0 copy-done.1
  142.2 0.0 copy-start.3
  142.2 3.7 %convolution_subtract_fusion = f32[2048,512]{1,0:T(8,128)S(1)} fusion(f32[2048,512]{1,0:T(8,128)S(1)} %copy-done.1, f32[2048,256]{0,1:T(8,128)S(1)} %fusion.6, f32[256,512]{1,0:T(8,128)S(1)} %fusion.2), kind=kOutput, calls=%fused_computation.4 | convolution fusion | flops 3222274048 | bytes 11010048 | tf_op jit(solution)/shard_map/dot_general | solution.py:48
  145.9 0.1 fusion
  146.1 0.0 copy-start.2
  146.1 0.9 dynamic-slice_select_fusion
  147.0 1.2 copy.29
  148.3 0.0 copy-done.2
  (15 shorter events, 0.1 us)
Async XLA Ops:
  7.2 6.3 %copy-start = (f32[256,2048]{1,0:T(8,128)S(1)}, f32[256,2048]{1,0:T(8,128)}, u32[]{:S(2)}) copy-start(f32[256,2048]{1,0:T(8,128)} %param.14) | copy-start | bytes 6291460
  7.2 4.8 %copy-start.7 = (s32[256]{0:T(256)S(1)}, s32[256]{0:T(256)}, u32[]{:S(2)}) copy-start(s32[256]{0:T(256)} %param.17) | copy-start | bytes 3076
  7.2 104.3 %all-reduce.3.cloned.1.call-start = ((), (), s32[]{:S(2)}) async-start(), calls=%async_computation.1 | async-start | bytes 2490368 | tf_op jit(solution)/shard_map/psum | solution.py:27
  25.9 112.5 %all-gather.2.cloned.1.call-start = ((), (), s32[]{:S(2)}) async-start(), calls=%async_computation | async-start | bytes 2621440 | tf_op jit(solution)/shard_map/all_gather | solution.py:38
  116.7 6.2 %copy-start.4 = (f32[256,512]{1,0:T(8,128)S(1)}, f32[256,512]{1,0:T(8,128)}, u32[]{:S(2)}) copy-start(f32[256,512]{1,0:T(8,128)} %get-tuple-element.42) | copy-start | bytes 1572868
  116.7 21.7 %copy-start.5 = (f32[256,256]{1,0:T(8,128)S(1)}, f32[256,256]{1,0:T(8,128)}, u32[]{:S(2)}) copy-start(f32[256,256]{1,0:T(8,128)} %param.15) | copy-start | bytes 786436
  138.4 3.8 %copy-start.1 = (f32[2048,512]{1,0:T(8,128)S(1)}, f32[2048,512]{1,0:T(8,128)}, u32[]{:S(2)}) copy-start(f32[2048,512]{1,0:T(8,128)} %fusion.1) | copy-start | bytes 12582916
  142.2 3.9 %copy-start.3 = (f32[2048,64]{0,1:T(8,128)S(1)}, f32[2048,64]{0,1:T(8,128)}, u32[]{:S(2)}) copy-start(f32[2048,64]{0,1:T(8,128)} %fusion.12) | copy-start | bytes 1572868
  142.2 4.8 %copy-start.6 = (f32[256,64]{0,1:T(8,128)S(1)}, f32[256,64]{0,1:T(8,128)}, u32[]{:S(2)}) copy-start(f32[256,64]{0,1:T(8,128)} %get-tuple-element.52) | copy-start | bytes 196612
  146.1 2.2 %copy-start.2 = (f32[2048,512]{1,0:T(8,128)}, f32[2048,512]{1,0:T(8,128)S(1)}, u32[]{:S(2)}) copy-start(f32[2048,512]{1,0:T(8,128)S(1)} %fusion) | copy-start | bytes 12582916
Sparse Core Ops, SparseCore 0:
  26.0 85.4 all-reduce.2
  116.7 21.5 all-gather.1
where the time goes:
time: 156 us; the launch traced here: 155 us
  waiting for transfers between devices  97.6 us (63%)
  local copies, waits for them, and re-layouts  22.2 us (14%)
  between operations  14.2 us (9%)
  matrix products  12.8 us (8%)
  other arithmetic  8.26 us (5%)
    psum x1, waiting for transfers between devices, on_device(): lax.psum((sketch_part, panel_pick, look_pick, panel_head, look_head), 'row')  85.5 us
    all_gather x1, waiting for transfers between devices, on_device(): lax.all_gather(swapped_panel, 'col', axis=1, tiled=True)  12 us
    unnamed x19, local copies, waits for them, and re-layouts  7.44 us
    scatter x1, local copies, waits for them, and re-layouts, on_device(): swapped_look = look_cols.at[target].set(look_orig, mode='drop')  6.15 us
    gather x1, local copies, waits for them, and re-layouts, on_device(): look_pick = jnp.where(owned_mask, look_cols[local_idx], 0.0)  4.19 us
    dot_general x1, matrix products, on_device(): jnp.dot(lax.all_gather(swapped_panel, 'col', axis=1, tiled=True), upper_t...  3.84 us
    dot_general x1, matrix products, on_device(): jnp.dot(sketch_map, panel_col, precision=high_prec, preferred_element_typ...  3.7 us
    dot_general x1, matrix products, on_device(): jnp.dot(factor, u_rows, precision=high_prec, preferred_element_type=jnp.f...  3.67 us
  transfers between devices with their start and end apart: 2, of which 2 were waited for; matrix products, arithmetic and copies ran while one was open for 6% of the time, Pallas kernels for 0%

commit v1 on v0

v1 whole, which is shorter than its diff:
```python
import functools

import jax
import jax.numpy as jnp
from jax import lax
from jax.experimental import pallas as pl
from jax.experimental.pallas import tpu as pltpu
from jax.sharding import PartitionSpec as P

F32, BF16, I32 = jnp.float32, jnp.bfloat16, jnp.int32
GROUP = 4
VMEM = pl.BlockSpec(memory_space=pltpu.VMEM)
SMEM = pl.BlockSpec(memory_space=pltpu.SMEM)
HBM = pl.BlockSpec(memory_space=pl.ANY)


def split2(x):
    hi = x.astype(BF16)
    return hi, (x - hi.astype(F32)).astype(BF16)


def split3(x):
    hi = x.astype(BF16)
    rest = x - hi.astype(F32)
    mid = rest.astype(BF16)
    return hi, mid, (rest - mid.astype(F32)).astype(BF16)


def mm(a, b, dims=((1,), (0,))):
    return lax.dot_general(a, b, (dims, ((), ())), preferred_element_type=F32)


def mm3(a, b, dims=((1,), (0,))):
    return mm(a[0], b[0], dims) + (mm(a[0], b[1], dims) + mm(a[1], b[0], dims))


def pick_kernel(tab, pos, look, panel, sketch_map, target, *rest):
    outs, (owned_list, extra, sem) = rest[:GROUP], rest[GROUP:]
    slots = target.shape[0]
    chunk = slots // GROUP
    extra_rows = extra.shape[0] // GROUP
    q = pos[1]
    nt = ((1,), (1,))
    for s in range(GROUP):
        base = (q ^ s) * chunk

        @pl.loop(0, chunk, unroll=8)
        def _(i, s=s, base=base):
            pltpu.make_async_copy(
                look.at[pl.ds(tab[base + i], 1), :], outs[s].at[pl.ds(i, 1), :], sem.at[s]
            ).start()

    def note(p, count):
        owned_list[count] = p
        return count + tab[slots + p]

    count = lax.fori_loop(0, slots, note, jnp.int32(0), unroll=8)
    owned_list[slots] = count

    width = panel.shape[1]
    step = min(512, width)
    sketch_sum = jnp.zeros((panel.shape[0], sketch_map.shape[0]), F32)
    pick_sum = jnp.zeros((panel.shape[0], slots), F32)
    for k in range(0, width, step):
        hi, mid, lo = split3(panel[:, k : k + step])
        sketch_sum += mm3((hi, mid), split2(sketch_map[:, k : k + step]), nt)
        column = lax.broadcasted_iota(I32, (slots, step), 1) + k
        hot = jnp.where(column == target[...], 1.0, 0.0).astype(BF16)
        pick_sum += (mm(hi, hot, nt) + mm(mid, hot, nt)) + mm(lo, hot, nt)
    split = sketch_map.shape[0]
    extra[:, :split] = sketch_sum
    extra[:, split:] = pick_sum
    for s in range(GROUP):
        rows = pl.ds(pl.multiple_of((q ^ s) * extra_rows, 8), extra_rows)
        outs[s][chunk : chunk + extra_rows, :] = extra[rows, :]
    for s in range(GROUP):
        pltpu.make_async_copy(
            look.at[pl.ds(0, chunk), :], outs[s].at[pl.ds(0, chunk), :], sem.at[s]
        ).wait()


def swap_kernel(panel, head, target, out):
    slots = target.shape[0]
    hi, mid, lo = split3(head[...])
    ones = jnp.ones((16, slots), BF16)
    width = panel.shape[1]
    step = min(512, width)
    for k in range(0, width, step):
        column = lax.broadcasted_iota(I32, (slots, step), 1) + k
        hot = jnp.where(column == target[...], 1.0, 0.0).astype(BF16)
        moved = (mm(hi, hot) + mm(mid, hot)) + mm(lo, hot)
        hit = mm(ones, hot)[:1, :] > 0.5
        out[:, k : k + step] = jnp.where(hit, moved, panel[:, k : k + step])


def factor_kernel(pos, *rest):
    blocks, (upper, upper_own, fac_hi, fac_lo, own_out, whole) = rest[:-6], rest[-6:]
    cw = blocks[0].shape[0]
    for k, block in enumerate(blocks):
        rows = pl.ds(pl.multiple_of((pos[2] ^ k) * cw, 8), cw)
        whole[rows, :] = block[...]
    nb = upper.shape[0]
    keep = lax.broadcasted_iota(I32, (nb, nb), 0) <= lax.broadcasted_iota(I32, (nb, nb), 1)
    tri = split2(jnp.where(keep, upper[...], 0.0))
    data = whole[...]
    fac = mm3(split2(data.T), tri)
    hi, lo = split2(fac)
    fac_hi[...] = hi
    fac_lo[...] = lo
    own_out[...] = mm3(split2(upper_own[...]), split2(data))


def final_kernel(pos, owned_list, tab, look, fac_hi, fac_lo, lower, target, *rest):
    picks, spread = rest[:GROUP], rest[GROUP : 2 * GROUP]
    _, updated, panel_out, sketch_out, buf, piv, got, extra, in_sem, out_sem, top_sem = rest[2 * GROUP :]
    row, q = pos[0], pos[1]
    slots = target.shape[0]
    chunk = slots // GROUP
    rows_dev = buf.shape[0]
    extra_rows = extra.shape[0] // GROUP
    blocks = rows_dev // slots

    def load(b):
        part = pl.ds(b * slots, slots)
        return pltpu.make_async_copy(look.at[part, :], buf.at[part, :], in_sem.at[b])

    def store(b):
        part = pl.ds(b * slots, slots)
        return pltpu.make_async_copy(buf.at[part, :], updated.at[part, :], out_sem.at[b])

    for b in range(blocks):
        load(b).start()
    for s in range(GROUP):
        part = pl.ds(pl.multiple_of((q ^ s) * chunk, 8), chunk)
        mine = target[part, :] >= 0
        there = spread[s][:chunk, :]
        piv[part, :] = jnp.where(mine, picks[s][:chunk, :], there)
        got[part, :] = there
        erows = pl.ds(pl.multiple_of((q ^ s) * extra_rows, 8), extra_rows)
        extra[erows, :] = spread[s][chunk : chunk + extra_rows, :]
    split = sketch_out.shape[1]
    sketch_out[...] = extra[:, :split]

    below = lax.broadcasted_iota(I32, (slots, slots), 0) > lax.broadcasted_iota(I32, (slots, slots), 1)
    low = split2(jnp.where(below, lower[...], 0.0))
    first = piv[...]
    u_rows = first + mm3(low, split2(first))
    u_hi, u_lo = split2(u_rows)

    for b in range(blocks):
        load(b).wait()

    count = owned_list[slots]

    def place(source):
        @pl.loop(0, count)
        def _(k):
            p = owned_list[k]
            buf[pl.ds(tab[p], 1), :] = source[pl.ds(p, 1), :]

    @pl.when(row == 0)
    def _():
        place(buf)

    @pl.when(row != 0)
    def _():
        place(got)

    for b in range(blocks):
        part = pl.ds(b * slots, slots)
        drop = mm3((fac_hi[part, :], fac_lo[part, :]), (u_hi, u_lo))
        new = buf[part, :] - drop
        if b == 0:
            new = jnp.where(row == 0, u_rows, new)
        buf[part, :] = new
        store(b).start()

    top = pltpu.make_async_copy(
        extra.at[:, pl.ds(split, slots)], panel_out.at[:, pl.ds(0, slots)], top_sem
    )

    @pl.when(row == 0)
    def _():
        top.start()
        top.wait()

    for b in range(blocks):
        store(b).wait()


def on_device(n_row, n_col, panel_col, look_cols, sketch_map, upper_inv, lower_inv, pivots):
    rows_dev, cw = panel_col.shape
    lw = look_cols.shape[1]
    nb, ks = upper_inv.shape[0], sketch_map.shape[0]
    chunk, extra_rows = nb // GROUP, cw // GROUP
    assert ks + nb == lw and n_row % GROUP == 0
    assert n_row & (n_row - 1) == 0 and n_col & (n_col - 1) == 0
    row, col = lax.axis_index("row"), lax.axis_index("col")
    q = row % GROUP
    pos = jnp.stack([row, q, col]).astype(I32)
    panel_t = panel_col.T
    owner = pivots // rows_dev
    owned = owner == row
    local = pivots - row * rows_dev
    source = jnp.where(owned, local, jnp.arange(nb, dtype=I32))
    tab = jnp.concatenate([source, owned.astype(I32)])
    target = jnp.where(owned, local, -1)[:, None]

    def across(v, s):
        return lax.ppermute(v, "row", [(i, i ^ s) for i in range(n_row)])

    head = panel_t[:, :nb]
    bit = n_row // 2
    while bit:
        sent = lax.ppermute(head, "row", [(i, i + bit) for i in range(0, n_row, 2 * bit)])
        head = jnp.where(row % (2 * bit) == bit, sent, head)
        bit //= 2

    message = jax.ShapeDtypeStruct((chunk + extra_rows, lw), F32)
    *picks, owned_list = pl.pallas_call(
        pick_kernel,
        out_shape=[message] * GROUP + [jax.ShapeDtypeStruct((nb + 8,), I32)],
        in_specs=[SMEM, SMEM, HBM, VMEM, VMEM, VMEM],
        out_specs=[VMEM] * GROUP + [SMEM],
        scratch_shapes=[pltpu.VMEM((cw, lw), F32), pltpu.SemaphoreType.DMA((GROUP,))],
        cost_estimate=pl.CostEstimate(flops=10**9, bytes_accessed=4 * 10**6, transcendentals=0),
        name="pick",
    )(tab, pos, look_cols, panel_t, sketch_map, target)

    slot_owner = lax.dynamic_slice_in_dim(owner, q * chunk, chunk)
    slot_owner = jnp.concatenate([slot_owner, jnp.full((extra_rows,), -1, I32)])[:, None]
    summed = slot_owner < 0
    got = [picks[0]] + [across(picks[s], s) for s in range(1, GROUP)]
    have = sum(jnp.where(summed | (slot_owner == (row ^ s)), got[s], 0.0) for s in range(GROUP))
    top = got[0]
    for s in range(1, GROUP):
        top = jnp.where(row == s, got[s], top)
    bit = GROUP
    while bit < n_row:
        inside = summed | (slot_owner // bit == row // bit)
        got = across(jnp.where(inside, have, top), bit)
        other = (row // bit) ^ 1
        theirs = slot_owner // bit == other
        have = jnp.where(theirs, 0.0, have) + jnp.where(summed | theirs, got, 0.0)
        top = jnp.where(other == 0, got, top)
        bit *= 2
    spread = [jnp.where(slot_owner == (row ^ s), top, have) for s in range(GROUP)]
    spread = spread[:1] + [across(spread[s], s) for s in range(1, GROUP)]

    swapped = pl.pallas_call(
        swap_kernel,
        out_shape=jax.ShapeDtypeStruct((cw, rows_dev), F32),
        in_specs=[VMEM, VMEM, VMEM],
        out_specs=VMEM,
        cost_estimate=pl.CostEstimate(flops=2 * 10**8, bytes_accessed=10**6, transcendentals=0),
        name="swap",
    )(panel_t, head, target)

    blocks = {0: swapped}
    bit = n_col // 2
    while bit:
        for k in list(blocks):
            blocks[k ^ bit] = lax.ppermute(blocks[k], "col", [(i, i ^ bit) for i in range(n_col)])
        bit //= 2
    blocks = [blocks[k] for k in range(n_col)]
    upper_own = lax.dynamic_slice_in_dim(jnp.triu(upper_inv), col * cw, cw, 1).T

    step = min(nb, rows_dev)
    lane_block = pl.BlockSpec((cw, step), lambda b: (0, b))
    whole_block = lambda shape: pl.BlockSpec(shape, lambda b: (0, 0))
    row_block = pl.BlockSpec((step, nb), lambda b: (b, 0))
    fac_hi, fac_lo, panel_out = pl.pallas_call(
        factor_kernel,
        grid=(rows_dev // step,),
        out_shape=[
            jax.ShapeDtypeStruct((rows_dev, nb), BF16),
            jax.ShapeDtypeStruct((rows_dev, nb), BF16),
            jax.ShapeDtypeStruct((cw, rows_dev), F32),
        ],
        in_specs=[SMEM] + [lane_block] * n_col + [whole_block((nb, nb)), whole_block((cw, nb))],
        out_specs=[row_block, row_block, lane_block],
        scratch_shapes=[pltpu.VMEM((nb, step), F32)],
        cost_estimate=pl.CostEstimate(flops=10**9, bytes_accessed=6 * 10**6, transcendentals=0),
        name="factor",
    )(pos, *blocks, upper_inv, upper_own)

    n_in = 8 + 2 * GROUP
    updated, panel_out, sketch_t = pl.pallas_call(
        final_kernel,
        out_shape=[
            jax.ShapeDtypeStruct((rows_dev, lw), F32),
            jax.ShapeDtypeStruct((cw, rows_dev), F32),
            jax.ShapeDtypeStruct((cw, ks), F32),
        ],
        in_specs=[SMEM, SMEM, SMEM, HBM] + [VMEM] * (4 + 2 * GROUP) + [HBM],
        out_specs=[HBM, HBM, VMEM],
        input_output_aliases={n_in: 1},
        scratch_shapes=[
            pltpu.VMEM((rows_dev, lw), F32),
            pltpu.VMEM((nb, lw), F32),
            pltpu.VMEM((nb, lw), F32),
            pltpu.VMEM((cw, lw), F32),
            pltpu.SemaphoreType.DMA((rows_dev // nb,)),
            pltpu.SemaphoreType.DMA((rows_dev // nb,)),
            pltpu.SemaphoreType.DMA,
        ],
        cost_estimate=pl.CostEstimate(flops=2 * 10**9, bytes_accessed=12 * 10**6, transcendentals=0),
        name="final",
    )(pos, owned_list, tab, look_cols, fac_hi, fac_lo, lower_inv, target, *picks, *spread, panel_out)
    return panel_out.T, updated, sketch_t.T


def solution(mesh):
    placed = (P("row", "col"), P("row", "col"), P(None, "row"), P(), P(), P())
    return jax.shard_map(
        functools.partial(on_device, mesh.shape["row"], mesh.shape["col"]),
        mesh=mesh,
        in_specs=placed,
        out_specs=(P("row", "col"), P("row", "col"), P(None, "col")),
        check_vma=False,
    )
```

time: 156 us -> 69 us (0.44)
  waiting for transfers between devices: 97.6 us -> 10.6 us
  Pallas kernels: 0 us -> 24.4 us
  starting transfers between devices: 0.08 us -> 21.1 us
  local copies, waits for them, and re-layouts: 22.2 us -> 4.19 us
  between operations: 14.2 us -> 0.85 us
  matrix products: 12.8 us -> 0 us
  other arithmetic: 8.26 us -> 6.63 us
    psum x1 -> x0, waiting for transfers between devices: 85.5 us -> none  [on_device(): lax.psum((sketch_part, panel_pick, look_pick, panel_head, look_head), 'row')]
    pallas_call x0 -> x4, Pallas kernels: none -> 24.4 us  [the longest x1 7.58 us: on_device(): pl.pallas_call(final_kernel, out_shape=[jax.ShapeDtypeStruct((rows_dev, l...]
    ppermute x0 -> x13, starting transfers between devices: none -> 21.1 us  [the longest x7 10.2 us: across(): return lax.ppermute(v, 'row', [(i, i ^ s) for i in range(n_row)])]
    dot_general x4 -> x0, matrix products: 12.8 us -> none  [the longest x1 3.84 us: on_device(): jnp.dot(lax.all_gather(swapped_panel, 'col', axis=1, tiled=True), upper_t...]
    all_gather x1 -> x0, waiting for transfers between devices: 12 us -> none  [on_device(): lax.all_gather(swapped_panel, 'col', axis=1, tiled=True)]
    ppermute x0 -> x13, waiting for transfers between devices: none -> 10.6 us  [the longest x3 7.02 us: on_device(): lax.ppermute(blocks[k], 'col', [(i, i ^ bit) for i in range(n_col)])]
    scatter x3 -> x0, local copies, waits for them, and re-layouts: 8.82 us -> none  [the longest x1 6.15 us: on_device(): swapped_look = look_cols.at[target].set(look_orig, mode='drop')]
    unnamed x19 -> x15, local copies, waits for them, and re-layouts: 7.44 us -> 2.38 us
  transfers between devices with their start and end apart: 2 -> 13, of which waited for: 2 -> 2; matrix products, arithmetic and copies ran while one was open for 6% -> 10% of each run, Pallas kernels for 0% -> 25%
where the time goes in v1:
time: 69 us; the launch traced here: 67.8 us
  Pallas kernels  24.4 us (35%)
  starting transfers between devices  21.1 us (31%)
  waiting for transfers between devices  10.6 us (15%)
  other arithmetic  6.63 us (10%)
  local copies, waits for them, and re-layouts  4.19 us (6%)
  between operations  0.85 us (1%)
    ppermute x7, starting transfers between devices, across(): return lax.ppermute(v, 'row', [(i, i ^ s) for i in range(n_row)])  10.2 us
    ppermute x3, starting transfers between devices, on_device(): lax.ppermute(head, 'row', [(i, i + bit) for i in range(0, n_row, 2 * bit)])  9.37 us
    pallas_call x1, Pallas kernels, on_device(): pl.pallas_call(final_kernel, out_shape=[jax.ShapeDtypeStruct((rows_dev, l...  7.58 us
    pallas_call x1, Pallas kernels, on_device(): pl.pallas_call(factor_kernel, grid=(rows_dev // step,), out_shape=[jax.Sh...  7.31 us
    ppermute x3, waiting for transfers between devices, on_device(): lax.ppermute(blocks[k], 'col', [(i, i ^ bit) for i in range(n_col)])  7.02 us
    pallas_call x1, Pallas kernels, on_device(): pl.pallas_call(pick_kernel, out_shape=[message] * GROUP + [jax.ShapeDtype...  6.72 us
    ppermute x3, waiting for transfers between devices, on_device(): lax.ppermute(head, 'row', [(i, i + bit) for i in range(0, n_row, 2 * bit)])  3.58 us
    pallas_call x1, Pallas kernels, on_device(): pl.pallas_call(swap_kernel, out_shape=jax.ShapeDtypeStruct((cw, rows_dev)...  2.8 us
  transfers between devices with their start and end apart: 13, of which 2 were waited for; matrix products, arithmetic and copies ran while one was open for 10% of the time, Pallas kernels for 25%

profile of v1, /device:TPU:0, one launch (start us, length us, event | category | flops | bytes accessed | tf_op | source)
XLA Modules:
  0.0 67.8 jit_solution(6936423308731281944)
XLA Ops:
  0.6 0.8 %slice.4 = f32[64,256]{1,0:T(8,128)S(1)} slice(f32[64,2048]{1,0:T(8,128)} %bitcast.9), slice={[0:64], [0:256]} | slice | bytes 131072 | tf_op jit(solution)/shard_map/slice | solution.py:212
  1.5 6.0 %collective-permute-start = (f32[64,256]{1,0:T(8,128)S(1)}, f32[64,256]{1,0:T(8,128)S(1)}, u32[]{:S(2)}, u32[]{:S(2)}) collective-permute-start(f32[64,256]{1,0:T(8,128)S(1)} %slice.4), channel_id=1, source_target_pairs={{0,16},{1,17},{2,18},{3,19}} | collective-permute-start | bytes 196616 | tf_op jit(solution)/shard_map/ppermute | solution.py:215
  7.5 0.7 %subtract_select_fusion = (s32[256]{0:T(256)S(1)}, pred[256]{0:T(512)(128)(4,1)S(1)}, s32[256]{0:T(256)S(1)}) fusion(s32[256]{0:T(256)} %param.11, s32[]{:T(128)S(6)} %mul.9, s32[]{:T(128)} %axis_index.23), kind=kLoop, calls=%fused_computation.23 | loop fusion | flops 4608 | bytes 3336 | tf_op jit(solution)/shard_map/jit(_where)/select_n | solution.py:207
  8.2 0.7 %iota_select_fusion = s32[256]{0:T(256)S(1)} fusion(pred[256]{0:T(512)(128)(4,1)S(1)} %get-tuple-element.43, s32[256]{0:T(256)} %param.11, s32[]{:T(128)S(6)} %mul.9), kind=kLoop, calls=%fused_computation.22 | loop fusion | flops 512 | bytes 2308 | tf_op jit(solution)/shard_map/jit(_where)/select_n | solution.py:205
  8.8 0.8 %copy.11.target = s32[256,1]{1,0:T(8,128)} copy(s32[256,1]{0,1:T(1,128)S(1)} %bitcast.14) | data formatting | bytes 2048 | tf_op jit(solution)/shard_map/broadcast_in_dim | solution.py:207
  9.6 0.6 pad_add_fusion.tab
  10.2 0.6 pad_add_fusion.1.pos
  10.8 0.8 %broadcast_select_fusion.6 = f32[64,256]{1,0:T(8,128)S(1)} fusion(f32[64,256]{1,0:T(8,128)S(1)} %collective-permute-done, pred[]{:T(512)S(6)} %eq.86, f32[64,2048]{1,0:T(8,128)} %bitcast.10), kind=kLoop, calls=%fused_computation.11 | loop fusion | flops 16384 | bytes 196609 | tf_op jit(solution)/shard_map/jit(_where)/select_n | solution.py:216
  11.7 1.4 %collective-permute-start.1 = (f32[64,256]{1,0:T(8,128)S(1)}, f32[64,256]{1,0:T(8,128)S(1)}, u32[]{:S(2)}, u32[]{:S(2)}) collective-permute-start(f32[64,256]{1,0:T(8,128)S(1)} %broadcast_select_fusion.6), channel_id=1, source_target_pairs={{0,8},{16,24},{1,9},{17,25},{2,10},{18,26},{3,11},{19,27}} | collective-permute-start | bytes 196616 | tf_op jit(solution)/shard_map/ppermute | solution.py:215
  13.1 6.7 %pick.1 = (f32[80,512]{1,0:T(8,128)}, f32[80,512]{1,0:T(8,128)}, f32[80,512]{1,0:T(8,128)}, f32[80,512]{1,0:T(8,128)}, s32[264]{0:T(512)}) custom-call(s32[512]{0:T(512)} %pad_add_fusion.tab, s32[3]{0:T(128)} %pad_add_fusion.1.pos, f32[2048,512]{1,0:T(8,128)} %look.3, f32[64,2048]{1,0:T(8,128)} %bitcast.11, f32[256,2048]{1,0:T(8,128)} %sketch_map.1, ...), custom_call_target="tpu_custom_call" | custom-call | flops 1000000000 | bytes 4000000 | tf_op jit(solution)/shard_map/pick/pallas_call | solution.py:220
  20.0 3.4 %collective-permute-start.8 = (f32[80,512]{1,0:T(8,128)}, f32[80,512]{1,0:T(8,128)S(1)}, u32[]{:S(2)}, u32[]{:S(2)}) collective-permute-start(f32[80,512]{1,0:T(8,128)} %get-tuple-element.20.rest_3_), channel_id=1, source_target_pairs={{0,12},{4,8},{8,4},{12,0},{16,28},{20,24},{24,20},{28,16},{1,13},{... | collective-permute-start | bytes 491528 | tf_op jit(solution)/shard_map/ppermute | solution.py:210
  23.4 0.1 dynamic_slice.7
  23.5 2.0 %collective-permute-start.2 = (f32[64,256]{1,0:T(8,128)S(1)}, f32[64,256]{1,0:T(8,128)S(1)}, u32[]{:S(2)}, u32[]{:S(2)}) collective-permute-start(f32[64,256]{1,0:T(8,128)S(1)} %broadcast_select_fusion.7), channel_id=1, source_target_pairs={{0,4},{8,12},{16,20},{24,28},{1,5},{9,13},{17,21},{25,29},{2,6},{1... | collective-permute-start | bytes 196616 | tf_op jit(solution)/shard_map/ppermute | solution.py:215
  25.5 3.6 %collective-permute-done.2 = f32[64,256]{1,0:T(8,128)S(1)} collective-permute-done((f32[64,256]{1,0:T(8,128)S(1)}, f32[64,256]{1,0:T(8,128)S(1)}, u32[]{:S(2)}, u32[]{:S(2)}) %collective-permute-start.2) | collective-permute-done | bytes 65568 | tf_op jit(solution)/shard_map/ppermute | solution.py:215
  29.1 0.6 broadcast_select_fusion.8.head
  29.7 2.8 %swap.1.rest_0_ = f32[64,2048]{1,0:T(8,128)} custom-call(f32[64,2048]{1,0:T(8,128)} %bitcast.12, f32[64,256]{1,0:T(8,128)} %broadcast_select_fusion.8.head, s32[256,1]{1,0:T(8,128)} %copy.11.target), custom_call_target="tpu_custom_call" | custom-call | flops 200000000 | bytes 1000000 | tf_op jit(solution)/shard_map/swap/pallas_call | solution.py:250
  32.5 1.5 %collective-permute-start.4 = (f32[64,2048]{1,0:T(8,128)}, f32[64,2048]{1,0:T(8,128)S(1)}, u32[]{:S(2)}, u32[]{:S(2)}) collective-permute-start(f32[64,2048]{1,0:T(8,128)} %swap.1.rest_0_), channel_id=1, source_target_pairs={{0,2},{1,3},{2,0},{3,1},{4,6},{5,7},{6,4},{7,5},{8,10},{9,11},{10,... | collective-permute-start | bytes 1572872 | tf_op jit(solution)/shard_map/ppermute | solution.py:263
  34.0 1.0 %broadcast_select_fusion.3 = (f32[80,512]{1,0:T(8,128)S(1)}, f32[80,512]{1,0:T(8,128)S(1)}, f32[80,512]{1,0:T(8,128)S(1)}) fusion(pred[80]{0:T(512)(128)(4,1)S(1)} %compare_or_fusion, f32[80,512]{1,0:T(8,128)S(1)} %collective-permute-done.8, f32[80,512]{1,0:T(8,128)S(1)} %collective-permute-done.7, f32[80,512]{1,0:T(8,128)S(1)} %collective-permute-done.6, ...), kind=kLoop, calls=%fused_computation.6 | loop fusion | flops 450560 | bytes 1147283 | tf_op jit(solution)/shard_map/jit(_where)/select_n | solution.py:241
  35.1 1.0 %collective-permute-start.9 = (f32[80,512]{1,0:T(8,128)S(1)}, f32[80,512]{1,0:T(8,128)S(1)}, u32[]{:S(2)}, u32[]{:S(2)}) collective-permute-start(f32[80,512]{1,0:T(8,128)S(1)} %get-tuple-element.31), channel_id=1, source_target_pairs={{0,16},{4,20},{8,24},{12,28},{16,0},{20,4},{24,8},{28,12},{1,17},{... | collective-permute-start | bytes 491528 | tf_op jit(solution)/shard_map/ppermute | solution.py:210
  36.1 0.1 constant_dynamic-slice_fusion
  36.2 0.1 copy.15
  36.4 7.0 %collective-permute-done.4.rest_2_ = f32[64,2048]{1,0:T(8,128)S(1)} collective-permute-done((f32[64,2048]{1,0:T(8,128)}, f32[64,2048]{1,0:T(8,128)S(1)}, u32[]{:S(2)}, u32[]{:S(2)}) %collective-permute-start.4) | collective-permute-done | bytes 524320 | tf_op jit(solution)/shard_map/ppermute | solution.py:263
  43.4 0.1 broadcast_select_fusion
  43.5 5.1 %collective-permute-start.12 = (f32[80,512]{1,0:T(8,128)S(1)}, f32[80,512]{1,0:T(8,128)S(1)}, u32[]{:S(2)}, u32[]{:S(2)}) collective-permute-start(f32[80,512]{1,0:T(8,128)S(1)} %get-tuple-element.25), channel_id=1, source_target_pairs={{0,12},{4,8},{8,4},{12,0},{16,28},{20,24},{24,20},{28,16},{1,13},{... | collective-permute-start | bytes 491528 | tf_op jit(solution)/shard_map/ppermute | solution.py:210
  48.6 0.7 %broadcast_select_fusion.1 = (f32[80,512]{1,0:T(8,128)S(1)}, f32[80,512]{1,0:T(8,128)S(1)}, f32[80,512]{1,0:T(8,128)}) fusion(f32[80,512]{1,0:T(8,128)S(1)} %get-tuple-element.27, f32[80,512]{1,0:T(8,128)S(1)} %get-tuple-element.26, pred[80]{0:T(512)(128)(4,1)S(1)} %get-tuple-element.53, pred[80]{0:T(512)(128)(4,1)S(1)} %get-tuple-element.51, ...), kind=kLoop, calls=%fused_computation.4 | loop fusion | flops 122880 | bytes 819440 | tf_op jit(solution)/shard_map/jit(_where)/select_n | solution.py:247
  49.4 0.6 collective-permute-start.10
  49.9 0.6 select_bitcast_fusion.rest_5_
  50.6 0.8 %copy-done.5 = f32[64,2048]{1,0:T(8,128)} copy-done((f32[64,2048]{1,0:T(8,128)}, f32[64,2048]{1,0:T(8,128)S(1)}, u32[]{:S(2)}) %copy-start.5) | copy-done | bytes 524312
  51.4 0.8 %copy-done.6 = f32[64,2048]{1,0:T(8,128)} copy-done((f32[64,2048]{1,0:T(8,128)}, f32[64,2048]{1,0:T(8,128)S(1)}, u32[]{:S(2)}) %copy-start.6) | copy-done | bytes 524312
  52.2 7.3 %factor.1 = (bf16[2048,256]{1,0:T(8,128)(2,1)}, bf16[2048,256]{1,0:T(8,128)(2,1)}, f32[64,2048]{1,0:T(8,128)}) custom-call(s32[3]{0:T(128)} %pad_add_fusion.1.pos, f32[64,2048]{1,0:T(8,128)} %swap.1.rest_0_, f32[64,2048]{1,0:T(8,128)} %copy-done.5, f32[64,2048]{1,0:T(8,128)} %copy-done.4, f32[64,2048]{1,0:T(8,128)} %copy-done.6, f32[256,256]{1,0:T(8,128)} %rest_4_.1, ...), custom_call_target="tpu_custom_call" | custom-call | flops 1000000000 | bytes 6000000 | tf_op jit(solution)/shard_map/factor/pallas_call | solution.py:272
  59.5 0.6 copy-done
  60.3 7.6 %final.1 = (f32[2048,512]{1,0:T(8,128)}, f32[64,2048]{1,0:T(8,128)}, f32[64,256]{1,0:T(8,128)}) custom-call(s32[3]{0:T(128)} %pad_add_fusion.1.pos, s32[264]{0:T(512)} %get-tuple-element.14.owned_list, s32[512]{0:T(512)} %pad_add_fusion.tab, f32[2048,512]{1,0:T(8,128)} %look.3, ...), custom_call_target="tpu_custom_call", output_to_operand_aliasing={{1}: (16, {})} | custom-call | flops 2000000000 | bytes 12000000 | tf_op jit(solution)/shard_map/final/pallas_call | solution.py:288
  (32 shorter events, 0.4 us)
Async XLA Ops:
  1.5 9.4 %collective-permute-start = (f32[64,256]{1,0:T(8,128)S(1)}, f32[64,256]{1,0:T(8,128)S(1)}, u32[]{:S(2)}, u32[]{:S(2)}) collective-permute-start(f32[64,256]{1,0:T(8,128)S(1)} %slice.4), channel_id=1, source_target_pairs={{0,16},{1,17},{2,18},{3,19}} | collective-permute-start | bytes 196616 | tf_op jit(solution)/shard_map/ppermute | solution.py:215
  11.7 24.4 %copy-start.3 = (f32[256,256]{1,0:T(8,128)S(1)}, f32[256,256]{1,0:T(8,128)}, u32[]{:S(2)}) copy-start(f32[256,256]{1,0:T(8,128)} %rest_4_.1) | copy-start | bytes 786436
  11.7 11.8 %collective-permute-start.1 = (f32[64,256]{1,0:T(8,128)S(1)}, f32[64,256]{1,0:T(8,128)S(1)}, u32[]{:S(2)}, u32[]{:S(2)}) collective-permute-start(f32[64,256]{1,0:T(8,128)S(1)} %broadcast_select_fusion.6), channel_id=1, source_target_pairs={{0,8},{16,24},{1,9},{17,25},{2,10},{18,26},{3,11},{19,27}} | collective-permute-start | bytes 196616 | tf_op jit(solution)/shard_map/ppermute | solution.py:215
  19.8 14.2 %collective-permute-start.6 = (f32[80,512]{1,0:T(8,128)}, f32[80,512]{1,0:T(8,128)S(1)}, u32[]{:S(2)}, u32[]{:S(2)}) collective-permute-start(f32[80,512]{1,0:T(8,128)} %get-tuple-element.18.rest_1_), channel_id=1, source_target_pairs={{0,4},{4,0},{8,12},{12,8},{16,20},{20,16},{24,28},{28,24},{1,5},{5... | collective-permute-start | bytes 491528 | tf_op jit(solution)/shard_map/ppermute | solution.py:210
  19.9 14.1 %collective-permute-start.7 = (f32[80,512]{1,0:T(8,128)}, f32[80,512]{1,0:T(8,128)S(1)}, u32[]{:S(2)}, u32[]{:S(2)}) collective-permute-start(f32[80,512]{1,0:T(8,128)} %get-tuple-element.19.rest_2_), channel_id=1, source_target_pairs={{0,8},{4,12},{8,0},{12,4},{16,24},{20,28},{24,16},{28,20},{1,9},{5... | collective-permute-start | bytes 491528 | tf_op jit(solution)/shard_map/ppermute | solution.py:210
  20.0 14.0 %collective-permute-start.8 = (f32[80,512]{1,0:T(8,128)}, f32[80,512]{1,0:T(8,128)S(1)}, u32[]{:S(2)}, u32[]{:S(2)}) collective-permute-start(f32[80,512]{1,0:T(8,128)} %get-tuple-element.20.rest_3_), channel_id=1, source_target_pairs={{0,12},{4,8},{8,4},{12,0},{16,28},{20,24},{24,20},{28,16},{1,13},{... | collective-permute-start | bytes 491528 | tf_op jit(solution)/shard_map/ppermute | solution.py:210
  23.5 5.6 %collective-permute-start.2 = (f32[64,256]{1,0:T(8,128)S(1)}, f32[64,256]{1,0:T(8,128)S(1)}, u32[]{:S(2)}, u32[]{:S(2)}) collective-permute-start(f32[64,256]{1,0:T(8,128)S(1)} %broadcast_select_fusion.7), channel_id=1, source_target_pairs={{0,4},{8,12},{16,20},{24,28},{1,5},{9,13},{17,21},{25,29},{2,6},{1... | collective-permute-start | bytes 196616 | tf_op jit(solution)/shard_map/ppermute | solution.py:215
  32.5 10.9 %collective-permute-start.4 = (f32[64,2048]{1,0:T(8,128)}, f32[64,2048]{1,0:T(8,128)S(1)}, u32[]{:S(2)}, u32[]{:S(2)}) collective-permute-start(f32[64,2048]{1,0:T(8,128)} %swap.1.rest_0_), channel_id=1, source_target_pairs={{0,2},{1,3},{2,0},{3,1},{4,6},{5,7},{6,4},{7,5},{8,10},{9,11},{10,... | collective-permute-start | bytes 1572872 | tf_op jit(solution)/shard_map/ppermute | solution.py:263
  35.1 8.3 %collective-permute-start.9 = (f32[80,512]{1,0:T(8,128)S(1)}, f32[80,512]{1,0:T(8,128)S(1)}, u32[]{:S(2)}, u32[]{:S(2)}) collective-permute-start(f32[80,512]{1,0:T(8,128)S(1)} %get-tuple-element.31), channel_id=1, source_target_pairs={{0,16},{4,20},{8,24},{12,28},{16,0},{20,4},{24,8},{28,12},{1,17},{... | collective-permute-start | bytes 491528 | tf_op jit(solution)/shard_map/ppermute | solution.py:210
  36.3 14.3 %collective-permute-start.3 = (f32[64,2048]{1,0:T(8,128)}, f32[64,2048]{1,0:T(8,128)S(1)}, u32[]{:S(2)}, u32[]{:S(2)}) collective-permute-start(f32[64,2048]{1,0:T(8,128)} %swap.1.rest_0_), channel_id=1, source_target_pairs={{0,1},{1,0},{2,3},{3,2},{4,5},{5,4},{6,7},{7,6},{8,9},{9,8},{10,11... | collective-permute-start | bytes 1572872 | tf_op jit(solution)/shard_map/ppermute | solution.py:263
  43.4 7.2 %copy-start.4 = (f32[64,2048]{1,0:T(8,128)}, f32[64,2048]{1,0:T(8,128)S(1)}, u32[]{:S(2)}) copy-start(f32[64,2048]{1,0:T(8,128)S(1)} %collective-permute-done.4.rest_2_) | copy-start | bytes 1572868
  43.4 7.2 %collective-permute-start.5 = (f32[64,2048]{1,0:T(8,128)S(1)}, f32[64,2048]{1,0:T(8,128)S(1)}, u32[]{:S(2)}, u32[]{:S(2)}) collective-permute-start(f32[64,2048]{1,0:T(8,128)S(1)} %collective-permute-done.4.rest_2_), channel_id=1, source_target_pairs={{0,1},{1,0},{2,3},{3,2},{4,5},{5,4},{6,7},{7,6},{8,9},{9,8},{10,11... | collective-permute-start | bytes 1572872 | tf_op jit(solution)/shard_map/ppermute | solution.py:263
  43.5 15.9 %collective-permute-start.12 = (f32[80,512]{1,0:T(8,128)S(1)}, f32[80,512]{1,0:T(8,128)S(1)}, u32[]{:S(2)}, u32[]{:S(2)}) collective-permute-start(f32[80,512]{1,0:T(8,128)S(1)} %get-tuple-element.25), channel_id=1, source_target_pairs={{0,12},{4,8},{8,4},{12,0},{16,28},{20,24},{24,20},{28,16},{1,13},{... | collective-permute-start | bytes 491528 | tf_op jit(solution)/shard_map/ppermute | solution.py:210
  49.4 10.1 %collective-permute-start.11 = (f32[80,512]{1,0:T(8,128)S(1)}, f32[80,512]{1,0:T(8,128)S(1)}, u32[]{:S(2)}, u32[]{:S(2)}) collective-permute-start(f32[80,512]{1,0:T(8,128)S(1)} %get-tuple-element.45), channel_id=1, source_target_pairs={{0,8},{4,12},{8,0},{12,4},{16,24},{20,28},{24,16},{28,20},{1,9},{5... | collective-permute-start | bytes 491528 | tf_op jit(solution)/shard_map/ppermute | solution.py:210
  49.4 10.2 %collective-permute-start.10 = (f32[80,512]{1,0:T(8,128)S(1)}, f32[80,512]{1,0:T(8,128)S(1)}, u32[]{:S(2)}, u32[]{:S(2)}) collective-permute-start(f32[80,512]{1,0:T(8,128)S(1)} %get-tuple-element.46), channel_id=1, source_target_pairs={{0,4},{4,0},{8,12},{12,8},{16,20},{20,16},{24,28},{28,24},{1,5},{5... | collective-permute-start | bytes 491528 | tf_op jit(solution)/shard_map/ppermute | solution.py:210
  50.6 0.8 %copy-start.5 = (f32[64,2048]{1,0:T(8,128)}, f32[64,2048]{1,0:T(8,128)S(1)}, u32[]{:S(2)}) copy-start(f32[64,2048]{1,0:T(8,128)S(1)} %collective-permute-done.3.rest_1_) | copy-start | bytes 1572868
  51.4 0.8 %copy-start.6 = (f32[64,2048]{1,0:T(8,128)}, f32[64,2048]{1,0:T(8,128)S(1)}, u32[]{:S(2)}) copy-start(f32[64,2048]{1,0:T(8,128)S(1)} %collective-permute-done.5.rest_3_) | copy-start | bytes 1572868
  59.5 0.7 copy-start
  59.5 0.7 %copy-start.1 = (f32[80,512]{1,0:T(8,128)}, f32[80,512]{1,0:T(8,128)S(1)}, u32[]{:S(2)}) copy-start(f32[80,512]{1,0:T(8,128)S(1)} %collective-permute-done.11.rest_6_) | copy-start | bytes 491524
  59.5 0.7 %copy-start.2 = (f32[80,512]{1,0:T(8,128)}, f32[80,512]{1,0:T(8,128)S(1)}, u32[]{:S(2)}) copy-start(f32[80,512]{1,0:T(8,128)S(1)} %collective-permute-done.10.rest_5_) | copy-start | bytes 491524

commit v2 on v1

v2 whole, which is shorter than its diff:
```python
import functools

import jax
import jax.numpy as jnp
from jax import lax
from jax.experimental import pallas as pl
from jax.experimental.pallas import tpu as pltpu
from jax.sharding import PartitionSpec as P


F32, BF16, I32 = jnp.float32, jnp.bfloat16, jnp.int32
GROUP = 4
GROUP_ROWS = 8
PICK_VMEM = 54_000_000
VMEM = pl.BlockSpec(memory_space=pltpu.VMEM)
SMEM = pl.BlockSpec(memory_space=pltpu.SMEM)
HBM = pl.BlockSpec(memory_space=pl.ANY)
FAR = pl.BlockSpec(memory_space=pltpu.HBM)


def split2(x):
    hi = x.astype(BF16)
    return hi, (x - hi.astype(F32)).astype(BF16)


def split3(x):
    hi = x.astype(BF16)
    rest = x - hi.astype(F32)
    mid = rest.astype(BF16)
    return hi, mid, (rest - mid.astype(F32)).astype(BF16)


def mm(a, b, dims=((1,), (0,))):
    return lax.dot_general(a, b, (dims, ((), ())), preferred_element_type=F32)


def mm3(a, b, dims=((1,), (0,))):
    return mm(a[0], b[0], dims) + (mm(a[0], b[1], dims) + mm(a[1], b[0], dims))


def pick_kernel(pivots, look, panel, sketch_map, pivot_row, *rest):
    outs, (head, pan, ske, extra, sem, in_sem) = rest[:GROUP], rest[GROUP:]
    slots = pivot_row.shape[1]
    rows_dev = panel.shape[1]
    chunk = slots // GROUP
    extra_rows = extra.shape[0] // GROUP
    split = sketch_map.shape[0]
    step = rows_dev // GROUP
    row = lax.axis_index("row")
    q = lax.rem(row, GROUP)
    first = row * rows_dev

    def loads(k):
        part = pl.ds(k * step, step)
        return (
            pltpu.make_async_copy(panel.at[:, part], pan.at[:, part], in_sem.at[k]),
            pltpu.make_async_copy(sketch_map.at[:, part], ske.at[:, part], in_sem.at[GROUP + k]),
        )

    for k in range(GROUP):
        for copy in loads(k):
            copy.start()
    target = pivot_row[...] - first
    sketch_sum = jnp.zeros((panel.shape[0], split), F32)
    pick_sum = jnp.zeros((panel.shape[0], slots), F32)
    for s in range(GROUP):
        base = (q ^ s) * chunk
        for i in range(chunk):
            there = pivots[base + i] - first
            owned = there.astype(jnp.uint32) < jnp.uint32(rows_dev)
            pltpu.make_async_copy(
                look.at[pl.ds(jnp.where(owned, there, base + i), 1), :],
                outs[s].at[pl.ds(i, 1), :],
                sem.at[s],
            ).start()
        for copy in loads(s):
            copy.wait()
        k = s * step
        hi, mid, lo = split3(pan[:, k : k + step])
        sketch_sum += mm3((hi, mid), split2(ske[:, k : k + step]), ((1,), (1,)))
        hot = one_hot(target, k, step)
        pick_sum += (mm(hi, hot) + mm(mid, hot)) + mm(lo, hot)
    head[...] = pan[:, :slots]
    extra[:, :split] = sketch_sum
    extra[:, split:] = pick_sum
    for s in range(GROUP):
        rows = pl.ds(pl.multiple_of((q ^ s) * extra_rows, 8), extra_rows)
        outs[s][chunk : chunk + extra_rows, :] = extra[rows, :]
    for s in range(GROUP):
        pltpu.make_async_copy(
            look.at[pl.ds(0, chunk), :], outs[s].at[pl.ds(0, chunk), :], sem.at[s]
        ).wait()


def list_kernel(pivots, owned_list, *, rows_dev):
    slots = pivots.shape[0]
    wide = slots + GROUP_ROWS
    first = lax.axis_index("row") * rows_dev

    def note(p, count):
        there = pivots[p] - first
        owned_list[count] = p
        owned_list[wide + count] = there
        return count + (there.astype(jnp.uint32) < jnp.uint32(rows_dev)).astype(I32)

    count = lax.fori_loop(0, slots, note, jnp.int32(0), unroll=64)
    last = jnp.maximum(count - 1, 0)
    for i in range(GROUP_ROWS):
        owned_list[count + i] = owned_list[last]
        owned_list[wide + count + i] = owned_list[wide + last]
    owned_list[2 * wide] = count


def one_hot(target, k, step):
    place = lax.broadcasted_iota(I32, (step, target.shape[1]), 0) + k
    return jnp.where(place == target, 1.0, 0.0).astype(BF16)


def place_rows(owned_list, slots, source, out):
    count = owned_list[2 * (slots + GROUP_ROWS)]

    @pl.loop(0, pl.cdiv(count, GROUP_ROWS))
    def _(k):
        rows = [
            source[pl.ds(owned_list[k * GROUP_ROWS + i], 1), :] for i in range(GROUP_ROWS)
        ]
        for i in range(GROUP_ROWS):
            out[pl.ds(owned_list[slots + GROUP_ROWS + k * GROUP_ROWS + i], 1), :] = rows[i]


def triangle(upper):
    shape = upper.shape
    keep = lax.broadcasted_iota(I32, shape, 0) <= lax.broadcasted_iota(I32, shape, 1)
    return split2(jnp.where(keep, upper[...], 0.0))


def factor_kernel(order, *rest):
    blocks, (upper, upper_own, fac_hi, fac_lo, own_out, whole) = rest[:-6], rest[-6:]
    cw, rows_dev = blocks[0].shape
    nb = upper.shape[0]
    col = lax.axis_index("col")
    tri = triangle(upper)
    own = split2(upper_own[...])
    for b in range(rows_dev // nb):
        lanes = pl.ds(b * nb, nb)
        for k, block in zip(order, blocks):
            rows = pl.ds(pl.multiple_of((col ^ k) * cw, 8), cw)
            whole[b % 2, rows, :] = block[:, lanes]
        data = whole[b % 2]
        fac_hi[lanes, :], fac_lo[lanes, :] = split2(mm3(split2(data.T), tri))
        own_out[:, lanes] = mm3(own, split2(data))


def head_kernel(order, pivot_row, *rest):
    heads, (upper, upper_own, hi_in, lo_in, own_in, fac_hi, fac_lo, own_out, top) = rest[:-9], rest[-9:]
    cw, rows_dev = own_in.shape
    nb = upper.shape[0]
    col = lax.axis_index("col")
    for k, head in zip(order, heads):
        top[pl.ds(pl.multiple_of((col ^ k) * cw, 8), cw), :] = head[...]
    data = top[...]
    hi, lo = split2(mm3(split2(data.T), triangle(upper)))
    lanes = 128
    right = jnp.concatenate([hi, lo, jnp.ones((nb, lanes), BF16)], axis=1)
    parts = split3(mm3(split2(upper_own[...]), split2(data)))
    left = jnp.concatenate([*parts, jnp.ones((16, nb), BF16)])
    first = lax.axis_index("row") * rows_dev
    for b in range(rows_dev // nb):
        part = pl.ds(b * nb, nb)
        hot = one_hot(pivot_row[...] - first, b * nb, nb)
        moved = mm(left, hot, ((1,), (1,)))
        new = (moved[:cw] + moved[cw : 2 * cw]) + moved[2 * cw : 3 * cw]
        own_out[:, part] = jnp.where(moved[3 * cw : 3 * cw + 1] > 0.5, new, own_in[:, part])
        moved = mm(hot, right)
        hit = jnp.concatenate([moved[:, 2 * nb :]] * (nb // lanes), axis=1) > 0.5
        fac_hi[part, :] = jnp.where(hit, moved[:, :nb], hi_in[part, :].astype(F32)).astype(BF16)
        fac_lo[part, :] = jnp.where(hit, moved[:, nb : 2 * nb], lo_in[part, :].astype(F32)).astype(BF16)


def final_kernel(owned_list, look, fac_hi, fac_lo, lower, target, *rest):
    picks, spread = rest[:GROUP], rest[GROUP : 2 * GROUP]
    _, updated, panel_out, sketch_out, buf, piv, got, extra, in_sem, out_sem, top_sem = rest[2 * GROUP :]
    row = lax.axis_index("row")
    q = lax.rem(row, GROUP)
    slots = target.shape[0]
    chunk = slots // GROUP
    rows_dev = buf.shape[0]
    extra_rows = extra.shape[0] // GROUP
    blocks = rows_dev // slots

    def load(b):
        part = pl.ds(b * slots, slots)
        return pltpu.make_async_copy(look.at[part, :], buf.at[part, :], in_sem.at[b])

    def store(b):
        part = pl.ds(b * slots, slots)
        return pltpu.make_async_copy(buf.at[part, :], updated.at[part, :], out_sem.at[b])

    for b in range(blocks):
        load(b).start()
    for s in range(GROUP):
        part = pl.ds(pl.multiple_of((q ^ s) * chunk, 8), chunk)
        mine = target[part, :] >= 0
        there = spread[s][:chunk, :]
        piv[part, :] = jnp.where(mine, picks[s][:chunk, :], there)
        got[part, :] = there
        erows = pl.ds(pl.multiple_of((q ^ s) * extra_rows, 8), extra_rows)
        extra[erows, :] = spread[s][chunk : chunk + extra_rows, :]
    split = sketch_out.shape[1]
    sketch_out[...] = extra[:, :split]

    below = lax.broadcasted_iota(I32, (slots, slots), 0) > lax.broadcasted_iota(I32, (slots, slots), 1)
    low = split2(jnp.where(below, lower[...], 0.0))
    first = piv[...]
    u_rows = first + mm3(low, split2(first))
    u_hi, u_lo = split2(u_rows)

    for b in range(blocks):
        load(b).wait()

    @pl.when(row == 0)
    def _():
        place_rows(owned_list, slots, buf, buf)

    @pl.when(row != 0)
    def _():
        place_rows(owned_list, slots, got, buf)

    for b in range(blocks):
        part = pl.ds(b * slots, slots)
        drop = mm3((fac_hi[part, :], fac_lo[part, :]), (u_hi, u_lo))
        new = buf[part, :] - drop
        if b == 0:
            new = jnp.where(row == 0, u_rows, new)
        buf[part, :] = new
        store(b).start()

    top = pltpu.make_async_copy(
        extra.at[:, pl.ds(split, slots)], panel_out.at[:, pl.ds(0, slots)], top_sem
    )

    @pl.when(row == 0)
    def _():
        top.start()
        top.wait()

    for b in range(blocks):
        store(b).wait()


def on_device(n_row, n_col, panel_col, look_cols, sketch_map, upper_inv, lower_inv, pivots):
    rows_dev, cw = panel_col.shape
    lw = look_cols.shape[1]
    nb, ks = upper_inv.shape[0], sketch_map.shape[0]
    chunk, extra_rows = nb // GROUP, cw // GROUP
    assert ks + nb == lw and n_row % GROUP == 0
    assert n_row & (n_row - 1) == 0 and n_col & (n_col - 1) == 0
    row, col = lax.axis_index("row"), lax.axis_index("col")
    q = row % GROUP
    panel_t = panel_col.T
    owner = pivots // rows_dev
    local = pivots - row * rows_dev
    pivot_row = pivots.reshape(1, nb)
    target = jnp.where(owner == row, local, -1)[:, None]

    def across(v, s):
        return lax.ppermute(v, "row", [(i, i ^ s) for i in range(n_row)])

    message = jax.ShapeDtypeStruct((chunk + extra_rows, lw), F32)
    *picks, head = pl.pallas_call(
        pick_kernel,
        out_shape=[message] * GROUP
        + [jax.ShapeDtypeStruct((cw, nb), F32)],
        in_specs=[SMEM, FAR, FAR, FAR, VMEM],
        out_specs=[VMEM] * (GROUP + 1),
        scratch_shapes=[
            pltpu.VMEM((cw, rows_dev), F32),
            pltpu.VMEM((ks, rows_dev), F32),
            pltpu.VMEM((cw, lw), F32),
            pltpu.SemaphoreType.DMA((GROUP,)),
            pltpu.SemaphoreType.DMA((2 * GROUP,)),
        ],
        cost_estimate=pl.CostEstimate(flops=10**9, bytes_accessed=4 * 10**6, transcendentals=0),
        compiler_params=pltpu.CompilerParams(vmem_limit_bytes=PICK_VMEM),
        name="pick",
    )(pivots, look_cols, panel_t, sketch_map, pivot_row)
    owned_list = pl.pallas_call(
        functools.partial(list_kernel, rows_dev=rows_dev),
        out_shape=jax.ShapeDtypeStruct((2 * (nb + GROUP_ROWS) + 8,), I32),
        in_specs=[SMEM],
        out_specs=SMEM,
        cost_estimate=pl.CostEstimate(flops=10**8, bytes_accessed=10**6, transcendentals=0),
        name="list",
    )(pivots)

    slot_owner = lax.dynamic_slice_in_dim(owner, q * chunk, chunk)
    slot_owner = jnp.concatenate([slot_owner, jnp.full((extra_rows,), -1, I32)])[:, None]
    summed = slot_owner < 0
    got = [picks[0]] + [across(picks[s], s) for s in range(1, GROUP)]
    have = sum(jnp.where(summed | (slot_owner == (row ^ s)), got[s], 0.0) for s in range(GROUP))
    top = got[0]
    for s in range(1, GROUP):
        top = jnp.where(row == s, got[s], top)
    bit = GROUP
    while bit < n_row:
        inside = summed | (slot_owner // bit == row // bit)
        got = across(jnp.where(inside, have, top), bit)
        other = (row // bit) ^ 1
        theirs = slot_owner // bit == other
        have = jnp.where(theirs, 0.0, have) + jnp.where(summed | theirs, got, 0.0)
        top = jnp.where(other == 0, got, top)
        bit *= 2
    spread = [jnp.where(slot_owner == (row ^ s), top, have) for s in range(GROUP)]
    spread = spread[:1] + [across(spread[s], s) for s in range(1, GROUP)]

    blocks = {0: panel_t}
    bit = n_col // 2
    while bit:
        for k in list(blocks):
            pairs = [(i, i ^ bit) for i in range(n_col)]
            blocks[k ^ bit] = lax.ppermute(blocks[k], "col", pairs)
        bit //= 2
    bit = 1
    while bit < n_row:
        sent = lax.ppermute(head, "row", [(i, i + bit) for i in range(bit)])
        head = jnp.where(row // bit == 1, sent, head)
        bit *= 2
    heads = {0: head}
    bit = n_col // 2
    while bit:
        pairs = [(i, i ^ bit) for i in range(n_col)]
        for k in list(heads):
            heads[k ^ bit] = lax.ppermute(heads[k], "col", pairs)
        bit //= 2
    order = list(heads)
    blocks = [blocks[k] for k in order]
    upper_own = lax.dynamic_slice_in_dim(jnp.triu(upper_inv), col * cw, cw, 1).T

    split_factor = [jax.ShapeDtypeStruct((rows_dev, nb), BF16)] * 2
    own_shape = jax.ShapeDtypeStruct((cw, rows_dev), F32)
    *raw, own_raw = pl.pallas_call(
        functools.partial(factor_kernel, order),
        out_shape=[*split_factor, own_shape],
        in_specs=[VMEM] * (n_col + 2),
        out_specs=[VMEM] * 3,
        scratch_shapes=[pltpu.VMEM((2, nb, nb), F32)],
        cost_estimate=pl.CostEstimate(flops=10**9, bytes_accessed=4 * 10**6, transcendentals=0),
        compiler_params=pltpu.CompilerParams(vmem_limit_bytes=12 << 20),
        name="factor",
    )(*blocks, upper_inv, upper_own)
    fac_hi, fac_lo, panel_out = pl.pallas_call(
        functools.partial(head_kernel, order),
        out_shape=[*split_factor, own_shape],
        in_specs=[VMEM] * (6 + n_col),
        out_specs=[VMEM] * 3,
        scratch_shapes=[pltpu.VMEM((nb, nb), F32)],
        cost_estimate=pl.CostEstimate(flops=10**9, bytes_accessed=4 * 10**6, transcendentals=0),
        compiler_params=pltpu.CompilerParams(vmem_limit_bytes=12 << 20),
        name="headfix",
    )(pivot_row, *heads.values(), upper_inv, upper_own, *raw, own_raw)

    n_in = 6 + 2 * GROUP
    updated, panel_out, sketch_t = pl.pallas_call(
        final_kernel,
        out_shape=[
            jax.ShapeDtypeStruct((rows_dev, lw), F32),
            jax.ShapeDtypeStruct((cw, rows_dev), F32),
            jax.ShapeDtypeStruct((cw, ks), F32),
        ],
        in_specs=[SMEM, HBM] + [VMEM] * (4 + 2 * GROUP) + [HBM],
        out_specs=[HBM, HBM, VMEM],
        input_output_aliases={n_in: 1},
        scratch_shapes=[
            pltpu.VMEM((rows_dev, lw), F32),
            pltpu.VMEM((nb, lw), F32),
            pltpu.VMEM((nb, lw), F32),
            pltpu.VMEM((cw, lw), F32),
            pltpu.SemaphoreType.DMA((rows_dev // nb,)),
            pltpu.SemaphoreType.DMA((rows_dev // nb,)),
            pltpu.SemaphoreType.DMA,
        ],
        cost_estimate=pl.CostEstimate(flops=2 * 10**9, bytes_accessed=12 * 10**6, transcendentals=0),
        compiler_params=pltpu.CompilerParams(vmem_limit_bytes=20 << 20),
        name="final",
    )(owned_list, look_cols, fac_hi, fac_lo, lower_inv, target, *picks, *spread, panel_out)
    return panel_out.T, updated, sketch_t.T


def solution(mesh):
    n_row, n_col = mesh.shape["row"], mesh.shape["col"]
    placed = (P("row", "col"), P("row", "col"), P(None, "row"), P(), P(), P())

    def step(*args):
        return on_device(n_row, n_col, *args)

    return jax.shard_map(
        step,
        mesh=mesh,
        in_specs=placed,
        out_specs=(P("row", "col"), P("row", "col"), P(None, "col")),
        check_vma=False,
    )
```

time: 69 us -> 50.9 us (0.74)
  Pallas kernels: 24.4 us -> 15 us
  other arithmetic: 6.63 us -> 2.97 us
  starting transfers between devices: 21.1 us -> 19.4 us
  local copies, waits for them, and re-layouts: 4.19 us -> 2.82 us
  waiting for transfers between devices: 10.6 us -> 9.34 us
    ppermute x6 -> x9, waiting for transfers between devices: 10.6 us -> 3.62 us  [the longest x3 3.55 us: on_device(): sent = lax.ppermute(head, 'row', [(i, i + bit) for i in range(bit)])]
    ppermute x7, waiting for transfers between devices: 0.02 us -> 5.71 us  [across(): return lax.ppermute(v, 'row', [(i, i ^ s) for i in range(n_row)])]
    pallas_call x2 -> x3, Pallas kernels: 10.1 us -> 6.27 us  [the longest x1 2.35 us: on_device(): pl.pallas_call(functools.partial(head_kernel, order), out_shape=[*split_f...]
    select_n x5 -> x4, other arithmetic: 2.87 us -> 0.04 us  [the longest x3 0.03 us: on_device(): head = jnp.where(row // bit == 1, sent, head)]
    pallas_call x1, Pallas kernels: 6.72 us -> 3.95 us  [on_device(): pl.pallas_call(pick_kernel, out_shape=[message] * GROUP + [jax.ShapeDtype...]
    pallas_call x1, Pallas kernels: 7.58 us -> 4.82 us  [on_device(): pl.pallas_call(final_kernel, out_shape=[jax.ShapeDtypeStruct((rows_dev, l...]
    ppermute x7, starting transfers between devices: 10.2 us -> 7.75 us  [across(): return lax.ppermute(v, 'row', [(i, i ^ s) for i in range(n_row)])]
    slice x1 -> x0, local copies, waits for them, and re-layouts: 0.85 us -> none  [on_device(): head = panel_t[:, :nb]]
  transfers between devices with their start and end apart: 13 -> 16, of which waited for: 2 -> 7; matrix products, arithmetic and copies ran while one was open for 10% -> 8% of each run, Pallas kernels for 25% -> 20%
where the time goes in v2:
time: 50.9 us; the launch traced here: 50.4 us
  starting transfers between devices  19.4 us (38%)
  Pallas kernels  15 us (29%)
  waiting for transfers between devices  9.34 us (18%)
  other arithmetic  2.97 us (6%)
  local copies, waits for them, and re-layouts  2.82 us (6%)
  between operations  0.89 us (2%)
    ppermute x7, starting transfers between devices, across(): return lax.ppermute(v, 'row', [(i, i ^ s) for i in range(n_row)])  7.75 us
    ppermute x3, starting transfers between devices, on_device(): sent = lax.ppermute(head, 'row', [(i, i + bit) for i in range(bit)])  7.32 us
    ppermute x7, waiting for transfers between devices, across(): return lax.ppermute(v, 'row', [(i, i ^ s) for i in range(n_row)])  5.71 us
    pallas_call x1, Pallas kernels, on_device(): pl.pallas_call(final_kernel, out_shape=[jax.ShapeDtypeStruct((rows_dev, l...  4.82 us
    pallas_call x1, Pallas kernels, on_device(): pl.pallas_call(pick_kernel, out_shape=[message] * GROUP + [jax.ShapeDtype...  3.95 us
    ppermute x3, waiting for transfers between devices, on_device(): sent = lax.ppermute(head, 'row', [(i, i + bit) for i in range(bit)])  3.55 us
    ppermute x3, starting transfers between devices, on_device(): blocks[k ^ bit] = lax.ppermute(blocks[k], 'col', pairs)  3.11 us
    unnamed x19, local copies, waits for them, and re-layouts  2.51 us
  transfers between devices with their start and end apart: 16, of which 7 were waited for; matrix products, arithmetic and copies ran while one was open for 8% of the time, Pallas kernels for 20%

profile of v2, /device:TPU:0, one launch (start us, length us, event | category | flops | bytes accessed | tf_op | source)
XLA Modules:
  0.0 50.4 jit_solution(8455521689560756763)
XLA Ops:
  0.6 0.6 %collective-permute-start.7 = (f32[64,2048]{1,0:T(8,128)}, f32[64,2048]{1,0:T(8,128)S(1)}, u32[]{:S(2)}, u32[]{:S(2)}) collective-permute-start(f32[64,2048]{1,0:T(8,128)} %bitcast.7), channel_id=1, source_target_pairs={{0,1},{1,0},{2,3},{3,2},{4,5},{5,4},{6,7},{7,6},{8,9},{9,8},{10,11... | collective-permute-start | bytes 1572872 | tf_op jit(solution)/shard_map/ppermute | solution.py:321
  1.2 2.6 %collective-permute-start.6 = (f32[64,2048]{1,0:T(8,128)}, f32[64,2048]{1,0:T(8,128)S(1)}, u32[]{:S(2)}, u32[]{:S(2)}) collective-permute-start(f32[64,2048]{1,0:T(8,128)} %bitcast.8), channel_id=1, source_target_pairs={{0,2},{1,3},{2,0},{3,1},{4,6},{5,7},{6,4},{7,5},{8,10},{9,11},{10,... | collective-permute-start | bytes 1572872 | tf_op jit(solution)/shard_map/ppermute | solution.py:321
  3.8 1.1 %copy-done.1 = f32[2048,64]{0,1:T(8,128)S(1)} copy-done((f32[2048,64]{0,1:T(8,128)S(1)}, f32[2048,64]{0,1:T(8,128)}, u32[]{:S(2)}) %copy-start.1) | copy-done | bytes 524312
  4.8 0.7 %copy-done.5 = s32[256]{0:T(256)S(1)} copy-done((s32[256]{0:T(256)S(1)}, s32[256]{0:T(256)}, u32[]{:S(2)}) %copy-start.5) | copy-done | bytes 1048
  5.5 4.0 %pick.1 = (f32[80,512]{1,0:T(8,128)S(1)}, f32[80,512]{1,0:T(8,128)S(1)}, f32[80,512]{1,0:T(8,128)S(1)}, f32[80,512]{1,0:T(8,128)S(1)}, f32[64,256]{1,0:T(8,128)S(1)}) custom-call(s32[256]{0:T(256)S(1)} %copy-done.5, f32[2048,512]{1,0:T(8,128)} %look.3, f32[64,2048]{1,0:T(8,128)S(1)} %bitcast.9, f32[256,2048]{1,0:T(8,128)} %sketch_map.1, s32[1,256]{1,0:T(1,128)S(1)} %bitcast.11), custom_call_target="tpu_custom_call" | custom-call | flops 1000000000 | bytes 4000000 | tf_op jit(solution)/shard_map/pick/pallas_call | solution.py:270
  9.5 3.4 %collective-permute-start = (f32[64,256]{1,0:T(8,128)S(1)}, f32[64,256]{1,0:T(8,128)S(1)}, u32[]{:S(2)}, u32[]{:S(2)}) collective-permute-start(f32[64,256]{1,0:T(8,128)S(1)} %get-tuple-element.17), channel_id=1, source_target_pairs={{0,4},{1,5},{2,6},{3,7}} | collective-permute-start | bytes 196616 | tf_op jit(solution)/shard_map/ppermute | solution.py:325
  13.0 0.3 collective-permute-start.10
  13.3 0.1 dynamic_slice.7
  13.5 0.1 constant_dynamic-slice_fusion
  13.6 0.7 %copy.13 = f32[256,64]{0,1:T(8,128)} copy(f32[256,64]{1,0:T(8,128)S(1)} %constant_dynamic-slice_fusion) | data formatting | bytes 131072
  14.3 1.1 %collective-permute-done = f32[64,256]{1,0:T(8,128)S(1)} collective-permute-done((f32[64,256]{1,0:T(8,128)S(1)}, f32[64,256]{1,0:T(8,128)S(1)}, u32[]{:S(2)}, u32[]{:S(2)}) %collective-permute-start) | collective-permute-done | bytes 65568 | tf_op jit(solution)/shard_map/ppermute | solution.py:325
  15.4 2.6 %collective-permute-start.1 = (f32[64,256]{1,0:T(8,128)S(1)}, f32[64,256]{1,0:T(8,128)S(1)}, u32[]{:S(2)}, u32[]{:S(2)}) collective-permute-start(f32[64,256]{1,0:T(8,128)S(1)} %broadcast_select_fusion.6), channel_id=1, source_target_pairs={{0,8},{4,12},{1,9},{5,13},{2,10},{6,14},{3,11},{7,15}} | collective-permute-start | bytes 196616 | tf_op jit(solution)/shard_map/ppermute | solution.py:325
  18.0 1.9 %collective-permute-done.1 = f32[64,256]{1,0:T(8,128)S(1)} collective-permute-done((f32[64,256]{1,0:T(8,128)S(1)}, f32[64,256]{1,0:T(8,128)S(1)}, u32[]{:S(2)}, u32[]{:S(2)}) %collective-permute-start.1) | collective-permute-done | bytes 65568 | tf_op jit(solution)/shard_map/ppermute | solution.py:325
  19.9 3.7 %collective-permute-start.11 = (f32[80,512]{1,0:T(8,128)S(1)}, f32[80,512]{1,0:T(8,128)S(1)}, u32[]{:S(2)}, u32[]{:S(2)}) collective-permute-start(f32[80,512]{1,0:T(8,128)S(1)} %get-tuple-element.26.rest_3_), channel_id=1, source_target_pairs={{0,12},{4,8},{8,4},{12,0},{16,28},{20,24},{24,20},{28,16},{1,13},{... | collective-permute-start | bytes 491528 | tf_op jit(solution)/shard_map/ppermute | solution.py:267
  23.6 1.3 %collective-permute-start.2 = (f32[64,256]{1,0:T(8,128)S(1)}, f32[64,256]{1,0:T(8,128)S(1)}, u32[]{:S(2)}, u32[]{:S(2)}) collective-permute-start(f32[64,256]{1,0:T(8,128)S(1)} %broadcast_select_fusion.7), channel_id=1, source_target_pairs={{0,16},{4,20},{8,24},{12,28},{1,17},{5,21},{9,25},{13,29},{2,18},{... | collective-permute-start | bytes 196616 | tf_op jit(solution)/shard_map/ppermute | solution.py:325
  25.0 2.3 %collective-permute-done.11 = f32[80,512]{1,0:T(8,128)S(1)} collective-permute-done((f32[80,512]{1,0:T(8,128)S(1)}, f32[80,512]{1,0:T(8,128)S(1)}, u32[]{:S(2)}, u32[]{:S(2)}) %collective-permute-start.11) | collective-permute-done | bytes 163872 | tf_op jit(solution)/shard_map/ppermute | solution.py:267
  27.3 0.8 %broadcast_select_fusion.3 = (f32[80,512]{1,0:T(8,128)}, f32[80,512]{1,0:T(8,128)S(1)}, f32[80,512]{1,0:T(8,128)}) fusion(pred[80]{0:T(512)(128)(4,1)S(1)} %compare_or_fusion, f32[80,512]{1,0:T(8,128)S(1)} %collective-permute-done.11, f32[80,512]{1,0:T(8,128)S(1)} %collective-permute-done.10, f32[80,512]{1,0:T(8,128)S(1)} %collective-permute-done.9, ...), kind=kLoop, calls=%fused_computation.6 | loop fusion | flops 450560 | bytes 1147283 | tf_op jit(solution)/shard_map/jit(_where)/select_n | solution.py:307
  28.1 0.6 %collective-permute-done.2 = f32[64,256]{1,0:T(8,128)S(1)} collective-permute-done((f32[64,256]{1,0:T(8,128)S(1)}, f32[64,256]{1,0:T(8,128)S(1)}, u32[]{:S(2)}, u32[]{:S(2)}) %collective-permute-start.2) | collective-permute-done | bytes 65568 | tf_op jit(solution)/shard_map/ppermute | solution.py:325
  28.7 0.6 %collective-permute-start.3 = (f32[64,256]{1,0:T(8,128)S(1)}, f32[64,256]{1,0:T(8,128)S(1)}, u32[]{:S(2)}, u32[]{:S(2)}) collective-permute-start(f32[64,256]{1,0:T(8,128)S(1)} %broadcast_select_fusion.8.rest_0_), channel_id=1, source_target_pairs={{0,2},{1,3},{2,0},{3,1},{4,6},{5,7},{6,4},{7,5},{8,10},{9,11},{10,... | collective-permute-start | bytes 196616 | tf_op jit(solution)/shard_map/ppermute | solution.py:333
  29.3 0.9 %select_bitcast_fusion.rest_5_ = f32[64,256]{1,0:T(8,128)S(1)} fusion(f32[256,64]{0,1:T(8,128)} %copy.13, s32[]{:T(128)S(6)} %select_n.134, s32[256]{0:T(256)S(1)} %iota_add_fusion), kind=kLoop, calls=%fused_computation.10 | loop fusion | flops 49152 | bytes 132100 | tf_op jit(solution)/shard_map/transpose | solution.py:337
  30.2 0.1 copy.12.target
  30.3 2.1 %list.1.owned_list = s32[536]{0:T(1024)} custom-call(s32[256]{0:T(256)} %pivots.3), custom_call_target="tpu_custom_call" | custom-call | flops 100000000 | bytes 1000000 | tf_op jit(solution)/shard_map/list/pallas_call | solution.py:287
  32.4 0.6 %collective-permute-start.4 = (f32[64,256]{1,0:T(8,128)S(1)}, f32[64,256]{1,0:T(8,128)S(1)}, u32[]{:S(2)}, u32[]{:S(2)}) collective-permute-start(f32[64,256]{1,0:T(8,128)S(1)} %broadcast_select_fusion.8.rest_0_), channel_id=1, source_target_pairs={{0,1},{1,0},{2,3},{3,2},{4,5},{5,4},{6,7},{7,6},{8,9},{9,8},{10,11... | collective-permute-start | bytes 196616 | tf_op jit(solution)/shard_map/ppermute | solution.py:333
  33.1 3.3 %collective-permute-done.12 = f32[80,512]{1,0:T(8,128)} collective-permute-done((f32[80,512]{1,0:T(8,128)}, f32[80,512]{1,0:T(8,128)}, u32[]{:S(2)}, u32[]{:S(2)}) %collective-permute-start.12) | collective-permute-done | bytes 163872 | tf_op jit(solution)/shard_map/ppermute | solution.py:267
  36.4 1.1 %broadcast_select_fusion = (f32[80,512]{1,0:T(8,128)S(1)}, f32[80,512]{1,0:T(8,128)S(1)}, f32[80,512]{1,0:T(8,128)S(1)}) fusion(pred[80]{0:T(512)(128)(4,1)S(1)} %get-tuple-element.54, f32[80,512]{1,0:T(8,128)} %collective-permute-done.12, pred[80]{0:T(512)(128)(4,1)S(1)} %get-tuple-element.59, f32[80,512]{1,0:T(8,128)} %get-tuple-element.39, ...), kind=kLoop, calls=%fused_computation.3 | loop fusion | flops 204800 | bytes 983281 | tf_op jit(solution)/shard_map/jit(_where)/select_n | solution.py:313
  37.5 1.7 %collective-permute-start.15 = (f32[80,512]{1,0:T(8,128)S(1)}, f32[80,512]{1,0:T(8,128)S(1)}, u32[]{:S(2)}, u32[]{:S(2)}) collective-permute-start(f32[80,512]{1,0:T(8,128)S(1)} %get-tuple-element.31), channel_id=1, source_target_pairs={{0,12},{4,8},{8,4},{12,0},{16,28},{20,24},{24,20},{28,16},{1,13},{... | collective-permute-start | bytes 491528 | tf_op jit(solution)/shard_map/ppermute | solution.py:267
  39.2 0.1 broadcast_select_fusion.1
  39.4 1.8 %collective-permute-start.13 = (f32[80,512]{1,0:T(8,128)S(1)}, f32[80,512]{1,0:T(8,128)S(1)}, u32[]{:S(2)}, u32[]{:S(2)}) collective-permute-start(f32[80,512]{1,0:T(8,128)S(1)} %get-tuple-element.51), channel_id=1, source_target_pairs={{0,4},{4,0},{8,12},{12,8},{16,20},{20,16},{24,28},{28,24},{1,5},{5... | collective-permute-start | bytes 491528 | tf_op jit(solution)/shard_map/ppermute | solution.py:267
  41.3 1.8 %factor.1 = (bf16[2048,256]{1,0:T(8,128)(2,1)S(1)}, bf16[2048,256]{1,0:T(8,128)(2,1)S(1)}, f32[64,2048]{1,0:T(8,128)S(1)}) custom-call(f32[64,2048]{1,0:T(8,128)S(1)} %bitcast.10, f32[64,2048]{1,0:T(8,128)S(1)} %collective-permute-done.6.rest_1_, f32[64,2048]{1,0:T(8,128)S(1)} %collective-permute-done.7.rest_2_, ...), custom_call_target="tpu_custom_call" | custom-call | flops 1000000000 | bytes 4000000 | tf_op jit(solution)/shard_map/factor/pallas_call | solution.py:341
  43.1 2.3 %headfix.1 = (bf16[2048,256]{1,0:T(8,128)(2,1)S(1)}, bf16[2048,256]{1,0:T(8,128)(2,1)S(1)}, f32[64,2048]{1,0:T(8,128)}) custom-call(s32[1,256]{1,0:T(1,128)S(1)} %bitcast.12, f32[64,256]{1,0:T(8,128)S(1)} %broadcast_select_fusion.8.rest_0_, f32[64,256]{1,0:T(8,128)S(1)} %collective-permute-done.3.rest_1_, f32[64,256]{1,0:T(8,128)S(1)} %collective-permute-done.4.rest_2_, ...), custom_call_target="tpu_custom_call" | custom-call | flops 1000000000 | bytes 4000000 | tf_op jit(solution)/shard_map/headfix/pallas_call | solution.py:351
  45.5 0.1 collective-permute-done.13.rest_5_
  45.6 4.8 %final.1 = (f32[2048,512]{1,0:T(8,128)}, f32[64,2048]{1,0:T(8,128)}, f32[64,256]{1,0:T(8,128)}) custom-call(s32[536]{0:T(1024)S(1)} %copy-done.8, f32[2048,512]{1,0:T(8,128)S(1)} %copy-done, bf16[2048,256]{1,0:T(8,128)(2,1)S(1)} %get-tuple-element.21.fac_hi, bf16[2048,256]{1,0:T(8,128)(2,1)S(1)} %get-tuple-element.22.fac_lo, ...), custom_call_target="tpu_custom_call", output_to_operand_aliasing={{1}: (14, {})} | custom-call | flops 2000000000 | bytes 12000000 | tf_op jit(solution)/shard_map/final/pallas_call | solution.py:363
  (38 shorter events, 0.4 us)
Async XLA Ops:
  0.6 12.7 %copy-start.6 = (s32[256]{0:T(256)S(1)}, s32[256]{0:T(256)}, u32[]{:S(2)}) copy-start(s32[256]{0:T(256)} %pivots.3) | copy-start | bytes 3076
  0.6 38.7 %collective-permute-start.7 = (f32[64,2048]{1,0:T(8,128)}, f32[64,2048]{1,0:T(8,128)S(1)}, u32[]{:S(2)}, u32[]{:S(2)}) collective-permute-start(f32[64,2048]{1,0:T(8,128)} %bitcast.7), channel_id=1, source_target_pairs={{0,1},{1,0},{2,3},{3,2},{4,5},{5,4},{6,7},{7,6},{8,9},{9,8},{10,11... | collective-permute-start | bytes 1572872 | tf_op jit(solution)/shard_map/ppermute | solution.py:321
  1.2 28.1 %collective-permute-start.6 = (f32[64,2048]{1,0:T(8,128)}, f32[64,2048]{1,0:T(8,128)S(1)}, u32[]{:S(2)}, u32[]{:S(2)}) collective-permute-start(f32[64,2048]{1,0:T(8,128)} %bitcast.8), channel_id=1, source_target_pairs={{0,2},{1,3},{2,0},{3,1},{4,6},{5,7},{6,4},{7,5},{8,10},{9,11},{10,... | collective-permute-start | bytes 1572872 | tf_op jit(solution)/shard_map/ppermute | solution.py:321
  3.8 1.1 %copy-start.1 = (f32[2048,64]{0,1:T(8,128)S(1)}, f32[2048,64]{0,1:T(8,128)}, u32[]{:S(2)}) copy-start(f32[2048,64]{0,1:T(8,128)} %param.6) | copy-start | bytes 1572868
  4.8 0.7 %copy-start.5 = (s32[256]{0:T(256)S(1)}, s32[256]{0:T(256)}, u32[]{:S(2)}) copy-start(s32[256]{0:T(256)} %pivots.3) | copy-start | bytes 3076
  5.5 7.9 %copy-start.4 = (f32[256,256]{1,0:T(8,128)S(1)}, f32[256,256]{1,0:T(8,128)}, u32[]{:S(2)}) copy-start(f32[256,256]{1,0:T(8,128)} %rest_4_.3) | copy-start | bytes 786436
  5.5 35.8 %copy-start.2 = (f32[2048,64]{0,1:T(8,128)S(1)}, f32[2048,64]{0,1:T(8,128)}, u32[]{:S(2)}) copy-start(f32[2048,64]{0,1:T(8,128)} %param.6) | copy-start | bytes 1572868
  9.5 5.9 %collective-permute-start = (f32[64,256]{1,0:T(8,128)S(1)}, f32[64,256]{1,0:T(8,128)S(1)}, u32[]{:S(2)}, u32[]{:S(2)}) collective-permute-start(f32[64,256]{1,0:T(8,128)S(1)} %get-tuple-element.17), channel_id=1, source_target_pairs={{0,4},{1,5},{2,6},{3,7}} | collective-permute-start | bytes 196616 | tf_op jit(solution)/shard_map/ppermute | solution.py:325
  12.9 10.7 %collective-permute-start.9 = (f32[80,512]{1,0:T(8,128)S(1)}, f32[80,512]{1,0:T(8,128)S(1)}, u32[]{:S(2)}, u32[]{:S(2)}) collective-permute-start(f32[80,512]{1,0:T(8,128)S(1)} %get-tuple-element.24.rest_1_), channel_id=1, source_target_pairs={{0,4},{4,0},{8,12},{12,8},{16,20},{20,16},{24,28},{28,24},{1,5},{5... | collective-permute-start | bytes 491528 | tf_op jit(solution)/shard_map/ppermute | solution.py:267
  13.0 12.0 %collective-permute-start.10 = (f32[80,512]{1,0:T(8,128)S(1)}, f32[80,512]{1,0:T(8,128)S(1)}, u32[]{:S(2)}, u32[]{:S(2)}) collective-permute-start(f32[80,512]{1,0:T(8,128)S(1)} %get-tuple-element.25.rest_2_), channel_id=1, source_target_pairs={{0,8},{4,12},{8,0},{12,4},{16,24},{20,28},{24,16},{28,20},{1,9},{5... | collective-permute-start | bytes 491528 | tf_op jit(solution)/shard_map/ppermute | solution.py:267
  13.5 29.7 %copy-start.7 = (s32[256]{0:T(256)S(1)}, s32[256]{0:T(256)}, u32[]{:S(2)}) copy-start(s32[256]{0:T(256)} %pivots.3) | copy-start | bytes 3076
  15.4 4.5 %collective-permute-start.1 = (f32[64,256]{1,0:T(8,128)S(1)}, f32[64,256]{1,0:T(8,128)S(1)}, u32[]{:S(2)}, u32[]{:S(2)}) collective-permute-start(f32[64,256]{1,0:T(8,128)S(1)} %broadcast_select_fusion.6), channel_id=1, source_target_pairs={{0,8},{4,12},{1,9},{5,13},{2,10},{6,14},{3,11},{7,15}} | collective-permute-start | bytes 196616 | tf_op jit(solution)/shard_map/ppermute | solution.py:325
  19.9 7.4 %collective-permute-start.11 = (f32[80,512]{1,0:T(8,128)S(1)}, f32[80,512]{1,0:T(8,128)S(1)}, u32[]{:S(2)}, u32[]{:S(2)}) collective-permute-start(f32[80,512]{1,0:T(8,128)S(1)} %get-tuple-element.26.rest_3_), channel_id=1, source_target_pairs={{0,12},{4,8},{8,4},{12,0},{16,28},{20,24},{24,20},{28,16},{1,13},{... | collective-permute-start | bytes 491528 | tf_op jit(solution)/shard_map/ppermute | solution.py:267
  23.6 5.1 %collective-permute-start.2 = (f32[64,256]{1,0:T(8,128)S(1)}, f32[64,256]{1,0:T(8,128)S(1)}, u32[]{:S(2)}, u32[]{:S(2)}) collective-permute-start(f32[64,256]{1,0:T(8,128)S(1)} %broadcast_select_fusion.7), channel_id=1, source_target_pairs={{0,16},{4,20},{8,24},{12,28},{1,17},{5,21},{9,25},{13,29},{2,18},{... | collective-permute-start | bytes 196616 | tf_op jit(solution)/shard_map/ppermute | solution.py:325
  28.1 8.3 %collective-permute-start.12 = (f32[80,512]{1,0:T(8,128)}, f32[80,512]{1,0:T(8,128)}, u32[]{:S(2)}, u32[]{:S(2)}) collective-permute-start(f32[80,512]{1,0:T(8,128)} %get-tuple-element.37), channel_id=1, source_target_pairs={{0,16},{4,20},{8,24},{12,28},{16,0},{20,4},{24,8},{28,12},{1,17},{... | collective-permute-start | bytes 491528 | tf_op jit(solution)/shard_map/ppermute | solution.py:267
  28.7 4.3 %collective-permute-start.3 = (f32[64,256]{1,0:T(8,128)S(1)}, f32[64,256]{1,0:T(8,128)S(1)}, u32[]{:S(2)}, u32[]{:S(2)}) collective-permute-start(f32[64,256]{1,0:T(8,128)S(1)} %broadcast_select_fusion.8.rest_0_), channel_id=1, source_target_pairs={{0,2},{1,3},{2,0},{3,1},{4,6},{5,7},{6,4},{7,5},{8,10},{9,11},{10,... | collective-permute-start | bytes 196616 | tf_op jit(solution)/shard_map/ppermute | solution.py:333
  29.3 10.1 %collective-permute-start.8 = (f32[64,2048]{1,0:T(8,128)S(1)}, f32[64,2048]{1,0:T(8,128)S(1)}, u32[]{:S(2)}, u32[]{:S(2)}) collective-permute-start(f32[64,2048]{1,0:T(8,128)S(1)} %collective-permute-done.6.rest_1_), channel_id=1, source_target_pairs={{0,1},{1,0},{2,3},{3,2},{4,5},{5,4},{6,7},{7,6},{8,9},{9,8},{10,11... | collective-permute-start | bytes 1572872 | tf_op jit(solution)/shard_map/ppermute | solution.py:321
  32.4 10.7 %collective-permute-start.4 = (f32[64,256]{1,0:T(8,128)S(1)}, f32[64,256]{1,0:T(8,128)S(1)}, u32[]{:S(2)}, u32[]{:S(2)}) collective-permute-start(f32[64,256]{1,0:T(8,128)S(1)} %broadcast_select_fusion.8.rest_0_), channel_id=1, source_target_pairs={{0,1},{1,0},{2,3},{3,2},{4,5},{5,4},{6,7},{7,6},{8,9},{9,8},{10,11... | collective-permute-start | bytes 196616 | tf_op jit(solution)/shard_map/ppermute | solution.py:333
  33.0 10.1 %collective-permute-start.5 = (f32[64,256]{1,0:T(8,128)S(1)}, f32[64,256]{1,0:T(8,128)S(1)}, u32[]{:S(2)}, u32[]{:S(2)}) collective-permute-start(f32[64,256]{1,0:T(8,128)S(1)} %collective-permute-done.3.rest_1_), channel_id=1, source_target_pairs={{0,1},{1,0},{2,3},{3,2},{4,5},{5,4},{6,7},{7,6},{8,9},{9,8},{10,11... | collective-permute-start | bytes 196616 | tf_op jit(solution)/shard_map/ppermute | solution.py:333
  37.5 8.1 %copy-start = (f32[2048,512]{1,0:T(8,128)S(1)}, f32[2048,512]{1,0:T(8,128)}, u32[]{:S(2)}) copy-start(f32[2048,512]{1,0:T(8,128)} %look.3) | copy-start | bytes 12582916
  37.5 8.1 %copy-start.3 = (f32[256,256]{1,0:T(8,128)S(1)}, f32[256,256]{1,0:T(8,128)}, u32[]{:S(2)}) copy-start(f32[256,256]{1,0:T(8,128)} %lower.1) | copy-start | bytes 786436
  37.5 8.1 %copy-start.8 = (s32[536]{0:T(1024)S(1)}, s32[536]{0:T(1024)}, u32[]{:S(2)}) copy-start(s32[536]{0:T(1024)} %list.1.owned_list) | copy-start | bytes 6436
  37.5 7.9 %collective-permute-start.15 = (f32[80,512]{1,0:T(8,128)S(1)}, f32[80,512]{1,0:T(8,128)S(1)}, u32[]{:S(2)}, u32[]{:S(2)}) collective-permute-start(f32[80,512]{1,0:T(8,128)S(1)} %get-tuple-element.31), channel_id=1, source_target_pairs={{0,12},{4,8},{8,4},{12,0},{16,28},{20,24},{24,20},{28,16},{1,13},{... | collective-permute-start | bytes 491528 | tf_op jit(solution)/shard_map/ppermute | solution.py:267
  39.3 6.1 %collective-permute-start.14 = (f32[80,512]{1,0:T(8,128)S(1)}, f32[80,512]{1,0:T(8,128)S(1)}, u32[]{:S(2)}, u32[]{:S(2)}) collective-permute-start(f32[80,512]{1,0:T(8,128)S(1)} %get-tuple-element.50), channel_id=1, source_target_pairs={{0,8},{4,12},{8,0},{12,4},{16,24},{20,28},{24,16},{28,20},{1,9},{5... | collective-permute-start | bytes 491528 | tf_op jit(solution)/shard_map/ppermute | solution.py:267
  39.4 6.1 %collective-permute-start.13 = (f32[80,512]{1,0:T(8,128)S(1)}, f32[80,512]{1,0:T(8,128)S(1)}, u32[]{:S(2)}, u32[]{:S(2)}) collective-permute-start(f32[80,512]{1,0:T(8,128)S(1)} %get-tuple-element.51), channel_id=1, source_target_pairs={{0,4},{4,0},{8,12},{12,8},{16,20},{20,16},{24,28},{28,24},{1,5},{5... | collective-permute-start | bytes 491528 | tf_op jit(solution)/shard_map/ppermute | solution.py:267

commit v3 on v2

--- a/solution.py
+++ b/solution.py
@@ -12,6 +12,8 @@
 GROUP = 4
 GROUP_ROWS = 8
 PICK_VMEM = 54_000_000
+FACTOR_VMEM = 12_000_000
+FINAL_VMEM = 20_000_000
 VMEM = pl.BlockSpec(memory_space=pltpu.VMEM)
 SMEM = pl.BlockSpec(memory_space=pltpu.SMEM)
 HBM = pl.BlockSpec(memory_space=pl.ANY)
@@ -135,54 +137,49 @@
 
 
 def factor_kernel(order, *rest):
-    blocks, (upper, upper_own, fac_hi, fac_lo, own_out, whole) = rest[:-6], rest[-6:]
+    blocks, (upper, fac_hi, fac_lo, whole) = rest[: len(order)], rest[len(order) :]
     cw, rows_dev = blocks[0].shape
     nb = upper.shape[0]
     col = lax.axis_index("col")
     tri = triangle(upper)
-    own = split2(upper_own[...])
     for b in range(rows_dev // nb):
         lanes = pl.ds(b * nb, nb)
         for k, block in zip(order, blocks):
-            rows = pl.ds(pl.multiple_of((col ^ k) * cw, 8), cw)
-            whole[b % 2, rows, :] = block[:, lanes]
-        data = whole[b % 2]
-        fac_hi[lanes, :], fac_lo[lanes, :] = split2(mm3(split2(data.T), tri))
-        own_out[:, lanes] = mm3(own, split2(data))
+            whole[b % 2, pl.ds(pl.multiple_of((col ^ k) * cw, 8), cw), :] = block[:, lanes]
+        fac_hi[lanes, :], fac_lo[lanes, :] = split2(mm3(split2(whole[b % 2].T), tri))
 
 
 def head_kernel(order, pivot_row, *rest):
-    heads, (upper, upper_own, hi_in, lo_in, own_in, fac_hi, fac_lo, own_out, top) = rest[:-9], rest[-9:]
-    cw, rows_dev = own_in.shape
+    heads, (upper, hi_in, lo_in, fac_hi, fac_lo, own_out, top) = rest[: len(order)], rest[len(order) :]
+    cw, rows_dev = own_out.shape
     nb = upper.shape[0]
     col = lax.axis_index("col")
     for k, head in zip(order, heads):
         top[pl.ds(pl.multiple_of((col ^ k) * cw, 8), cw), :] = head[...]
-    data = top[...]
-    hi, lo = split2(mm3(split2(data.T), triangle(upper)))
+    hi, lo = split2(mm3(split2(top[...].T), triangle(upper)))
     lanes = 128
     right = jnp.concatenate([hi, lo, jnp.ones((nb, lanes), BF16)], axis=1)
-    parts = split3(mm3(split2(upper_own[...]), split2(data)))
-    left = jnp.concatenate([*parts, jnp.ones((16, nb), BF16)])
-    first = lax.axis_index("row") * rows_dev
+    place = lax.broadcasted_iota(I32, (cw, nb), 1) - lax.broadcasted_iota(I32, (cw, nb), 0)
+    mine = jnp.where(place == col * cw, 1.0, 0.0).astype(BF16)
+    target = pivot_row[...] - lax.axis_index("row") * rows_dev
+    nt = ((1,), (1,))
     for b in range(rows_dev // nb):
         part = pl.ds(b * nb, nb)
-        hot = one_hot(pivot_row[...] - first, b * nb, nb)
-        moved = mm(left, hot, ((1,), (1,)))
-        new = (moved[:cw] + moved[cw : 2 * cw]) + moved[2 * cw : 3 * cw]
-        own_out[:, part] = jnp.where(moved[3 * cw : 3 * cw + 1] > 0.5, new, own_in[:, part])
-        moved = mm(hot, right)
+        moved = mm(one_hot(target, b * nb, nb), right)
         hit = jnp.concatenate([moved[:, 2 * nb :]] * (nb // lanes), axis=1) > 0.5
-        fac_hi[part, :] = jnp.where(hit, moved[:, :nb], hi_in[part, :].astype(F32)).astype(BF16)
-        fac_lo[part, :] = jnp.where(hit, moved[:, nb : 2 * nb], lo_in[part, :].astype(F32)).astype(BF16)
-
-
-def final_kernel(owned_list, look, fac_hi, fac_lo, lower, target, *rest):
+        hi = jnp.where(hit, moved[:, :nb], hi_in[part, :].astype(F32)).astype(BF16)
+        lo = jnp.where(hit, moved[:, nb : 2 * nb], lo_in[part, :].astype(F32)).astype(BF16)
+        fac_hi[part, :] = hi
+        fac_lo[part, :] = lo
+        own_out[:, part] = mm(mine, hi, nt) + mm(mine, lo, nt)
+
+
+def final_kernel(owned_list, look, fac_hi, fac_lo, lower, pivot_row, *rest):
     picks, spread = rest[:GROUP], rest[GROUP : 2 * GROUP]
-    _, updated, panel_out, sketch_out, buf, piv, got, extra, in_sem, out_sem, top_sem = rest[2 * GROUP :]
+    _, updated, panel_out, sketch_out, buf, piv, got, extra, column, in_sem, out_sem, top_sem = rest[2 * GROUP :]
     row = lax.axis_index("row")
     q = lax.rem(row, GROUP)
-    slots = target.shape[0]
+    slots = pivot_row.shape[1]
     chunk = slots // GROUP
     rows_dev = buf.shape[0]
     extra_rows = extra.shape[0] // GROUP
@@ -198,9 +195,12 @@
 
     for b in range(blocks):
         load(b).start()
+    there = pivot_row[...] - row * rows_dev
+    here = jnp.where((there >= 0) & (there < rows_dev), 1.0, 0.0)
+    column[...] = jnp.broadcast_to(here, (128, slots)).T
     for s in range(GROUP):
         part = pl.ds(pl.multiple_of((q ^ s) * chunk, 8), chunk)
-        mine = target[part, :] >= 0
+        mine = column[part, :1] > 0.5
         there = spread[s][:chunk, :]
         piv[part, :] = jnp.where(mine, picks[s][:chunk, :], there)
         got[part, :] = there
@@ -255,13 +255,11 @@
     chunk, extra_rows = nb // GROUP, cw // GROUP
     assert ks + nb == lw and n_row % GROUP == 0
     assert n_row & (n_row - 1) == 0 and n_col & (n_col - 1) == 0
-    row, col = lax.axis_index("row"), lax.axis_index("col")
+    row = lax.axis_index("row")
     q = row % GROUP
     panel_t = panel_col.T
     owner = pivots // rows_dev
-    local = pivots - row * rows_dev
     pivot_row = pivots.reshape(1, nb)
-    target = jnp.where(owner == row, local, -1)[:, None]
 
     def across(v, s):
         return lax.ppermute(v, "row", [(i, i ^ s) for i in range(n_row)])
@@ -334,30 +332,27 @@
         bit //= 2
     order = list(heads)
     blocks = [blocks[k] for k in order]
-    upper_own = lax.dynamic_slice_in_dim(jnp.triu(upper_inv), col * cw, cw, 1).T
-
     split_factor = [jax.ShapeDtypeStruct((rows_dev, nb), BF16)] * 2
-    own_shape = jax.ShapeDtypeStruct((cw, rows_dev), F32)
-    *raw, own_raw = pl.pallas_call(
+    raw = pl.pallas_call(
         functools.partial(factor_kernel, order),
-        out_shape=[*split_factor, own_shape],
-        in_specs=[VMEM] * (n_col + 2),
-        out_specs=[VMEM] * 3,
+        out_shape=split_factor,
+        in_specs=[VMEM] * (n_col + 1),
+        out_specs=[VMEM] * 2,
         scratch_shapes=[pltpu.VMEM((2, nb, nb), F32)],
         cost_estimate=pl.CostEstimate(flops=10**9, bytes_accessed=4 * 10**6, transcendentals=0),
-        compiler_params=pltpu.CompilerParams(vmem_limit_bytes=12 << 20),
+        compiler_params=pltpu.CompilerParams(vmem_limit_bytes=FACTOR_VMEM),
         name="factor",
-    )(*blocks, upper_inv, upper_own)
+    )(*blocks, upper_inv)
     fac_hi, fac_lo, panel_out = pl.pallas_call(
         functools.partial(head_kernel, order),
-        out_shape=[*split_factor, own_shape],
-        in_specs=[VMEM] * (6 + n_col),
+        out_shape=[*split_factor, jax.ShapeDtypeStruct((cw, rows_dev), F32)],
+        in_specs=[VMEM] * (4 + n_col),
         out_specs=[VMEM] * 3,
         scratch_shapes=[pltpu.VMEM((nb, nb), F32)],
         cost_estimate=pl.CostEstimate(flops=10**9, bytes_accessed=4 * 10**6, transcendentals=0),
-        compiler_params=pltpu.CompilerParams(vmem_limit_bytes=12 << 20),
+        compiler_params=pltpu.CompilerParams(vmem_limit_bytes=FACTOR_VMEM),
         name="headfix",
-    )(pivot_row, *heads.values(), upper_inv, upper_own, *raw, own_raw)
+    )(pivot_row, *heads.values(), upper_inv, *raw)
 
     n_in = 6 + 2 * GROUP
     updated, panel_out, sketch_t = pl.pallas_call(
@@ -375,14 +370,15 @@
             pltpu.VMEM((nb, lw), F32),
             pltpu.VMEM((nb, lw), F32),
             pltpu.VMEM((cw, lw), F32),
+            pltpu.VMEM((nb, 128), F32),
             pltpu.SemaphoreType.DMA((rows_dev // nb,)),
             pltpu.SemaphoreType.DMA((rows_dev // nb,)),
             pltpu.SemaphoreType.DMA,
         ],
         cost_estimate=pl.CostEstimate(flops=2 * 10**9, bytes_accessed=12 * 10**6, transcendentals=0),
-        compiler_params=pltpu.CompilerParams(vmem_limit_bytes=20 << 20),
+        compiler_params=pltpu.CompilerParams(vmem_limit_bytes=FINAL_VMEM),
         name="final",
-    )(owned_list, look_cols, fac_hi, fac_lo, lower_inv, target, *picks, *spread, panel_out)
+    )(owned_list, look_cols, fac_hi, fac_lo, lower_inv, pivot_row, *picks, *spread, panel_out)
     return panel_out.T, updated, sketch_t.T
 
 

time: 50.9 us -> 50.6 us (level)
  the two profiles are of different devices: /device:TPU:0 before, /device:TPU:29 now
where the time goes in v3:
time: 50.6 us; the launch traced here: 50.3 us
  Pallas kernels  17.1 us (34%)
  starting transfers between devices  15.8 us (31%)
  waiting for transfers between devices  12.6 us (25%)
  other arithmetic  1.99 us (4%)
  local copies, waits for them, and re-layouts  1.87 us (4%)
  between operations  0.9 us (2%)
    ppermute x7, starting transfers between devices, across(): return lax.ppermute(v, 'row', [(i, i ^ s) for i in range(n_row)])  8.52 us
    ppermute x7, waiting for transfers between devices, across(): return lax.ppermute(v, 'row', [(i, i ^ s) for i in range(n_row)])  6.94 us
    pallas_call x1, Pallas kernels, on_device(): pl.pallas_call(final_kernel, out_shape=[jax.ShapeDtypeStruct((rows_dev, l...  6.02 us
    ppermute x3, waiting for transfers between devices, on_device(): sent = lax.ppermute(head, 'row', [(i, i + bit) for i in range(bit)])  5.63 us
    pallas_call x1, Pallas kernels, on_device(): pl.pallas_call(pick_kernel, out_shape=[message] * GROUP + [jax.ShapeDtype...  3.96 us
    pallas_call x1, Pallas kernels, on_device(): pl.pallas_call(functools.partial(head_kernel, order), out_shape=[*split_f...  3.73 us
    ppermute x3, starting transfers between devices, on_device(): blocks[k ^ bit] = lax.ppermute(blocks[k], 'col', pairs)  2.75 us
    ppermute x3, starting transfers between devices, on_device(): sent = lax.ppermute(head, 'row', [(i, i + bit) for i in range(bit)])  2.62 us
  transfers between devices with their start and end apart: 16, of which 4 were waited for; matrix products, arithmetic and copies ran while one was open for 4% of the time, Pallas kernels for 22%

profile of v3, /device:TPU:29, one launch (start us, length us, event | category | flops | bytes accessed | tf_op | source)
XLA Modules:
  0.0 50.3 jit_solution(9981148799109723405)
XLA Ops:
  0.6 1.3 %collective-permute-start.6 = (f32[64,2048]{1,0:T(8,128)}, f32[64,2048]{1,0:T(8,128)S(1)}, u32[]{:S(2)}, u32[]{:S(2)}) collective-permute-start(f32[64,2048]{1,0:T(8,128)} %bitcast.4), channel_id=1, source_target_pairs={{0,2},{1,3},{2,0},{3,1},{4,6},{5,7},{6,4},{7,5},{8,10},{9,11},{10,... | collective-permute-start | bytes 1572872 | tf_op jit(solution)/shard_map/ppermute | solution.py:319
  1.9 1.1 %copy-done.1 = f32[2048,64]{0,1:T(8,128)S(1)} copy-done((f32[2048,64]{0,1:T(8,128)S(1)}, f32[2048,64]{0,1:T(8,128)}, u32[]{:S(2)}) %copy-start.1) | copy-done | bytes 524312
  3.0 0.7 %copy-done.4 = s32[256]{0:T(256)S(1)} copy-done((s32[256]{0:T(256)S(1)}, s32[256]{0:T(256)}, u32[]{:S(2)}) %copy-start.4) | copy-done | bytes 1048
  3.7 4.0 %pick.1 = (f32[80,512]{1,0:T(8,128)S(1)}, f32[80,512]{1,0:T(8,128)S(1)}, f32[80,512]{1,0:T(8,128)S(1)}, f32[80,512]{1,0:T(8,128)S(1)}, f32[64,256]{1,0:T(8,128)S(1)}) custom-call(s32[256]{0:T(256)S(1)} %copy-done.4, f32[2048,512]{1,0:T(8,128)} %look.3, f32[64,2048]{1,0:T(8,128)S(1)} %bitcast.5, f32[256,2048]{1,0:T(8,128)} %sketch_map.1, s32[1,256]{1,0:T(1,128)S(1)} %bitcast.8), custom_call_target="tpu_custom_call" | custom-call | flops 1000000000 | bytes 4000000 | tf_op jit(solution)/shard_map/pick/pallas_call | solution.py:268
  7.7 0.7 %collective-permute-start = (f32[64,256]{1,0:T(8,128)S(1)}, f32[64,256]{1,0:T(8,128)S(1)}, u32[]{:S(2)}, u32[]{:S(2)}) collective-permute-start(f32[64,256]{1,0:T(8,128)S(1)} %get-tuple-element.16), channel_id=1, source_target_pairs={{0,4},{1,5},{2,6},{3,7}} | collective-permute-start | bytes 196616 | tf_op jit(solution)/shard_map/ppermute | solution.py:323
  8.3 0.3 collective-permute-start.9
  8.6 0.2 collective-permute-start.10
  8.8 2.3 %collective-permute-start.11 = (f32[80,512]{1,0:T(8,128)S(1)}, f32[80,512]{1,0:T(8,128)S(1)}, u32[]{:S(2)}, u32[]{:S(2)}) collective-permute-start(f32[80,512]{1,0:T(8,128)S(1)} %get-tuple-element.24.rest_3_), channel_id=1, source_target_pairs={{0,12},{4,8},{8,4},{12,0},{16,28},{20,24},{24,20},{28,16},{1,13},{... | collective-permute-start | bytes 491528 | tf_op jit(solution)/shard_map/ppermute | solution.py:265
  11.1 0.1 dynamic_slice.3
  11.2 0.7 %collective-permute-start.1 = (f32[64,256]{1,0:T(8,128)S(1)}, f32[64,256]{1,0:T(8,128)S(1)}, u32[]{:S(2)}, u32[]{:S(2)}) collective-permute-start(f32[64,256]{1,0:T(8,128)S(1)} %broadcast_select_fusion.6), channel_id=1, source_target_pairs={{0,8},{4,12},{1,9},{5,13},{2,10},{6,14},{3,11},{7,15}} | collective-permute-start | bytes 196616 | tf_op jit(solution)/shard_map/ppermute | solution.py:323
  12.0 1.3 %collective-permute-start.2 = (f32[64,256]{1,0:T(8,128)S(1)}, f32[64,256]{1,0:T(8,128)S(1)}, u32[]{:S(2)}, u32[]{:S(2)}) collective-permute-start(f32[64,256]{1,0:T(8,128)S(1)} %broadcast_select_fusion.7), channel_id=1, source_target_pairs={{0,16},{4,20},{8,24},{12,28},{1,17},{5,21},{9,25},{13,29},{2,18},{... | collective-permute-start | bytes 196616 | tf_op jit(solution)/shard_map/ppermute | solution.py:323
  13.3 4.3 %collective-permute-done.11 = f32[80,512]{1,0:T(8,128)S(1)} collective-permute-done((f32[80,512]{1,0:T(8,128)S(1)}, f32[80,512]{1,0:T(8,128)S(1)}, u32[]{:S(2)}, u32[]{:S(2)}) %collective-permute-start.11) | collective-permute-done | bytes 163872 | tf_op jit(solution)/shard_map/ppermute | solution.py:265
  17.6 0.8 %broadcast_select_fusion.3 = (f32[80,512]{1,0:T(8,128)}, f32[80,512]{1,0:T(8,128)S(1)}, f32[80,512]{1,0:T(8,128)S(1)}) fusion(pred[80]{0:T(512)(128)(4,1)S(1)} %compare_or_fusion, f32[80,512]{1,0:T(8,128)S(1)} %collective-permute-done.11, f32[80,512]{1,0:T(8,128)S(1)} %collective-permute-done.10, f32[80,512]{1,0:T(8,128)S(1)} %collective-permute-done.9, ...), kind=kLoop, calls=%fused_computation.6 | loop fusion | flops 450560 | bytes 1147283 | tf_op jit(solution)/shard_map/jit(_where)/select_n | solution.py:305
  18.4 3.0 %collective-permute-start.12 = (f32[80,512]{1,0:T(8,128)}, f32[80,512]{1,0:T(8,128)}, u32[]{:S(2)}, u32[]{:S(2)}) collective-permute-start(f32[80,512]{1,0:T(8,128)} %get-tuple-element.35), channel_id=1, source_target_pairs={{0,16},{4,20},{8,24},{12,28},{16,0},{20,4},{24,8},{28,12},{1,17},{... | collective-permute-start | bytes 491528 | tf_op jit(solution)/shard_map/ppermute | solution.py:265
  21.4 5.6 %collective-permute-done.2 = f32[64,256]{1,0:T(8,128)S(1)} collective-permute-done((f32[64,256]{1,0:T(8,128)S(1)}, f32[64,256]{1,0:T(8,128)S(1)}, u32[]{:S(2)}, u32[]{:S(2)}) %collective-permute-start.2) | collective-permute-done | bytes 65568 | tf_op jit(solution)/shard_map/ppermute | solution.py:323
  27.1 0.3 collective-permute-start.3
  27.4 1.4 %collective-permute-start.7 = (f32[64,2048]{1,0:T(8,128)S(1)}, f32[64,2048]{1,0:T(8,128)S(1)}, u32[]{:S(2)}, u32[]{:S(2)}) collective-permute-start(f32[64,2048]{1,0:T(8,128)S(1)} %bitcast.6), channel_id=1, source_target_pairs={{0,1},{1,0},{2,3},{3,2},{4,5},{5,4},{6,7},{7,6},{8,9},{9,8},{10,11... | collective-permute-start | bytes 1572872 | tf_op jit(solution)/shard_map/ppermute | solution.py:319
  28.8 0.1 collective-permute-start.8
  28.9 2.1 %list.1.owned_list = s32[536]{0:T(1024)} custom-call(s32[256]{0:T(256)} %pivots.3), custom_call_target="tpu_custom_call" | custom-call | flops 100000000 | bytes 1000000 | tf_op jit(solution)/shard_map/list/pallas_call | solution.py:285
  31.0 0.5 %collective-permute-start.4 = (f32[64,256]{1,0:T(8,128)S(1)}, f32[64,256]{1,0:T(8,128)S(1)}, u32[]{:S(2)}, u32[]{:S(2)}) collective-permute-start(f32[64,256]{1,0:T(8,128)S(1)} %broadcast_select_fusion.8.rest_0_), channel_id=1, source_target_pairs={{0,1},{1,0},{2,3},{3,2},{4,5},{5,4},{6,7},{7,6},{8,9},{9,8},{10,11... | collective-permute-start | bytes 196616 | tf_op jit(solution)/shard_map/ppermute | solution.py:331
  31.5 1.1 %collective-permute-start.5 = (f32[64,256]{1,0:T(8,128)S(1)}, f32[64,256]{1,0:T(8,128)S(1)}, u32[]{:S(2)}, u32[]{:S(2)}) collective-permute-start(f32[64,256]{1,0:T(8,128)S(1)} %collective-permute-done.3.rest_1_), channel_id=1, source_target_pairs={{0,1},{1,0},{2,3},{3,2},{4,5},{5,4},{6,7},{7,6},{8,9},{9,8},{10,11... | collective-permute-start | bytes 196616 | tf_op jit(solution)/shard_map/ppermute | solution.py:331
  32.6 1.0 %broadcast_select_fusion = (f32[80,512]{1,0:T(8,128)S(1)}, f32[80,512]{1,0:T(8,128)S(1)}, f32[80,512]{1,0:T(8,128)S(1)}) fusion(pred[80]{0:T(512)(128)(4,1)S(1)} %get-tuple-element.50, f32[80,512]{1,0:T(8,128)} %collective-permute-done.12, pred[80]{0:T(512)(128)(4,1)S(1)} %get-tuple-element.55, f32[80,512]{1,0:T(8,128)S(1)} %get-tuple-element.37, ...), kind=kLoop, calls=%fused_computation.3 | loop fusion | flops 204800 | bytes 983281 | tf_op jit(solution)/shard_map/jit(_where)/select_n | solution.py:311
  33.6 0.0 copy-start
  33.6 0.1 collective-permute-start.15
  33.7 0.1 broadcast_select_fusion.1
  33.8 1.9 %collective-permute-start.14 = (f32[80,512]{1,0:T(8,128)S(1)}, f32[80,512]{1,0:T(8,128)S(1)}, u32[]{:S(2)}, u32[]{:S(2)}) collective-permute-start(f32[80,512]{1,0:T(8,128)S(1)} %get-tuple-element.46), channel_id=1, source_target_pairs={{0,8},{4,12},{8,0},{12,4},{16,24},{20,28},{24,16},{28,20},{1,9},{5... | collective-permute-start | bytes 491528 | tf_op jit(solution)/shard_map/ppermute | solution.py:265
  35.7 0.8 %collective-permute-start.13 = (f32[80,512]{1,0:T(8,128)S(1)}, f32[80,512]{1,0:T(8,128)S(1)}, u32[]{:S(2)}, u32[]{:S(2)}) collective-permute-start(f32[80,512]{1,0:T(8,128)S(1)} %get-tuple-element.47), channel_id=1, source_target_pairs={{0,4},{4,0},{8,12},{12,8},{16,20},{20,16},{24,28},{28,24},{1,5},{5... | collective-permute-start | bytes 491528 | tf_op jit(solution)/shard_map/ppermute | solution.py:265
  36.5 1.3 %factor.1 = (bf16[2048,256]{1,0:T(8,128)(2,1)S(1)}, bf16[2048,256]{1,0:T(8,128)(2,1)S(1)}) custom-call(f32[64,2048]{1,0:T(8,128)S(1)} %bitcast.7, f32[64,2048]{1,0:T(8,128)S(1)} %collective-permute-done.6.rest_1_, f32[64,2048]{1,0:T(8,128)S(1)} %collective-permute-done.7.rest_2_, f32[64,2048]{1,0:T(8,128)S(1)} %collective-permute-done.8.rest_3_, ...), custom_call_target="tpu_custom_call" | custom-call | flops 1000000000 | bytes 4000000 | tf_op jit(solution)/shard_map/factor/pallas_call | solution.py:336
  37.9 3.7 %headfix.1 = (bf16[2048,256]{1,0:T(8,128)(2,1)S(1)}, bf16[2048,256]{1,0:T(8,128)(2,1)S(1)}, f32[64,2048]{1,0:T(8,128)}) custom-call(s32[1,256]{1,0:T(1,128)S(1)} %bitcast.9, f32[64,256]{1,0:T(8,128)S(1)} %broadcast_select_fusion.8.rest_0_, f32[64,256]{1,0:T(8,128)S(1)} %collective-permute-done.3.rest_1_, f32[64,256]{1,0:T(8,128)S(1)} %collective-permute-done.4.rest_2_, ...), custom_call_target="tpu_custom_call" | custom-call | flops 1000000000 | bytes 4000000 | tf_op jit(solution)/shard_map/headfix/pallas_call | solution.py:346
  41.6 1.7 %collective-permute-done.14.rest_6_ = f32[80,512]{1,0:T(8,128)S(1)} collective-permute-done((f32[80,512]{1,0:T(8,128)S(1)}, f32[80,512]{1,0:T(8,128)S(1)}, u32[]{:S(2)}, u32[]{:S(2)}) %collective-permute-start.14) | collective-permute-done | bytes 163872 | tf_op jit(solution)/shard_map/ppermute | solution.py:265
  43.4 0.8 %collective-permute-done.13.rest_5_ = f32[80,512]{1,0:T(8,128)S(1)} collective-permute-done((f32[80,512]{1,0:T(8,128)S(1)}, f32[80,512]{1,0:T(8,128)S(1)}, u32[]{:S(2)}, u32[]{:S(2)}) %collective-permute-start.13) | collective-permute-done | bytes 163872 | tf_op jit(solution)/shard_map/ppermute | solution.py:265
  44.2 6.0 %final.1 = (f32[2048,512]{1,0:T(8,128)}, f32[64,2048]{1,0:T(8,128)}, f32[64,256]{1,0:T(8,128)}) custom-call(s32[536]{0:T(1024)S(1)} %copy-done.7, f32[2048,512]{1,0:T(8,128)S(1)} %copy-done, bf16[2048,256]{1,0:T(8,128)(2,1)S(1)} %get-tuple-element.19.fac_hi, bf16[2048,256]{1,0:T(8,128)(2,1)S(1)} %get-tuple-element.20.fac_lo, ...), custom_call_target="tpu_custom_call", output_to_operand_aliasing={{1}: (14, {})} | custom-call | flops 2000000000 | bytes 12000000 | tf_op jit(solution)/shard_map/final/pallas_call | solution.py:358
  (33 shorter events, 0.1 us)
Async XLA Ops:
  0.6 10.4 %copy-start.5 = (s32[256]{0:T(256)S(1)}, s32[256]{0:T(256)}, u32[]{:S(2)}) copy-start(s32[256]{0:T(256)} %pivots.3) | copy-start | bytes 3076
  0.6 28.2 %collective-permute-start.6 = (f32[64,2048]{1,0:T(8,128)}, f32[64,2048]{1,0:T(8,128)S(1)}, u32[]{:S(2)}, u32[]{:S(2)}) collective-permute-start(f32[64,2048]{1,0:T(8,128)} %bitcast.4), channel_id=1, source_target_pairs={{0,2},{1,3},{2,0},{3,1},{4,6},{5,7},{6,4},{7,5},{8,10},{9,11},{10,... | collective-permute-start | bytes 1572872 | tf_op jit(solution)/shard_map/ppermute | solution.py:319
  1.9 1.1 %copy-start.1 = (f32[2048,64]{0,1:T(8,128)S(1)}, f32[2048,64]{0,1:T(8,128)}, u32[]{:S(2)}) copy-start(f32[2048,64]{0,1:T(8,128)} %param.6) | copy-start | bytes 1572868
  3.0 0.7 %copy-start.4 = (s32[256]{0:T(256)S(1)}, s32[256]{0:T(256)}, u32[]{:S(2)}) copy-start(s32[256]{0:T(256)} %pivots.3) | copy-start | bytes 3076
  3.7 23.7 %copy-start.2 = (f32[2048,64]{0,1:T(8,128)S(1)}, f32[2048,64]{0,1:T(8,128)}, u32[]{:S(2)}) copy-start(f32[2048,64]{0,1:T(8,128)} %param.6) | copy-start | bytes 1572868
  3.7 32.9 %copy-start.8 = (f32[256,256]{1,0:T(8,128)S(1)}, f32[256,256]{1,0:T(8,128)}, u32[]{:S(2)}) copy-start(f32[256,256]{1,0:T(8,128)} %rest_4_.3) | copy-start | bytes 786436
  7.6 30.3 %copy-start.6 = (s32[256]{0:T(256)S(1)}, s32[256]{0:T(256)}, u32[]{:S(2)}) copy-start(s32[256]{0:T(256)} %pivots.3) | copy-start | bytes 3076
  7.7 3.5 %collective-permute-start = (f32[64,256]{1,0:T(8,128)S(1)}, f32[64,256]{1,0:T(8,128)S(1)}, u32[]{:S(2)}, u32[]{:S(2)}) collective-permute-start(f32[64,256]{1,0:T(8,128)S(1)} %get-tuple-element.16), channel_id=1, source_target_pairs={{0,4},{1,5},{2,6},{3,7}} | collective-permute-start | bytes 196616 | tf_op jit(solution)/shard_map/ppermute | solution.py:323
  8.3 4.9 %collective-permute-start.9 = (f32[80,512]{1,0:T(8,128)S(1)}, f32[80,512]{1,0:T(8,128)S(1)}, u32[]{:S(2)}, u32[]{:S(2)}) collective-permute-start(f32[80,512]{1,0:T(8,128)S(1)} %get-tuple-element.22.rest_1_), channel_id=1, source_target_pairs={{0,4},{4,0},{8,12},{12,8},{16,20},{20,16},{24,28},{28,24},{1,5},{5... | collective-permute-start | bytes 491528 | tf_op jit(solution)/shard_map/ppermute | solution.py:265
  8.6 4.7 %collective-permute-start.10 = (f32[80,512]{1,0:T(8,128)S(1)}, f32[80,512]{1,0:T(8,128)S(1)}, u32[]{:S(2)}, u32[]{:S(2)}) collective-permute-start(f32[80,512]{1,0:T(8,128)S(1)} %get-tuple-element.23.rest_2_), channel_id=1, source_target_pairs={{0,8},{4,12},{8,0},{12,4},{16,24},{20,28},{24,16},{28,20},{1,9},{5... | collective-permute-start | bytes 491528 | tf_op jit(solution)/shard_map/ppermute | solution.py:265
  8.8 8.8 %collective-permute-start.11 = (f32[80,512]{1,0:T(8,128)S(1)}, f32[80,512]{1,0:T(8,128)S(1)}, u32[]{:S(2)}, u32[]{:S(2)}) collective-permute-start(f32[80,512]{1,0:T(8,128)S(1)} %get-tuple-element.24.rest_3_), channel_id=1, source_target_pairs={{0,12},{4,8},{8,4},{12,0},{16,28},{20,24},{24,20},{28,16},{1,13},{... | collective-permute-start | bytes 491528 | tf_op jit(solution)/shard_map/ppermute | solution.py:265
  11.2 0.7 %collective-permute-start.1 = (f32[64,256]{1,0:T(8,128)S(1)}, f32[64,256]{1,0:T(8,128)S(1)}, u32[]{:S(2)}, u32[]{:S(2)}) collective-permute-start(f32[64,256]{1,0:T(8,128)S(1)} %broadcast_select_fusion.6), channel_id=1, source_target_pairs={{0,8},{4,12},{1,9},{5,13},{2,10},{6,14},{3,11},{7,15}} | collective-permute-start | bytes 196616 | tf_op jit(solution)/shard_map/ppermute | solution.py:323
  12.0 15.1 %collective-permute-start.2 = (f32[64,256]{1,0:T(8,128)S(1)}, f32[64,256]{1,0:T(8,128)S(1)}, u32[]{:S(2)}, u32[]{:S(2)}) collective-permute-start(f32[64,256]{1,0:T(8,128)S(1)} %broadcast_select_fusion.7), channel_id=1, source_target_pairs={{0,16},{4,20},{8,24},{12,28},{1,17},{5,21},{9,25},{13,29},{2,18},{... | collective-permute-start | bytes 196616 | tf_op jit(solution)/shard_map/ppermute | solution.py:323
  18.4 14.2 %collective-permute-start.12 = (f32[80,512]{1,0:T(8,128)}, f32[80,512]{1,0:T(8,128)}, u32[]{:S(2)}, u32[]{:S(2)}) collective-permute-start(f32[80,512]{1,0:T(8,128)} %get-tuple-element.35), channel_id=1, source_target_pairs={{0,16},{4,20},{8,24},{12,28},{16,0},{20,4},{24,8},{28,12},{1,17},{... | collective-permute-start | bytes 491528 | tf_op jit(solution)/shard_map/ppermute | solution.py:265
  27.1 4.4 %collective-permute-start.3 = (f32[64,256]{1,0:T(8,128)S(1)}, f32[64,256]{1,0:T(8,128)S(1)}, u32[]{:S(2)}, u32[]{:S(2)}) collective-permute-start(f32[64,256]{1,0:T(8,128)S(1)} %broadcast_select_fusion.8.rest_0_), channel_id=1, source_target_pairs={{0,2},{1,3},{2,0},{3,1},{4,6},{5,7},{6,4},{7,5},{8,10},{9,11},{10,... | collective-permute-start | bytes 196616 | tf_op jit(solution)/shard_map/ppermute | solution.py:331
  27.4 6.4 %collective-permute-start.7 = (f32[64,2048]{1,0:T(8,128)S(1)}, f32[64,2048]{1,0:T(8,128)S(1)}, u32[]{:S(2)}, u32[]{:S(2)}) collective-permute-start(f32[64,2048]{1,0:T(8,128)S(1)} %bitcast.6), channel_id=1, source_target_pairs={{0,1},{1,0},{2,3},{3,2},{4,5},{5,4},{6,7},{7,6},{8,9},{9,8},{10,11... | collective-permute-start | bytes 1572872 | tf_op jit(solution)/shard_map/ppermute | solution.py:319
  28.8 6.9 %collective-permute-start.8 = (f32[64,2048]{1,0:T(8,128)S(1)}, f32[64,2048]{1,0:T(8,128)S(1)}, u32[]{:S(2)}, u32[]{:S(2)}) collective-permute-start(f32[64,2048]{1,0:T(8,128)S(1)} %collective-permute-done.6.rest_1_), channel_id=1, source_target_pairs={{0,1},{1,0},{2,3},{3,2},{4,5},{5,4},{6,7},{7,6},{8,9},{9,8},{10,11... | collective-permute-start | bytes 1572872 | tf_op jit(solution)/shard_map/ppermute | solution.py:319
  31.0 6.9 %collective-permute-start.4 = (f32[64,256]{1,0:T(8,128)S(1)}, f32[64,256]{1,0:T(8,128)S(1)}, u32[]{:S(2)}, u32[]{:S(2)}) collective-permute-start(f32[64,256]{1,0:T(8,128)S(1)} %broadcast_select_fusion.8.rest_0_), channel_id=1, source_target_pairs={{0,1},{1,0},{2,3},{3,2},{4,5},{5,4},{6,7},{7,6},{8,9},{9,8},{10,11... | collective-permute-start | bytes 196616 | tf_op jit(solution)/shard_map/ppermute | solution.py:331
  31.5 6.4 %collective-permute-start.5 = (f32[64,256]{1,0:T(8,128)S(1)}, f32[64,256]{1,0:T(8,128)S(1)}, u32[]{:S(2)}, u32[]{:S(2)}) collective-permute-start(f32[64,256]{1,0:T(8,128)S(1)} %collective-permute-done.3.rest_1_), channel_id=1, source_target_pairs={{0,1},{1,0},{2,3},{3,2},{4,5},{5,4},{6,7},{7,6},{8,9},{9,8},{10,11... | collective-permute-start | bytes 196616 | tf_op jit(solution)/shard_map/ppermute | solution.py:331
  33.6 10.6 %copy-start = (f32[2048,512]{1,0:T(8,128)S(1)}, f32[2048,512]{1,0:T(8,128)}, u32[]{:S(2)}) copy-start(f32[2048,512]{1,0:T(8,128)} %look.3) | copy-start | bytes 12582916
  33.6 10.6 %copy-start.3 = (f32[256,256]{1,0:T(8,128)S(1)}, f32[256,256]{1,0:T(8,128)}, u32[]{:S(2)}) copy-start(f32[256,256]{1,0:T(8,128)} %lower.1) | copy-start | bytes 786436
  33.6 10.6 %copy-start.7 = (s32[536]{0:T(1024)S(1)}, s32[536]{0:T(1024)}, u32[]{:S(2)}) copy-start(s32[536]{0:T(1024)} %list.1.owned_list) | copy-start | bytes 6436
  33.6 8.0 %collective-permute-start.15 = (f32[80,512]{1,0:T(8,128)S(1)}, f32[80,512]{1,0:T(8,128)S(1)}, u32[]{:S(2)}, u32[]{:S(2)}) collective-permute-start(f32[80,512]{1,0:T(8,128)S(1)} %get-tuple-element.29), channel_id=1, source_target_pairs={{0,12},{4,8},{8,4},{12,0},{16,28},{20,24},{24,20},{28,16},{1,13},{... | collective-permute-start | bytes 491528 | tf_op jit(solution)/shard_map/ppermute | solution.py:265
  33.8 9.5 %collective-permute-start.14 = (f32[80,512]{1,0:T(8,128)S(1)}, f32[80,512]{1,0:T(8,128)S(1)}, u32[]{:S(2)}, u32[]{:S(2)}) collective-permute-start(f32[80,512]{1,0:T(8,128)S(1)} %get-tuple-element.46), channel_id=1, source_target_pairs={{0,8},{4,12},{8,0},{12,4},{16,24},{20,28},{24,16},{28,20},{1,9},{5... | collective-permute-start | bytes 491528 | tf_op jit(solution)/shard_map/ppermute | solution.py:265
  35.7 8.5 %collective-permute-start.13 = (f32[80,512]{1,0:T(8,128)S(1)}, f32[80,512]{1,0:T(8,128)S(1)}, u32[]{:S(2)}, u32[]{:S(2)}) collective-permute-start(f32[80,512]{1,0:T(8,128)S(1)} %get-tuple-element.47), channel_id=1, source_target_pairs={{0,4},{4,0},{8,12},{12,8},{16,20},{20,16},{24,28},{28,24},{1,5},{5... | collective-permute-start | bytes 491528 | tf_op jit(solution)/shard_map/ppermute | solution.py:265

commit v4 on v3

--- a/solution.py
+++ b/solution.py
@@ -37,7 +37,9 @@
 
 
 def mm3(a, b, dims=((1,), (0,))):
-    return mm(a[0], b[0], dims) + (mm(a[0], b[1], dims) + mm(a[1], b[0], dims))
+    left = jnp.concatenate([a[0], a[0], a[1]], axis=dims[0][0])
+    right = jnp.concatenate([b[0], b[1], b[0]], axis=dims[1][0])
+    return mm(left, right, dims)
 
 
 def pick_kernel(pivots, look, panel, sketch_map, pivot_row, *rest):
@@ -94,25 +96,6 @@
         ).wait()
 
 
-def list_kernel(pivots, owned_list, *, rows_dev):
-    slots = pivots.shape[0]
-    wide = slots + GROUP_ROWS
-    first = lax.axis_index("row") * rows_dev
-
-    def note(p, count):
-        there = pivots[p] - first
-        owned_list[count] = p
-        owned_list[wide + count] = there
-        return count + (there.astype(jnp.uint32) < jnp.uint32(rows_dev)).astype(I32)
-
-    count = lax.fori_loop(0, slots, note, jnp.int32(0), unroll=64)
-    last = jnp.maximum(count - 1, 0)
-    for i in range(GROUP_ROWS):
-        owned_list[count + i] = owned_list[last]
-        owned_list[wide + count + i] = owned_list[wide + last]
-    owned_list[2 * wide] = count
-
-
 def one_hot(target, k, step):
     place = lax.broadcasted_iota(I32, (step, target.shape[1]), 0) + k
     return jnp.where(place == target, 1.0, 0.0).astype(BF16)
@@ -136,45 +119,66 @@
     return split2(jnp.where(keep, upper[...], 0.0))
 
 
-def factor_kernel(order, *rest):
-    blocks, (upper, fac_hi, fac_lo, whole) = rest[: len(order)], rest[len(order) :]
+def factor_kernel(order, pivots, pivot_row, *rest):
+    blocks, (upper, upper_own, fac_hi, fac_lo, own_out, owned_list, whole) = (
+        rest[: len(order)],
+        rest[len(order) :],
+    )
     cw, rows_dev = blocks[0].shape
     nb = upper.shape[0]
+    wide = nb + GROUP_ROWS
     col = lax.axis_index("col")
+    first = lax.axis_index("row") * rows_dev
+    target = pivot_row[...] - first
     tri = triangle(upper)
-    for b in range(rows_dev // nb):
+    own = split2(upper_own[...])
+    steps = rows_dev // nb
+    count = jnp.int32(0)
+    for b in range(steps):
         lanes = pl.ds(b * nb, nb)
         for k, block in zip(order, blocks):
             whole[b % 2, pl.ds(pl.multiple_of((col ^ k) * cw, 8), cw), :] = block[:, lanes]
-        fac_hi[lanes, :], fac_lo[lanes, :] = split2(mm3(split2(whole[b % 2].T), tri))
+        for p in range(b * nb // steps, (b + 1) * nb // steps):
+            there = pivots[p] - first
+            owned_list[count] = p
+            owned_list[wide + count] = there
+            count = count + (there.astype(jnp.uint32) < jnp.uint32(rows_dev)).astype(I32)
+        data = whole[b % 2]
+        place = lax.broadcasted_iota(I32, (nb, nb), 0) + b * nb
+        hit = jnp.max(jnp.where(place == target, 1.0, 0.0), axis=1, keepdims=True)
+        fac = jnp.where(hit > 0.5, 0.0, mm3(split2(data.T), tri))
+        fac_hi[lanes, :], fac_lo[lanes, :] = split2(fac)
+        own_out[:, lanes] = mm3(own, split2(data))
+    last = jnp.maximum(count - 1, 0)
+    for i in range(GROUP_ROWS):
+        owned_list[count + i] = owned_list[last]
+        owned_list[wide + count + i] = owned_list[wide + last]
+    owned_list[2 * wide] = count
 
 
 def head_kernel(order, pivot_row, *rest):
-    heads, (upper, hi_in, lo_in, fac_hi, fac_lo, own_out, top) = rest[: len(order)], rest[len(order) :]
-    cw, rows_dev = own_out.shape
+    heads, (upper, upper_own, own_in, top_hi, top_lo, own_out, top) = (
+        rest[: len(order)],
+        rest[len(order) :],
+    )
+    cw, rows_dev = own_in.shape
     nb = upper.shape[0]
     col = lax.axis_index("col")
     for k, head in zip(order, heads):
         top[pl.ds(pl.multiple_of((col ^ k) * cw, 8), cw), :] = head[...]
-    hi, lo = split2(mm3(split2(top[...].T), triangle(upper)))
-    lanes = 128
-    right = jnp.concatenate([hi, lo, jnp.ones((nb, lanes), BF16)], axis=1)
-    place = lax.broadcasted_iota(I32, (cw, nb), 1) - lax.broadcasted_iota(I32, (cw, nb), 0)
-    mine = jnp.where(place == col * cw, 1.0, 0.0).astype(BF16)
+    data = top[...]
+    top_hi[...], top_lo[...] = split2(mm3(split2(data.T), triangle(upper)))
+    parts = split3(mm3(split2(upper_own[...]), split2(data)))
+    left = jnp.concatenate([*parts, jnp.ones((16, nb), BF16)])
     target = pivot_row[...] - lax.axis_index("row") * rows_dev
-    nt = ((1,), (1,))
     for b in range(rows_dev // nb):
         part = pl.ds(b * nb, nb)
-        moved = mm(one_hot(target, b * nb, nb), right)
-        hit = jnp.concatenate([moved[:, 2 * nb :]] * (nb // lanes), axis=1) > 0.5
-        hi = jnp.where(hit, moved[:, :nb], hi_in[part, :].astype(F32)).astype(BF16)
-        lo = jnp.where(hit, moved[:, nb : 2 * nb], lo_in[part, :].astype(F32)).astype(BF16)
-        fac_hi[part, :] = hi
-        fac_lo[part, :] = lo
-        own_out[:, part] = mm(mine, hi, nt) + mm(mine, lo, nt)
-
-
-def final_kernel(owned_list, look, fac_hi, fac_lo, lower, pivot_row, *rest):
+        moved = mm(left, one_hot(target, b * nb, nb), ((1,), (1,)))
+        new = (moved[:cw] + moved[cw : 2 * cw]) + moved[2 * cw : 3 * cw]
+        own_out[:, part] = jnp.where(moved[3 * cw : 3 * cw + 1] > 0.5, new, own_in[:, part])
+
+
+def final_kernel(owned_list, look, fac_hi, fac_lo, top_hi, top_lo, lower, pivot_row, *rest):
     picks, spread = rest[:GROUP], rest[GROUP : 2 * GROUP]
     _, updated, panel_out, sketch_out, buf, piv, got, extra, column, in_sem, out_sem, top_sem = rest[2 * GROUP :]
     row = lax.axis_index("row")
@@ -215,16 +219,12 @@
     u_rows = first + mm3(low, split2(first))
     u_hi, u_lo = split2(u_rows)
 
-    for b in range(blocks):
+    load(0).wait()
+    base = jnp.where(row == 0, buf[:slots, :], got[...])
+    got[...] = base - mm3((top_hi[...], top_lo[...]), (u_hi, u_lo))
+    for b in range(1, blocks):
         load(b).wait()
-
-    @pl.when(row == 0)
-    def _():
-        place_rows(owned_list, slots, buf, buf)
-
-    @pl.when(row != 0)
-    def _():
-        place_rows(owned_list, slots, got, buf)
+    place_rows(owned_list, slots, got, buf)
 
     for b in range(blocks):
         part = pl.ds(b * slots, slots)
@@ -255,7 +255,7 @@
     chunk, extra_rows = nb // GROUP, cw // GROUP
     assert ks + nb == lw and n_row % GROUP == 0
     assert n_row & (n_row - 1) == 0 and n_col & (n_col - 1) == 0
-    row = lax.axis_index("row")
+    row, col = lax.axis_index("row"), lax.axis_index("col")
     q = row % GROUP
     panel_t = panel_col.T
     owner = pivots // rows_dev
@@ -282,14 +282,6 @@
         compiler_params=pltpu.CompilerParams(vmem_limit_bytes=PICK_VMEM),
         name="pick",
     )(pivots, look_cols, panel_t, sketch_map, pivot_row)
-    owned_list = pl.pallas_call(
-        functools.partial(list_kernel, rows_dev=rows_dev),
-        out_shape=jax.ShapeDtypeStruct((2 * (nb + GROUP_ROWS) + 8,), I32),
-        in_specs=[SMEM],
-        out_specs=SMEM,
-        cost_estimate=pl.CostEstimate(flops=10**8, bytes_accessed=10**6, transcendentals=0),
-        name="list",
-    )(pivots)
 
     slot_owner = lax.dynamic_slice_in_dim(owner, q * chunk, chunk)
     slot_owner = jnp.concatenate([slot_owner, jnp.full((extra_rows,), -1, I32)])[:, None]
@@ -332,29 +324,31 @@
         bit //= 2
     order = list(heads)
     blocks = [blocks[k] for k in order]
-    split_factor = [jax.ShapeDtypeStruct((rows_dev, nb), BF16)] * 2
-    raw = pl.pallas_call(
+    upper_own = lax.dynamic_slice_in_dim(jnp.triu(upper_inv), col * cw, cw, 1).T
+    own_shape = jax.ShapeDtypeStruct((cw, rows_dev), F32)
+    fac_hi, fac_lo, own_raw, owned_list = pl.pallas_call(
         functools.partial(factor_kernel, order),
-        out_shape=split_factor,
-        in_specs=[VMEM] * (n_col + 1),
-        out_specs=[VMEM] * 2,
+        out_shape=[jax.ShapeDtypeStruct((rows_dev, nb), BF16)] * 2
+        + [own_shape, jax.ShapeDtypeStruct((2 * (nb + GROUP_ROWS) + 8,), I32)],
+        in_specs=[SMEM] + [VMEM] * (n_col + 3),
+        out_specs=[VMEM] * 3 + [SMEM],
         scratch_shapes=[pltpu.VMEM((2, nb, nb), F32)],
         cost_estimate=pl.CostEstimate(flops=10**9, bytes_accessed=4 * 10**6, transcendentals=0),
         compiler_params=pltpu.CompilerParams(vmem_limit_bytes=FACTOR_VMEM),
         name="factor",
-    )(*blocks, upper_inv)
-    fac_hi, fac_lo, panel_out = pl.pallas_call(
+    )(pivots, pivot_row, *blocks, upper_inv, upper_own)
+    top_hi, top_lo, panel_out = pl.pallas_call(
         functools.partial(head_kernel, order),
-        out_shape=[*split_factor, jax.ShapeDtypeStruct((cw, rows_dev), F32)],
+        out_shape=[jax.ShapeDtypeStruct((nb, nb), BF16)] * 2 + [own_shape],
         in_specs=[VMEM] * (4 + n_col),
         out_specs=[VMEM] * 3,
         scratch_shapes=[pltpu.VMEM((nb, nb), F32)],
         cost_estimate=pl.CostEstimate(flops=10**9, bytes_accessed=4 * 10**6, transcendentals=0),
         compiler_params=pltpu.CompilerParams(vmem_limit_bytes=FACTOR_VMEM),
         name="headfix",
-    )(pivot_row, *heads.values(), upper_inv, *raw)
-
-    n_in = 6 + 2 * GROUP
+    )(pivot_row, *heads.values(), upper_inv, upper_own, own_raw)
+
+    n_in = 8 + 2 * GROUP
     updated, panel_out, sketch_t = pl.pallas_call(
         final_kernel,
         out_shape=[
@@ -362,7 +356,7 @@
             jax.ShapeDtypeStruct((cw, rows_dev), F32),
             jax.ShapeDtypeStruct((cw, ks), F32),
         ],
-        in_specs=[SMEM, HBM] + [VMEM] * (4 + 2 * GROUP) + [HBM],
+        in_specs=[SMEM, HBM] + [VMEM] * (6 + 2 * GROUP) + [HBM],
         out_specs=[HBM, HBM, VMEM],
         input_output_aliases={n_in: 1},
         scratch_shapes=[
@@ -378,7 +372,7 @@
         cost_estimate=pl.CostEstimate(flops=2 * 10**9, bytes_accessed=12 * 10**6, transcendentals=0),
         compiler_params=pltpu.CompilerParams(vmem_limit_bytes=FINAL_VMEM),
         name="final",
-    )(owned_list, look_cols, fac_hi, fac_lo, lower_inv, pivot_row, *picks, *spread, panel_out)
+    )(owned_list, look_cols, fac_hi, fac_lo, top_hi, top_lo, lower_inv, pivot_row, *picks, *spread, panel_out)
     return panel_out.T, updated, sketch_t.T
 
 

time: 50.6 us -> 53.3 us (1.053)
  the two profiles are of different devices: /device:TPU:29 before, /device:TPU:0 now
where the time goes in v4:
time: 53.3 us; the launch traced here: 52.9 us
  starting transfers between devices  19.9 us (37%)
  Pallas kernels  14.4 us (27%)
  waiting for transfers between devices  11 us (21%)
  other arithmetic  4.04 us (8%)
  local copies, waits for them, and re-layouts  2.67 us (5%)
  between operations  0.86 us (2%)
    ppermute x3, starting transfers between devices, on_device(): sent = lax.ppermute(head, 'row', [(i, i + bit) for i in range(bit)])  7.86 us
    ppermute x7, starting transfers between devices, across(): return lax.ppermute(v, 'row', [(i, i ^ s) for i in range(n_row)])  7.74 us
    ppermute x7, waiting for transfers between devices, across(): return lax.ppermute(v, 'row', [(i, i ^ s) for i in range(n_row)])  5.65 us
    pallas_call x1, Pallas kernels, on_device(): pl.pallas_call(final_kernel, out_shape=[jax.ShapeDtypeStruct((rows_dev, l...  5.31 us
    pallas_call x1, Pallas kernels, on_device(): pl.pallas_call(pick_kernel, out_shape=[message] * GROUP + [jax.ShapeDtype...  3.82 us
    pallas_call x1, Pallas kernels, on_device(): pl.pallas_call(functools.partial(factor_kernel, order), out_shape=[jax.Sh...  3.72 us
    ppermute x3, starting transfers between devices, on_device(): blocks[k ^ bit] = lax.ppermute(blocks[k], 'col', pairs)  3.11 us
    ppermute x3, waiting for transfers between devices, on_device(): sent = lax.ppermute(head, 'row', [(i, i + bit) for i in range(bit)])  3.07 us
  transfers between devices with their start and end apart: 16, of which 6 were waited for; matrix products, arithmetic and copies ran while one was open for 9% of the time, Pallas kernels for 17%

profile of v4, /device:TPU:0, one launch (start us, length us, event | category | flops | bytes accessed | tf_op | source)
XLA Modules:
  0.0 52.9 jit_solution(6189696043961308866)
XLA Ops:
  0.6 0.6 %collective-permute-start.1 = (f32[64,2048]{1,0:T(8,128)}, f32[64,2048]{1,0:T(8,128)S(1)}, u32[]{:S(2)}, u32[]{:S(2)}) collective-permute-start(f32[64,2048]{1,0:T(8,128)} %bitcast.6), channel_id=1, source_target_pairs={{0,1},{1,0},{2,3},{3,2},{4,5},{5,4},{6,7},{7,6},{8,9},{9,8},{10,11... | collective-permute-start | bytes 1572872 | tf_op jit(solution)/shard_map/ppermute | solution.py:311
  1.2 2.6 %collective-permute-start = (f32[64,2048]{1,0:T(8,128)}, f32[64,2048]{1,0:T(8,128)S(1)}, u32[]{:S(2)}, u32[]{:S(2)}) collective-permute-start(f32[64,2048]{1,0:T(8,128)} %bitcast.7), channel_id=1, source_target_pairs={{0,2},{1,3},{2,0},{3,1},{4,6},{5,7},{6,4},{7,5},{8,10},{9,11},{10,... | collective-permute-start | bytes 1572872 | tf_op jit(solution)/shard_map/ppermute | solution.py:311
  3.8 1.1 %copy-done.1 = f32[2048,64]{0,1:T(8,128)S(1)} copy-done((f32[2048,64]{0,1:T(8,128)S(1)}, f32[2048,64]{0,1:T(8,128)}, u32[]{:S(2)}) %copy-start.1) | copy-done | bytes 524312
  4.8 0.7 %copy-done.5 = s32[256]{0:T(256)S(1)} copy-done((s32[256]{0:T(256)S(1)}, s32[256]{0:T(256)}, u32[]{:S(2)}) %copy-start.5) | copy-done | bytes 1048
  5.5 3.8 %pick.1 = (f32[80,512]{1,0:T(8,128)S(1)}, f32[80,512]{1,0:T(8,128)S(1)}, f32[80,512]{1,0:T(8,128)S(1)}, f32[80,512]{1,0:T(8,128)S(1)}, f32[64,256]{1,0:T(8,128)S(1)}) custom-call(s32[256]{0:T(256)S(1)} %copy-done.5, f32[2048,512]{1,0:T(8,128)} %look.3, f32[64,2048]{1,0:T(8,128)S(1)} %bitcast.8, f32[256,2048]{1,0:T(8,128)} %sketch_map.1, s32[1,256]{1,0:T(1,128)S(1)} %bitcast.10), custom_call_target="tpu_custom_call" | custom-call | flops 1000000000 | bytes 4000000 | tf_op jit(solution)/shard_map/pick/pallas_call | solution.py:268
  9.3 3.4 %collective-permute-start.3 = (f32[64,256]{1,0:T(8,128)S(1)}, f32[64,256]{1,0:T(8,128)S(1)}, u32[]{:S(2)}, u32[]{:S(2)}) collective-permute-start(f32[64,256]{1,0:T(8,128)S(1)} %get-tuple-element.21), channel_id=1, source_target_pairs={{0,4},{1,5},{2,6},{3,7}} | collective-permute-start | bytes 196616 | tf_op jit(solution)/shard_map/ppermute | solution.py:315
  12.9 0.3 collective-permute-start.10
  13.2 0.1 dynamic_slice.7
  13.3 0.6 %fusion.2 = (pred[80]{0:T(512)(128)(4,1)S(1)}, pred[80]{0:T(512)(128)(4,1)}, pred[80]{0:T(512)(128)(4,1)S(1)}, pred[80]{0:T(512)(128)(4,1)S(1)}, pred[80]{0:T(51...) fusion(s32[64]{0:T(128)S(1)} %dynamic_slice.7, ...), kind=kLoop, calls=%fused_computation.33 | loop fusion | flops 2000 | bytes 1396 | tf_op jit(solution)/shard_map/or | solution.py:290
  13.9 0.1 constant_dynamic-slice_fusion
  14.0 0.7 %copy.11 = f32[256,64]{0,1:T(8,128)} copy(f32[256,64]{1,0:T(8,128)S(1)} %constant_dynamic-slice_fusion) | data formatting | bytes 131072
  14.7 0.5 %collective-permute-done.3 = f32[64,256]{1,0:T(8,128)S(1)} collective-permute-done((f32[64,256]{1,0:T(8,128)S(1)}, f32[64,256]{1,0:T(8,128)S(1)}, u32[]{:S(2)}, u32[]{:S(2)}) %collective-permute-start.3) | collective-permute-done | bytes 65568 | tf_op jit(solution)/shard_map/ppermute | solution.py:315
  15.3 3.1 %collective-permute-start.4 = (f32[64,256]{1,0:T(8,128)S(1)}, f32[64,256]{1,0:T(8,128)S(1)}, u32[]{:S(2)}, u32[]{:S(2)}) collective-permute-start(f32[64,256]{1,0:T(8,128)S(1)} %broadcast_select_fusion.6), channel_id=1, source_target_pairs={{0,8},{4,12},{1,9},{5,13},{2,10},{6,14},{3,11},{7,15}} | collective-permute-start | bytes 196616 | tf_op jit(solution)/shard_map/ppermute | solution.py:315
  18.4 1.9 %collective-permute-done.4 = f32[64,256]{1,0:T(8,128)S(1)} collective-permute-done((f32[64,256]{1,0:T(8,128)S(1)}, f32[64,256]{1,0:T(8,128)S(1)}, u32[]{:S(2)}, u32[]{:S(2)}) %collective-permute-start.4) | collective-permute-done | bytes 65568 | tf_op jit(solution)/shard_map/ppermute | solution.py:315
  20.3 3.7 %collective-permute-start.11 = (f32[80,512]{1,0:T(8,128)S(1)}, f32[80,512]{1,0:T(8,128)S(1)}, u32[]{:S(2)}, u32[]{:S(2)}) collective-permute-start(f32[80,512]{1,0:T(8,128)S(1)} %get-tuple-element.28.rest_3_), channel_id=1, source_target_pairs={{0,12},{4,8},{8,4},{12,0},{16,28},{20,24},{24,20},{28,16},{1,13},{... | collective-permute-start | bytes 491528 | tf_op jit(solution)/shard_map/ppermute | solution.py:265
  24.1 1.3 %collective-permute-start.5 = (f32[64,256]{1,0:T(8,128)S(1)}, f32[64,256]{1,0:T(8,128)S(1)}, u32[]{:S(2)}, u32[]{:S(2)}) collective-permute-start(f32[64,256]{1,0:T(8,128)S(1)} %broadcast_select_fusion.7), channel_id=1, source_target_pairs={{0,16},{4,20},{8,24},{12,28},{1,17},{5,21},{9,25},{13,29},{2,18},{... | collective-permute-start | bytes 196616 | tf_op jit(solution)/shard_map/ppermute | solution.py:315
  25.4 2.3 %collective-permute-done.11 = f32[80,512]{1,0:T(8,128)S(1)} collective-permute-done((f32[80,512]{1,0:T(8,128)S(1)}, f32[80,512]{1,0:T(8,128)S(1)}, u32[]{:S(2)}, u32[]{:S(2)}) %collective-permute-start.11) | collective-permute-done | bytes 163872 | tf_op jit(solution)/shard_map/ppermute | solution.py:265
  27.7 0.8 %broadcast_select_fusion.3 = (f32[80,512]{1,0:T(8,128)}, f32[80,512]{1,0:T(8,128)S(1)}, f32[80,512]{1,0:T(8,128)S(1)}) fusion(pred[80]{0:T(512)(128)(4,1)S(1)} %compare_or_fusion, f32[80,512]{1,0:T(8,128)S(1)} %collective-permute-done.11, f32[80,512]{1,0:T(8,128)S(1)} %collective-permute-done.10, f32[80,512]{1,0:T(8,128)S(1)} %collective-permute-done.9, ...), kind=kLoop, calls=%fused_computation.6 | loop fusion | flops 450560 | bytes 1147283 | tf_op jit(solution)/shard_map/jit(_where)/select_n | solution.py:297
  28.5 0.7 %collective-permute-done.5 = f32[64,256]{1,0:T(8,128)S(1)} collective-permute-done((f32[64,256]{1,0:T(8,128)S(1)}, f32[64,256]{1,0:T(8,128)S(1)}, u32[]{:S(2)}, u32[]{:S(2)}) %collective-permute-start.5) | collective-permute-done | bytes 65568 | tf_op jit(solution)/shard_map/ppermute | solution.py:315
  29.2 0.6 %collective-permute-start.6 = (f32[64,256]{1,0:T(8,128)S(1)}, f32[64,256]{1,0:T(8,128)S(1)}, u32[]{:S(2)}, u32[]{:S(2)}) collective-permute-start(f32[64,256]{1,0:T(8,128)S(1)} %broadcast_select_fusion.8.rest_0_), channel_id=1, source_target_pairs={{0,2},{1,3},{2,0},{3,1},{4,6},{5,7},{6,4},{7,5},{8,10},{9,11},{10,... | collective-permute-start | bytes 196616 | tf_op jit(solution)/shard_map/ppermute | solution.py:323
  29.8 0.9 %select_bitcast_fusion.rest_5_ = f32[64,256]{1,0:T(8,128)S(1)} fusion(f32[256,64]{0,1:T(8,128)} %copy.11, s32[]{:T(128)S(6)} %select_n.122, s32[256]{0:T(256)S(1)} %iota_add_fusion), kind=kLoop, calls=%fused_computation.10 | loop fusion | flops 49152 | bytes 132100 | tf_op jit(solution)/shard_map/transpose | solution.py:327
  30.6 0.6 %collective-permute-start.7 = (f32[64,256]{1,0:T(8,128)S(1)}, f32[64,256]{1,0:T(8,128)S(1)}, u32[]{:S(2)}, u32[]{:S(2)}) collective-permute-start(f32[64,256]{1,0:T(8,128)S(1)} %broadcast_select_fusion.8.rest_0_), channel_id=1, source_target_pairs={{0,1},{1,0},{2,3},{3,2},{4,5},{5,4},{6,7},{7,6},{8,9},{9,8},{10,11... | collective-permute-start | bytes 196616 | tf_op jit(solution)/shard_map/ppermute | solution.py:323
  31.2 2.3 %collective-permute-done.6.rest_1_ = f32[64,256]{1,0:T(8,128)S(1)} collective-permute-done((f32[64,256]{1,0:T(8,128)S(1)}, f32[64,256]{1,0:T(8,128)S(1)}, u32[]{:S(2)}, u32[]{:S(2)}) %collective-permute-start.6) | collective-permute-done | bytes 65568 | tf_op jit(solution)/shard_map/ppermute | solution.py:323
  33.5 3.3 %collective-permute-done.12 = f32[80,512]{1,0:T(8,128)} collective-permute-done((f32[80,512]{1,0:T(8,128)}, f32[80,512]{1,0:T(8,128)}, u32[]{:S(2)}, u32[]{:S(2)}) %collective-permute-start.12) | collective-permute-done | bytes 163872 | tf_op jit(solution)/shard_map/ppermute | solution.py:265
  36.8 1.0 %broadcast_select_fusion = (f32[80,512]{1,0:T(8,128)S(1)}, f32[80,512]{1,0:T(8,128)S(1)}, f32[80,512]{1,0:T(8,128)S(1)}) fusion(pred[80]{0:T(512)(128)(4,1)S(1)} %get-tuple-element.54, f32[80,512]{1,0:T(8,128)} %collective-permute-done.12, pred[80]{0:T(512)(128)(4,1)S(1)} %get-tuple-element.59, f32[80,512]{1,0:T(8,128)S(1)} %get-tuple-element.41, ...), kind=kLoop, calls=%fused_computation.3 | loop fusion | flops 204800 | bytes 983281 | tf_op jit(solution)/shard_map/jit(_where)/select_n | solution.py:303
  37.8 1.7 %collective-permute-start.15 = (f32[80,512]{1,0:T(8,128)S(1)}, f32[80,512]{1,0:T(8,128)S(1)}, u32[]{:S(2)}, u32[]{:S(2)}) collective-permute-start(f32[80,512]{1,0:T(8,128)S(1)} %get-tuple-element.33), channel_id=1, source_target_pairs={{0,12},{4,8},{8,4},{12,0},{16,28},{20,24},{24,20},{28,16},{1,13},{... | collective-permute-start | bytes 491528 | tf_op jit(solution)/shard_map/ppermute | solution.py:265
  39.5 0.8 %broadcast_select_fusion.1 = (f32[80,512]{1,0:T(8,128)S(1)}, f32[80,512]{1,0:T(8,128)S(1)}, f32[80,512]{1,0:T(8,128)S(1)}) fusion(f32[80,512]{1,0:T(8,128)S(1)} %get-tuple-element.35, f32[80,512]{1,0:T(8,128)S(1)} %get-tuple-element.34, pred[80]{0:T(512)(128)(4,1)} %get-tuple-element.58, pred[80]{0:T(512)(128)(4,1)} %get-tuple-element.56, ...), kind=kLoop, calls=%fused_computation.4 | loop fusion | flops 122880 | bytes 819440 | tf_op jit(solution)/shard_map/jit(_where)/select_n | solution.py:303
  40.3 0.1 collective-permute-start.14
  40.4 1.8 %collective-permute-start.13 = (f32[80,512]{1,0:T(8,128)S(1)}, f32[80,512]{1,0:T(8,128)S(1)}, u32[]{:S(2)}, u32[]{:S(2)}) collective-permute-start(f32[80,512]{1,0:T(8,128)S(1)} %get-tuple-element.51), channel_id=1, source_target_pairs={{0,4},{4,0},{8,12},{12,8},{16,20},{20,16},{24,28},{28,24},{1,5},{5... | collective-permute-start | bytes 491528 | tf_op jit(solution)/shard_map/ppermute | solution.py:265
  42.3 3.7 %factor.1 = (bf16[2048,256]{1,0:T(8,128)(2,1)S(1)}, bf16[2048,256]{1,0:T(8,128)(2,1)S(1)}, f32[64,2048]{1,0:T(8,128)S(1)}, s32[536]{0:T(1024)S(1)}) custom-call(s32[256]{0:T(256)S(1)} %copy-done.6, s32[1,256]{1,0:T(1,128)S(1)} %bitcast.11, f32[64,2048]{1,0:T(8,128)S(1)} %bitcast.9, f32[64,2048]{1,0:T(8,128)S(1)} %collective-permute-done.rest_1_, ...), custom_call_target="tpu_custom_call" | custom-call | flops 1000000000 | bytes 4000000 | tf_op jit(solution)/shard_map/factor/pallas_call | solution.py:329
  46.0 1.6 %headfix.1 = (bf16[256,256]{1,0:T(8,128)(2,1)S(1)}, bf16[256,256]{1,0:T(8,128)(2,1)S(1)}, f32[64,2048]{1,0:T(8,128)}) custom-call(s32[1,256]{1,0:T(1,128)S(1)} %bitcast.12, f32[64,256]{1,0:T(8,128)S(1)} %broadcast_select_fusion.8.rest_0_, f32[64,256]{1,0:T(8,128)S(1)} %collective-permute-done.6.rest_1_, f32[64,256]{1,0:T(8,128)S(1)} %collective-permute-done.7.rest_2_, ...), custom_call_target="tpu_custom_call" | custom-call | flops 1000000000 | bytes 4000000 | tf_op jit(solution)/shard_map/headfix/pallas_call | solution.py:340
  47.6 5.3 %final.1 = (f32[2048,512]{1,0:T(8,128)}, f32[64,2048]{1,0:T(8,128)}, f32[64,256]{1,0:T(8,128)}) custom-call(s32[536]{0:T(1024)S(1)} %get-tuple-element.18.owned_list, f32[2048,512]{1,0:T(8,128)S(1)} %copy-done, bf16[2048,256]{1,0:T(8,128)(2,1)S(1)} %get-tuple-element.19.fac_hi, ...), custom_call_target="tpu_custom_call", output_to_operand_aliasing={{1}: (16, {})} | custom-call | flops 2000000000 | bytes 12000000 | tf_op jit(solution)/shard_map/final/pallas_call | solution.py:352
  (32 shorter events, 0.2 us)
Async XLA Ops:
  0.6 12.6 %copy-start.6 = (s32[256]{0:T(256)S(1)}, s32[256]{0:T(256)}, u32[]{:S(2)}) copy-start(s32[256]{0:T(256)} %pivots.3) | copy-start | bytes 3076
  0.6 39.7 %collective-permute-start.1 = (f32[64,2048]{1,0:T(8,128)}, f32[64,2048]{1,0:T(8,128)S(1)}, u32[]{:S(2)}, u32[]{:S(2)}) collective-permute-start(f32[64,2048]{1,0:T(8,128)} %bitcast.6), channel_id=1, source_target_pairs={{0,1},{1,0},{2,3},{3,2},{4,5},{5,4},{6,7},{7,6},{8,9},{9,8},{10,11... | collective-permute-start | bytes 1572872 | tf_op jit(solution)/shard_map/ppermute | solution.py:311
  1.2 28.6 %collective-permute-start = (f32[64,2048]{1,0:T(8,128)}, f32[64,2048]{1,0:T(8,128)S(1)}, u32[]{:S(2)}, u32[]{:S(2)}) collective-permute-start(f32[64,2048]{1,0:T(8,128)} %bitcast.7), channel_id=1, source_target_pairs={{0,2},{1,3},{2,0},{3,1},{4,6},{5,7},{6,4},{7,5},{8,10},{9,11},{10,... | collective-permute-start | bytes 1572872 | tf_op jit(solution)/shard_map/ppermute | solution.py:311
  3.8 1.1 %copy-start.1 = (f32[2048,64]{0,1:T(8,128)S(1)}, f32[2048,64]{0,1:T(8,128)}, u32[]{:S(2)}) copy-start(f32[2048,64]{0,1:T(8,128)} %param.6) | copy-start | bytes 1572868
  4.8 0.7 %copy-start.5 = (s32[256]{0:T(256)S(1)}, s32[256]{0:T(256)}, u32[]{:S(2)}) copy-start(s32[256]{0:T(256)} %pivots.3) | copy-start | bytes 3076
  5.5 8.4 %copy-start.4 = (f32[256,256]{1,0:T(8,128)S(1)}, f32[256,256]{1,0:T(8,128)}, u32[]{:S(2)}) copy-start(f32[256,256]{1,0:T(8,128)} %rest_4_.3) | copy-start | bytes 786436
  5.5 36.7 %copy-start.2 = (f32[2048,64]{0,1:T(8,128)S(1)}, f32[2048,64]{0,1:T(8,128)}, u32[]{:S(2)}) copy-start(f32[2048,64]{0,1:T(8,128)} %param.6) | copy-start | bytes 1572868
  9.3 5.9 %collective-permute-start.3 = (f32[64,256]{1,0:T(8,128)S(1)}, f32[64,256]{1,0:T(8,128)S(1)}, u32[]{:S(2)}, u32[]{:S(2)}) collective-permute-start(f32[64,256]{1,0:T(8,128)S(1)} %get-tuple-element.21), channel_id=1, source_target_pairs={{0,4},{1,5},{2,6},{3,7}} | collective-permute-start | bytes 196616 | tf_op jit(solution)/shard_map/ppermute | solution.py:315
  12.8 11.3 %collective-permute-start.9 = (f32[80,512]{1,0:T(8,128)S(1)}, f32[80,512]{1,0:T(8,128)S(1)}, u32[]{:S(2)}, u32[]{:S(2)}) collective-permute-start(f32[80,512]{1,0:T(8,128)S(1)} %get-tuple-element.26.rest_1_), channel_id=1, source_target_pairs={{0,4},{4,0},{8,12},{12,8},{16,20},{20,16},{24,28},{28,24},{1,5},{5... | collective-permute-start | bytes 491528 | tf_op jit(solution)/shard_map/ppermute | solution.py:265
  12.9 12.5 %collective-permute-start.10 = (f32[80,512]{1,0:T(8,128)S(1)}, f32[80,512]{1,0:T(8,128)S(1)}, u32[]{:S(2)}, u32[]{:S(2)}) collective-permute-start(f32[80,512]{1,0:T(8,128)S(1)} %get-tuple-element.27.rest_2_), channel_id=1, source_target_pairs={{0,8},{4,12},{8,0},{12,4},{16,24},{20,28},{24,16},{28,20},{1,9},{5... | collective-permute-start | bytes 491528 | tf_op jit(solution)/shard_map/ppermute | solution.py:265
  15.3 5.0 %collective-permute-start.4 = (f32[64,256]{1,0:T(8,128)S(1)}, f32[64,256]{1,0:T(8,128)S(1)}, u32[]{:S(2)}, u32[]{:S(2)}) collective-permute-start(f32[64,256]{1,0:T(8,128)S(1)} %broadcast_select_fusion.6), channel_id=1, source_target_pairs={{0,8},{4,12},{1,9},{5,13},{2,10},{6,14},{3,11},{7,15}} | collective-permute-start | bytes 196616 | tf_op jit(solution)/shard_map/ppermute | solution.py:315
  20.3 7.4 %collective-permute-start.11 = (f32[80,512]{1,0:T(8,128)S(1)}, f32[80,512]{1,0:T(8,128)S(1)}, u32[]{:S(2)}, u32[]{:S(2)}) collective-permute-start(f32[80,512]{1,0:T(8,128)S(1)} %get-tuple-element.28.rest_3_), channel_id=1, source_target_pairs={{0,12},{4,8},{8,4},{12,0},{16,28},{20,24},{24,20},{28,16},{1,13},{... | collective-permute-start | bytes 491528 | tf_op jit(solution)/shard_map/ppermute | solution.py:265
  24.1 5.1 %collective-permute-start.5 = (f32[64,256]{1,0:T(8,128)S(1)}, f32[64,256]{1,0:T(8,128)S(1)}, u32[]{:S(2)}, u32[]{:S(2)}) collective-permute-start(f32[64,256]{1,0:T(8,128)S(1)} %broadcast_select_fusion.7), channel_id=1, source_target_pairs={{0,16},{4,20},{8,24},{12,28},{1,17},{5,21},{9,25},{13,29},{2,18},{... | collective-permute-start | bytes 196616 | tf_op jit(solution)/shard_map/ppermute | solution.py:315
  28.5 8.3 %collective-permute-start.12 = (f32[80,512]{1,0:T(8,128)}, f32[80,512]{1,0:T(8,128)}, u32[]{:S(2)}, u32[]{:S(2)}) collective-permute-start(f32[80,512]{1,0:T(8,128)} %get-tuple-element.39), channel_id=1, source_target_pairs={{0,16},{4,20},{8,24},{12,28},{16,0},{20,4},{24,8},{28,12},{1,17},{... | collective-permute-start | bytes 491528 | tf_op jit(solution)/shard_map/ppermute | solution.py:265
  29.2 4.3 %collective-permute-start.6 = (f32[64,256]{1,0:T(8,128)S(1)}, f32[64,256]{1,0:T(8,128)S(1)}, u32[]{:S(2)}, u32[]{:S(2)}) collective-permute-start(f32[64,256]{1,0:T(8,128)S(1)} %broadcast_select_fusion.8.rest_0_), channel_id=1, source_target_pairs={{0,2},{1,3},{2,0},{3,1},{4,6},{5,7},{6,4},{7,5},{8,10},{9,11},{10,... | collective-permute-start | bytes 196616 | tf_op jit(solution)/shard_map/ppermute | solution.py:323
  29.8 10.6 %collective-permute-start.2 = (f32[64,2048]{1,0:T(8,128)S(1)}, f32[64,2048]{1,0:T(8,128)S(1)}, u32[]{:S(2)}, u32[]{:S(2)}) collective-permute-start(f32[64,2048]{1,0:T(8,128)S(1)} %collective-permute-done.rest_1_), channel_id=1, source_target_pairs={{0,1},{1,0},{2,3},{3,2},{4,5},{5,4},{6,7},{7,6},{8,9},{9,8},{10,11... | collective-permute-start | bytes 1572872 | tf_op jit(solution)/shard_map/ppermute | solution.py:311
  30.6 15.3 %collective-permute-start.7 = (f32[64,256]{1,0:T(8,128)S(1)}, f32[64,256]{1,0:T(8,128)S(1)}, u32[]{:S(2)}, u32[]{:S(2)}) collective-permute-start(f32[64,256]{1,0:T(8,128)S(1)} %broadcast_select_fusion.8.rest_0_), channel_id=1, source_target_pairs={{0,1},{1,0},{2,3},{3,2},{4,5},{5,4},{6,7},{7,6},{8,9},{9,8},{10,11... | collective-permute-start | bytes 196616 | tf_op jit(solution)/shard_map/ppermute | solution.py:323
  33.5 12.5 %collective-permute-start.8 = (f32[64,256]{1,0:T(8,128)S(1)}, f32[64,256]{1,0:T(8,128)S(1)}, u32[]{:S(2)}, u32[]{:S(2)}) collective-permute-start(f32[64,256]{1,0:T(8,128)S(1)} %collective-permute-done.6.rest_1_), channel_id=1, source_target_pairs={{0,1},{1,0},{2,3},{3,2},{4,5},{5,4},{6,7},{7,6},{8,9},{9,8},{10,11... | collective-permute-start | bytes 196616 | tf_op jit(solution)/shard_map/ppermute | solution.py:323
  37.8 9.8 %copy-start = (f32[2048,512]{1,0:T(8,128)S(1)}, f32[2048,512]{1,0:T(8,128)}, u32[]{:S(2)}) copy-start(f32[2048,512]{1,0:T(8,128)} %look.3) | copy-start | bytes 12582916
  37.8 9.8 %copy-start.3 = (f32[256,256]{1,0:T(8,128)S(1)}, f32[256,256]{1,0:T(8,128)}, u32[]{:S(2)}) copy-start(f32[256,256]{1,0:T(8,128)} %lower.1) | copy-start | bytes 786436
  37.8 9.7 %collective-permute-start.15 = (f32[80,512]{1,0:T(8,128)S(1)}, f32[80,512]{1,0:T(8,128)S(1)}, u32[]{:S(2)}, u32[]{:S(2)}) collective-permute-start(f32[80,512]{1,0:T(8,128)S(1)} %get-tuple-element.33), channel_id=1, source_target_pairs={{0,12},{4,8},{8,4},{12,0},{16,28},{20,24},{24,20},{28,16},{1,13},{... | collective-permute-start | bytes 491528 | tf_op jit(solution)/shard_map/ppermute | solution.py:265
  40.3 7.3 %collective-permute-start.14 = (f32[80,512]{1,0:T(8,128)S(1)}, f32[80,512]{1,0:T(8,128)S(1)}, u32[]{:S(2)}, u32[]{:S(2)}) collective-permute-start(f32[80,512]{1,0:T(8,128)S(1)} %get-tuple-element.50), channel_id=1, source_target_pairs={{0,8},{4,12},{8,0},{12,4},{16,24},{20,28},{24,16},{28,20},{1,9},{5... | collective-permute-start | bytes 491528 | tf_op jit(solution)/shard_map/ppermute | solution.py:265
  40.4 7.2 %collective-permute-start.13 = (f32[80,512]{1,0:T(8,128)S(1)}, f32[80,512]{1,0:T(8,128)S(1)}, u32[]{:S(2)}, u32[]{:S(2)}) collective-permute-start(f32[80,512]{1,0:T(8,128)S(1)} %get-tuple-element.51), channel_id=1, source_target_pairs={{0,4},{4,0},{8,12},{12,8},{16,20},{20,16},{24,28},{28,24},{1,5},{5... | collective-permute-start | bytes 491528 | tf_op jit(solution)/shard_map/ppermute | solution.py:265

commit v5 on v4

--- a/solution.py
+++ b/solution.py
@@ -102,15 +102,12 @@
 
 
 def place_rows(owned_list, slots, source, out):
-    count = owned_list[2 * (slots + GROUP_ROWS)]
-
-    @pl.loop(0, pl.cdiv(count, GROUP_ROWS))
+    @pl.loop(0, pl.cdiv(owned_list[slots + GROUP_ROWS], GROUP_ROWS))
     def _(k):
-        rows = [
-            source[pl.ds(owned_list[k * GROUP_ROWS + i], 1), :] for i in range(GROUP_ROWS)
-        ]
-        for i in range(GROUP_ROWS):
-            out[pl.ds(owned_list[slots + GROUP_ROWS + k * GROUP_ROWS + i], 1), :] = rows[i]
+        entries = [owned_list[k * GROUP_ROWS + i] for i in range(GROUP_ROWS)]
+        rows = [source[pl.ds(entry >> 16, 1), :] for entry in entries]
+        for entry, value in zip(entries, rows):
+            out[pl.ds(entry & 0xFFFF, 1), :] = value
 
 
 def triangle(upper):
@@ -140,8 +137,7 @@
             whole[b % 2, pl.ds(pl.multiple_of((col ^ k) * cw, 8), cw), :] = block[:, lanes]
         for p in range(b * nb // steps, (b + 1) * nb // steps):
             there = pivots[p] - first
-            owned_list[count] = p
-            owned_list[wide + count] = there
+            owned_list[count] = there + (p << 16)
             count = count + (there.astype(jnp.uint32) < jnp.uint32(rows_dev)).astype(I32)
         data = whole[b % 2]
         place = lax.broadcasted_iota(I32, (nb, nb), 0) + b * nb
@@ -149,11 +145,10 @@
         fac = jnp.where(hit > 0.5, 0.0, mm3(split2(data.T), tri))
         fac_hi[lanes, :], fac_lo[lanes, :] = split2(fac)
         own_out[:, lanes] = mm3(own, split2(data))
-    last = jnp.maximum(count - 1, 0)
+    last = owned_list[jnp.maximum(count - 1, 0)]
     for i in range(GROUP_ROWS):
-        owned_list[count + i] = owned_list[last]
-        owned_list[wide + count + i] = owned_list[wide + last]
-    owned_list[2 * wide] = count
+        owned_list[count + i] = last
+    owned_list[wide] = count
 
 
 def head_kernel(order, pivot_row, *rest):
@@ -220,8 +215,12 @@
     u_hi, u_lo = split2(u_rows)
 
     load(0).wait()
-    base = jnp.where(row == 0, buf[:slots, :], got[...])
-    got[...] = base - mm3((top_hi[...], top_lo[...]), (u_hi, u_lo))
+
+    @pl.when(owned_list[slots + GROUP_ROWS] > 0)
+    def _():
+        base = jnp.where(row == 0, buf[:slots, :], got[...])
+        got[...] = base - mm3((top_hi[...], top_lo[...]), (u_hi, u_lo))
+
     for b in range(1, blocks):
         load(b).wait()
     place_rows(owned_list, slots, got, buf)
@@ -252,6 +251,7 @@
     rows_dev, cw = panel_col.shape
     lw = look_cols.shape[1]
     nb, ks = upper_inv.shape[0], sketch_map.shape[0]
+    assert rows_dev <= 1 << 16 and nb < 1 << 15
     chunk, extra_rows = nb // GROUP, cw // GROUP
     assert ks + nb == lw and n_row % GROUP == 0
     assert n_row & (n_row - 1) == 0 and n_col & (n_col - 1) == 0
@@ -329,7 +329,7 @@
     fac_hi, fac_lo, own_raw, owned_list = pl.pallas_call(
         functools.partial(factor_kernel, order),
         out_shape=[jax.ShapeDtypeStruct((rows_dev, nb), BF16)] * 2
-        + [own_shape, jax.ShapeDtypeStruct((2 * (nb + GROUP_ROWS) + 8,), I32)],
+        + [own_shape, jax.ShapeDtypeStruct((nb + 2 * GROUP_ROWS,), I32)],
         in_specs=[SMEM] + [VMEM] * (n_col + 3),
         out_specs=[VMEM] * 3 + [SMEM],
         scratch_shapes=[pltpu.VMEM((2, nb, nb), F32)],

time: 53.3 us -> 52.7 us (0.989)
  no operation moved by 1% of the time
where the time goes in v5:
time: 52.7 us; the launch traced here: 52.4 us
  starting transfers between devices  19.9 us (38%)
  Pallas kernels  13.9 us (26%)
  waiting for transfers between devices  11 us (21%)
  other arithmetic  4.04 us (8%)
  local copies, waits for them, and re-layouts  2.67 us (5%)
  between operations  0.86 us (2%)
    ppermute x3, starting transfers between devices, on_device(): sent = lax.ppermute(head, 'row', [(i, i + bit) for i in range(bit)])  7.86 us
    ppermute x7, starting transfers between devices, across(): return lax.ppermute(v, 'row', [(i, i ^ s) for i in range(n_row)])  7.74 us
    ppermute x7, waiting for transfers between devices, across(): return lax.ppermute(v, 'row', [(i, i ^ s) for i in range(n_row)])  5.65 us
    pallas_call x1, Pallas kernels, on_device(): pl.pallas_call(final_kernel, out_shape=[jax.ShapeDtypeStruct((rows_dev, l...  4.93 us
    pallas_call x1, Pallas kernels, on_device(): pl.pallas_call(pick_kernel, out_shape=[message] * GROUP + [jax.ShapeDtype...  3.82 us
    pallas_call x1, Pallas kernels, on_device(): pl.pallas_call(functools.partial(factor_kernel, order), out_shape=[jax.Sh...  3.58 us
    ppermute x3, starting transfers between devices, on_device(): blocks[k ^ bit] = lax.ppermute(blocks[k], 'col', pairs)  3.11 us
    ppermute x3, waiting for transfers between devices, on_device(): sent = lax.ppermute(head, 'row', [(i, i + bit) for i in range(bit)])  3.07 us
  transfers between devices with their start and end apart: 16, of which 6 were waited for; matrix products, arithmetic and copies ran while one was open for 9% of the time, Pallas kernels for 17%

profile of v5, /device:TPU:0, one launch (start us, length us, event | category | flops | bytes accessed | tf_op | source)
XLA Modules:
  0.0 52.4 jit_solution(15054289052685285421)
XLA Ops:
  0.6 0.6 %collective-permute-start.1 = (f32[64,2048]{1,0:T(8,128)}, f32[64,2048]{1,0:T(8,128)S(1)}, u32[]{:S(2)}, u32[]{:S(2)}) collective-permute-start(f32[64,2048]{1,0:T(8,128)} %bitcast.6), channel_id=1, source_target_pairs={{0,1},{1,0},{2,3},{3,2},{4,5},{5,4},{6,7},{7,6},{8,9},{9,8},{10,11... | collective-permute-start | bytes 1572872 | tf_op jit(solution)/shard_map/ppermute | solution.py:311
  1.2 2.6 %collective-permute-start = (f32[64,2048]{1,0:T(8,128)}, f32[64,2048]{1,0:T(8,128)S(1)}, u32[]{:S(2)}, u32[]{:S(2)}) collective-permute-start(f32[64,2048]{1,0:T(8,128)} %bitcast.7), channel_id=1, source_target_pairs={{0,2},{1,3},{2,0},{3,1},{4,6},{5,7},{6,4},{7,5},{8,10},{9,11},{10,... | collective-permute-start | bytes 1572872 | tf_op jit(solution)/shard_map/ppermute | solution.py:311
  3.8 1.1 %copy-done.1 = f32[2048,64]{0,1:T(8,128)S(1)} copy-done((f32[2048,64]{0,1:T(8,128)S(1)}, f32[2048,64]{0,1:T(8,128)}, u32[]{:S(2)}) %copy-start.1) | copy-done | bytes 524312
  4.8 0.7 %copy-done.5 = s32[256]{0:T(256)S(1)} copy-done((s32[256]{0:T(256)S(1)}, s32[256]{0:T(256)}, u32[]{:S(2)}) %copy-start.5) | copy-done | bytes 1048
  5.5 3.8 %pick.1 = (f32[80,512]{1,0:T(8,128)S(1)}, f32[80,512]{1,0:T(8,128)S(1)}, f32[80,512]{1,0:T(8,128)S(1)}, f32[80,512]{1,0:T(8,128)S(1)}, f32[64,256]{1,0:T(8,128)S(1)}) custom-call(s32[256]{0:T(256)S(1)} %copy-done.5, f32[2048,512]{1,0:T(8,128)} %look.3, f32[64,2048]{1,0:T(8,128)S(1)} %bitcast.8, f32[256,2048]{1,0:T(8,128)} %sketch_map.1, s32[1,256]{1,0:T(1,128)S(1)} %bitcast.10), custom_call_target="tpu_custom_call" | custom-call | flops 1000000000 | bytes 4000000 | tf_op jit(solution)/shard_map/pick/pallas_call | solution.py:268
  9.3 3.4 %collective-permute-start.3 = (f32[64,256]{1,0:T(8,128)S(1)}, f32[64,256]{1,0:T(8,128)S(1)}, u32[]{:S(2)}, u32[]{:S(2)}) collective-permute-start(f32[64,256]{1,0:T(8,128)S(1)} %get-tuple-element.21), channel_id=1, source_target_pairs={{0,4},{1,5},{2,6},{3,7}} | collective-permute-start | bytes 196616 | tf_op jit(solution)/shard_map/ppermute | solution.py:315
  12.9 0.3 collective-permute-start.10
  13.2 0.1 dynamic_slice.7
  13.3 0.6 %fusion.2 = (pred[80]{0:T(512)(128)(4,1)S(1)}, pred[80]{0:T(512)(128)(4,1)}, pred[80]{0:T(512)(128)(4,1)S(1)}, pred[80]{0:T(512)(128)(4,1)S(1)}, pred[80]{0:T(51...) fusion(s32[64]{0:T(128)S(1)} %dynamic_slice.7, ...), kind=kLoop, calls=%fused_computation.33 | loop fusion | flops 2000 | bytes 1396 | tf_op jit(solution)/shard_map/or | solution.py:290
  13.9 0.1 constant_dynamic-slice_fusion
  14.0 0.7 %copy.11 = f32[256,64]{0,1:T(8,128)} copy(f32[256,64]{1,0:T(8,128)S(1)} %constant_dynamic-slice_fusion) | data formatting | bytes 131072
  14.7 0.5 %collective-permute-done.3 = f32[64,256]{1,0:T(8,128)S(1)} collective-permute-done((f32[64,256]{1,0:T(8,128)S(1)}, f32[64,256]{1,0:T(8,128)S(1)}, u32[]{:S(2)}, u32[]{:S(2)}) %collective-permute-start.3) | collective-permute-done | bytes 65568 | tf_op jit(solution)/shard_map/ppermute | solution.py:315
  15.3 3.1 %collective-permute-start.4 = (f32[64,256]{1,0:T(8,128)S(1)}, f32[64,256]{1,0:T(8,128)S(1)}, u32[]{:S(2)}, u32[]{:S(2)}) collective-permute-start(f32[64,256]{1,0:T(8,128)S(1)} %broadcast_select_fusion.6), channel_id=1, source_target_pairs={{0,8},{4,12},{1,9},{5,13},{2,10},{6,14},{3,11},{7,15}} | collective-permute-start | bytes 196616 | tf_op jit(solution)/shard_map/ppermute | solution.py:315
  18.4 1.9 %collective-permute-done.4 = f32[64,256]{1,0:T(8,128)S(1)} collective-permute-done((f32[64,256]{1,0:T(8,128)S(1)}, f32[64,256]{1,0:T(8,128)S(1)}, u32[]{:S(2)}, u32[]{:S(2)}) %collective-permute-start.4) | collective-permute-done | bytes 65568 | tf_op jit(solution)/shard_map/ppermute | solution.py:315
  20.3 3.7 %collective-permute-start.11 = (f32[80,512]{1,0:T(8,128)S(1)}, f32[80,512]{1,0:T(8,128)S(1)}, u32[]{:S(2)}, u32[]{:S(2)}) collective-permute-start(f32[80,512]{1,0:T(8,128)S(1)} %get-tuple-element.28.rest_3_), channel_id=1, source_target_pairs={{0,12},{4,8},{8,4},{12,0},{16,28},{20,24},{24,20},{28,16},{1,13},{... | collective-permute-start | bytes 491528 | tf_op jit(solution)/shard_map/ppermute | solution.py:265
  24.1 1.3 %collective-permute-start.5 = (f32[64,256]{1,0:T(8,128)S(1)}, f32[64,256]{1,0:T(8,128)S(1)}, u32[]{:S(2)}, u32[]{:S(2)}) collective-permute-start(f32[64,256]{1,0:T(8,128)S(1)} %broadcast_select_fusion.7), channel_id=1, source_target_pairs={{0,16},{4,20},{8,24},{12,28},{1,17},{5,21},{9,25},{13,29},{2,18},{... | collective-permute-start | bytes 196616 | tf_op jit(solution)/shard_map/ppermute | solution.py:315
  25.4 2.3 %collective-permute-done.11 = f32[80,512]{1,0:T(8,128)S(1)} collective-permute-done((f32[80,512]{1,0:T(8,128)S(1)}, f32[80,512]{1,0:T(8,128)S(1)}, u32[]{:S(2)}, u32[]{:S(2)}) %collective-permute-start.11) | collective-permute-done | bytes 163872 | tf_op jit(solution)/shard_map/ppermute | solution.py:265
  27.7 0.8 %broadcast_select_fusion.3 = (f32[80,512]{1,0:T(8,128)}, f32[80,512]{1,0:T(8,128)S(1)}, f32[80,512]{1,0:T(8,128)S(1)}) fusion(pred[80]{0:T(512)(128)(4,1)S(1)} %compare_or_fusion, f32[80,512]{1,0:T(8,128)S(1)} %collective-permute-done.11, f32[80,512]{1,0:T(8,128)S(1)} %collective-permute-done.10, f32[80,512]{1,0:T(8,128)S(1)} %collective-permute-done.9, ...), kind=kLoop, calls=%fused_computation.6 | loop fusion | flops 450560 | bytes 1147283 | tf_op jit(solution)/shard_map/jit(_where)/select_n | solution.py:297
  28.5 0.7 %collective-permute-done.5 = f32[64,256]{1,0:T(8,128)S(1)} collective-permute-done((f32[64,256]{1,0:T(8,128)S(1)}, f32[64,256]{1,0:T(8,128)S(1)}, u32[]{:S(2)}, u32[]{:S(2)}) %collective-permute-start.5) | collective-permute-done | bytes 65568 | tf_op jit(solution)/shard_map/ppermute | solution.py:315
  29.2 0.6 %collective-permute-start.6 = (f32[64,256]{1,0:T(8,128)S(1)}, f32[64,256]{1,0:T(8,128)S(1)}, u32[]{:S(2)}, u32[]{:S(2)}) collective-permute-start(f32[64,256]{1,0:T(8,128)S(1)} %broadcast_select_fusion.8.rest_0_), channel_id=1, source_target_pairs={{0,2},{1,3},{2,0},{3,1},{4,6},{5,7},{6,4},{7,5},{8,10},{9,11},{10,... | collective-permute-start | bytes 196616 | tf_op jit(solution)/shard_map/ppermute | solution.py:323
  29.8 0.9 %select_bitcast_fusion.rest_5_ = f32[64,256]{1,0:T(8,128)S(1)} fusion(f32[256,64]{0,1:T(8,128)} %copy.11, s32[]{:T(128)S(6)} %select_n.122, s32[256]{0:T(256)S(1)} %iota_add_fusion), kind=kLoop, calls=%fused_computation.10 | loop fusion | flops 49152 | bytes 132100 | tf_op jit(solution)/shard_map/transpose | solution.py:327
  30.6 0.6 %collective-permute-start.7 = (f32[64,256]{1,0:T(8,128)S(1)}, f32[64,256]{1,0:T(8,128)S(1)}, u32[]{:S(2)}, u32[]{:S(2)}) collective-permute-start(f32[64,256]{1,0:T(8,128)S(1)} %broadcast_select_fusion.8.rest_0_), channel_id=1, source_target_pairs={{0,1},{1,0},{2,3},{3,2},{4,5},{5,4},{6,7},{7,6},{8,9},{9,8},{10,11... | collective-permute-start | bytes 196616 | tf_op jit(solution)/shard_map/ppermute | solution.py:323
  31.2 2.3 %collective-permute-done.6.rest_1_ = f32[64,256]{1,0:T(8,128)S(1)} collective-permute-done((f32[64,256]{1,0:T(8,128)S(1)}, f32[64,256]{1,0:T(8,128)S(1)}, u32[]{:S(2)}, u32[]{:S(2)}) %collective-permute-start.6) | collective-permute-done | bytes 65568 | tf_op jit(solution)/shard_map/ppermute | solution.py:323
  33.5 3.3 %collective-permute-done.12 = f32[80,512]{1,0:T(8,128)} collective-permute-done((f32[80,512]{1,0:T(8,128)}, f32[80,512]{1,0:T(8,128)}, u32[]{:S(2)}, u32[]{:S(2)}) %collective-permute-start.12) | collective-permute-done | bytes 163872 | tf_op jit(solution)/shard_map/ppermute | solution.py:265
  36.8 1.0 %broadcast_select_fusion = (f32[80,512]{1,0:T(8,128)S(1)}, f32[80,512]{1,0:T(8,128)S(1)}, f32[80,512]{1,0:T(8,128)S(1)}) fusion(pred[80]{0:T(512)(128)(4,1)S(1)} %get-tuple-element.54, f32[80,512]{1,0:T(8,128)} %collective-permute-done.12, pred[80]{0:T(512)(128)(4,1)S(1)} %get-tuple-element.59, f32[80,512]{1,0:T(8,128)S(1)} %get-tuple-element.41, ...), kind=kLoop, calls=%fused_computation.3 | loop fusion | flops 204800 | bytes 983281 | tf_op jit(solution)/shard_map/jit(_where)/select_n | solution.py:303
  37.8 1.7 %collective-permute-start.15 = (f32[80,512]{1,0:T(8,128)S(1)}, f32[80,512]{1,0:T(8,128)S(1)}, u32[]{:S(2)}, u32[]{:S(2)}) collective-permute-start(f32[80,512]{1,0:T(8,128)S(1)} %get-tuple-element.33), channel_id=1, source_target_pairs={{0,12},{4,8},{8,4},{12,0},{16,28},{20,24},{24,20},{28,16},{1,13},{... | collective-permute-start | bytes 491528 | tf_op jit(solution)/shard_map/ppermute | solution.py:265
  39.5 0.8 %broadcast_select_fusion.1 = (f32[80,512]{1,0:T(8,128)S(1)}, f32[80,512]{1,0:T(8,128)S(1)}, f32[80,512]{1,0:T(8,128)S(1)}) fusion(f32[80,512]{1,0:T(8,128)S(1)} %get-tuple-element.35, f32[80,512]{1,0:T(8,128)S(1)} %get-tuple-element.34, pred[80]{0:T(512)(128)(4,1)} %get-tuple-element.58, pred[80]{0:T(512)(128)(4,1)} %get-tuple-element.56, ...), kind=kLoop, calls=%fused_computation.4 | loop fusion | flops 122880 | bytes 819440 | tf_op jit(solution)/shard_map/jit(_where)/select_n | solution.py:303
  40.3 0.1 collective-permute-start.14
  40.4 1.8 %collective-permute-start.13 = (f32[80,512]{1,0:T(8,128)S(1)}, f32[80,512]{1,0:T(8,128)S(1)}, u32[]{:S(2)}, u32[]{:S(2)}) collective-permute-start(f32[80,512]{1,0:T(8,128)S(1)} %get-tuple-element.51), channel_id=1, source_target_pairs={{0,4},{4,0},{8,12},{12,8},{16,20},{20,16},{24,28},{28,24},{1,5},{5... | collective-permute-start | bytes 491528 | tf_op jit(solution)/shard_map/ppermute | solution.py:265
  42.3 3.6 %factor.1 = (bf16[2048,256]{1,0:T(8,128)(2,1)S(1)}, bf16[2048,256]{1,0:T(8,128)(2,1)S(1)}, f32[64,2048]{1,0:T(8,128)S(1)}, s32[272]{0:T(512)S(1)}) custom-call(s32[256]{0:T(256)S(1)} %copy-done.6, s32[1,256]{1,0:T(1,128)S(1)} %bitcast.11, f32[64,2048]{1,0:T(8,128)S(1)} %bitcast.9, f32[64,2048]{1,0:T(8,128)S(1)} %collective-permute-done.rest_1_, ...), custom_call_target="tpu_custom_call" | custom-call | flops 1000000000 | bytes 4000000 | tf_op jit(solution)/shard_map/factor/pallas_call | solution.py:329
  45.9 1.6 %headfix.1 = (bf16[256,256]{1,0:T(8,128)(2,1)S(1)}, bf16[256,256]{1,0:T(8,128)(2,1)S(1)}, f32[64,2048]{1,0:T(8,128)}) custom-call(s32[1,256]{1,0:T(1,128)S(1)} %bitcast.12, f32[64,256]{1,0:T(8,128)S(1)} %broadcast_select_fusion.8.rest_0_, f32[64,256]{1,0:T(8,128)S(1)} %collective-permute-done.6.rest_1_, f32[64,256]{1,0:T(8,128)S(1)} %collective-permute-done.7.rest_2_, ...), custom_call_target="tpu_custom_call" | custom-call | flops 1000000000 | bytes 4000000 | tf_op jit(solution)/shard_map/headfix/pallas_call | solution.py:340
  47.5 4.9 %final.1 = (f32[2048,512]{1,0:T(8,128)}, f32[64,2048]{1,0:T(8,128)}, f32[64,256]{1,0:T(8,128)}) custom-call(s32[272]{0:T(512)S(1)} %get-tuple-element.18.owned_list, f32[2048,512]{1,0:T(8,128)S(1)} %copy-done, bf16[2048,256]{1,0:T(8,128)(2,1)S(1)} %get-tuple-element.19.fac_hi, ...), custom_call_target="tpu_custom_call", output_to_operand_aliasing={{1}: (16, {})} | custom-call | flops 2000000000 | bytes 12000000 | tf_op jit(solution)/shard_map/final/pallas_call | solution.py:352
  (32 shorter events, 0.2 us)
Async XLA Ops:
  0.6 12.6 %copy-start.6 = (s32[256]{0:T(256)S(1)}, s32[256]{0:T(256)}, u32[]{:S(2)}) copy-start(s32[256]{0:T(256)} %pivots.3) | copy-start | bytes 3076
  0.6 39.7 %collective-permute-start.1 = (f32[64,2048]{1,0:T(8,128)}, f32[64,2048]{1,0:T(8,128)S(1)}, u32[]{:S(2)}, u32[]{:S(2)}) collective-permute-start(f32[64,2048]{1,0:T(8,128)} %bitcast.6), channel_id=1, source_target_pairs={{0,1},{1,0},{2,3},{3,2},{4,5},{5,4},{6,7},{7,6},{8,9},{9,8},{10,11... | collective-permute-start | bytes 1572872 | tf_op jit(solution)/shard_map/ppermute | solution.py:311
  1.2 28.6 %collective-permute-start = (f32[64,2048]{1,0:T(8,128)}, f32[64,2048]{1,0:T(8,128)S(1)}, u32[]{:S(2)}, u32[]{:S(2)}) collective-permute-start(f32[64,2048]{1,0:T(8,128)} %bitcast.7), channel_id=1, source_target_pairs={{0,2},{1,3},{2,0},{3,1},{4,6},{5,7},{6,4},{7,5},{8,10},{9,11},{10,... | collective-permute-start | bytes 1572872 | tf_op jit(solution)/shard_map/ppermute | solution.py:311
  3.8 1.1 %copy-start.1 = (f32[2048,64]{0,1:T(8,128)S(1)}, f32[2048,64]{0,1:T(8,128)}, u32[]{:S(2)}) copy-start(f32[2048,64]{0,1:T(8,128)} %param.6) | copy-start | bytes 1572868
  4.8 0.7 %copy-start.5 = (s32[256]{0:T(256)S(1)}, s32[256]{0:T(256)}, u32[]{:S(2)}) copy-start(s32[256]{0:T(256)} %pivots.3) | copy-start | bytes 3076
  5.5 8.4 %copy-start.4 = (f32[256,256]{1,0:T(8,128)S(1)}, f32[256,256]{1,0:T(8,128)}, u32[]{:S(2)}) copy-start(f32[256,256]{1,0:T(8,128)} %rest_4_.3) | copy-start | bytes 786436
  5.5 36.7 %copy-start.2 = (f32[2048,64]{0,1:T(8,128)S(1)}, f32[2048,64]{0,1:T(8,128)}, u32[]{:S(2)}) copy-start(f32[2048,64]{0,1:T(8,128)} %param.6) | copy-start | bytes 1572868
  9.3 5.9 %collective-permute-start.3 = (f32[64,256]{1,0:T(8,128)S(1)}, f32[64,256]{1,0:T(8,128)S(1)}, u32[]{:S(2)}, u32[]{:S(2)}) collective-permute-start(f32[64,256]{1,0:T(8,128)S(1)} %get-tuple-element.21), channel_id=1, source_target_pairs={{0,4},{1,5},{2,6},{3,7}} | collective-permute-start | bytes 196616 | tf_op jit(solution)/shard_map/ppermute | solution.py:315
  12.8 11.3 %collective-permute-start.9 = (f32[80,512]{1,0:T(8,128)S(1)}, f32[80,512]{1,0:T(8,128)S(1)}, u32[]{:S(2)}, u32[]{:S(2)}) collective-permute-start(f32[80,512]{1,0:T(8,128)S(1)} %get-tuple-element.26.rest_1_), channel_id=1, source_target_pairs={{0,4},{4,0},{8,12},{12,8},{16,20},{20,16},{24,28},{28,24},{1,5},{5... | collective-permute-start | bytes 491528 | tf_op jit(solution)/shard_map/ppermute | solution.py:265
  12.9 12.5 %collective-permute-start.10 = (f32[80,512]{1,0:T(8,128)S(1)}, f32[80,512]{1,0:T(8,128)S(1)}, u32[]{:S(2)}, u32[]{:S(2)}) collective-permute-start(f32[80,512]{1,0:T(8,128)S(1)} %get-tuple-element.27.rest_2_), channel_id=1, source_target_pairs={{0,8},{4,12},{8,0},{12,4},{16,24},{20,28},{24,16},{28,20},{1,9},{5... | collective-permute-start | bytes 491528 | tf_op jit(solution)/shard_map/ppermute | solution.py:265
  15.3 5.0 %collective-permute-start.4 = (f32[64,256]{1,0:T(8,128)S(1)}, f32[64,256]{1,0:T(8,128)S(1)}, u32[]{:S(2)}, u32[]{:S(2)}) collective-permute-start(f32[64,256]{1,0:T(8,128)S(1)} %broadcast_select_fusion.6), channel_id=1, source_target_pairs={{0,8},{4,12},{1,9},{5,13},{2,10},{6,14},{3,11},{7,15}} | collective-permute-start | bytes 196616 | tf_op jit(solution)/shard_map/ppermute | solution.py:315
  20.3 7.4 %collective-permute-start.11 = (f32[80,512]{1,0:T(8,128)S(1)}, f32[80,512]{1,0:T(8,128)S(1)}, u32[]{:S(2)}, u32[]{:S(2)}) collective-permute-start(f32[80,512]{1,0:T(8,128)S(1)} %get-tuple-element.28.rest_3_), channel_id=1, source_target_pairs={{0,12},{4,8},{8,4},{12,0},{16,28},{20,24},{24,20},{28,16},{1,13},{... | collective-permute-start | bytes 491528 | tf_op jit(solution)/shard_map/ppermute | solution.py:265
  24.1 5.1 %collective-permute-start.5 = (f32[64,256]{1,0:T(8,128)S(1)}, f32[64,256]{1,0:T(8,128)S(1)}, u32[]{:S(2)}, u32[]{:S(2)}) collective-permute-start(f32[64,256]{1,0:T(8,128)S(1)} %broadcast_select_fusion.7), channel_id=1, source_target_pairs={{0,16},{4,20},{8,24},{12,28},{1,17},{5,21},{9,25},{13,29},{2,18},{... | collective-permute-start | bytes 196616 | tf_op jit(solution)/shard_map/ppermute | solution.py:315
  28.5 8.3 %collective-permute-start.12 = (f32[80,512]{1,0:T(8,128)}, f32[80,512]{1,0:T(8,128)}, u32[]{:S(2)}, u32[]{:S(2)}) collective-permute-start(f32[80,512]{1,0:T(8,128)} %get-tuple-element.39), channel_id=1, source_target_pairs={{0,16},{4,20},{8,24},{12,28},{16,0},{20,4},{24,8},{28,12},{1,17},{... | collective-permute-start | bytes 491528 | tf_op jit(solution)/shard_map/ppermute | solution.py:265
  29.2 4.3 %collective-permute-start.6 = (f32[64,256]{1,0:T(8,128)S(1)}, f32[64,256]{1,0:T(8,128)S(1)}, u32[]{:S(2)}, u32[]{:S(2)}) collective-permute-start(f32[64,256]{1,0:T(8,128)S(1)} %broadcast_select_fusion.8.rest_0_), channel_id=1, source_target_pairs={{0,2},{1,3},{2,0},{3,1},{4,6},{5,7},{6,4},{7,5},{8,10},{9,11},{10,... | collective-permute-start | bytes 196616 | tf_op jit(solution)/shard_map/ppermute | solution.py:323
  29.8 10.6 %collective-permute-start.2 = (f32[64,2048]{1,0:T(8,128)S(1)}, f32[64,2048]{1,0:T(8,128)S(1)}, u32[]{:S(2)}, u32[]{:S(2)}) collective-permute-start(f32[64,2048]{1,0:T(8,128)S(1)} %collective-permute-done.rest_1_), channel_id=1, source_target_pairs={{0,1},{1,0},{2,3},{3,2},{4,5},{5,4},{6,7},{7,6},{8,9},{9,8},{10,11... | collective-permute-start | bytes 1572872 | tf_op jit(solution)/shard_map/ppermute | solution.py:311
  30.6 15.2 %collective-permute-start.7 = (f32[64,256]{1,0:T(8,128)S(1)}, f32[64,256]{1,0:T(8,128)S(1)}, u32[]{:S(2)}, u32[]{:S(2)}) collective-permute-start(f32[64,256]{1,0:T(8,128)S(1)} %broadcast_select_fusion.8.rest_0_), channel_id=1, source_target_pairs={{0,1},{1,0},{2,3},{3,2},{4,5},{5,4},{6,7},{7,6},{8,9},{9,8},{10,11... | collective-permute-start | bytes 196616 | tf_op jit(solution)/shard_map/ppermute | solution.py:323
  33.5 12.3 %collective-permute-start.8 = (f32[64,256]{1,0:T(8,128)S(1)}, f32[64,256]{1,0:T(8,128)S(1)}, u32[]{:S(2)}, u32[]{:S(2)}) collective-permute-start(f32[64,256]{1,0:T(8,128)S(1)} %collective-permute-done.6.rest_1_), channel_id=1, source_target_pairs={{0,1},{1,0},{2,3},{3,2},{4,5},{5,4},{6,7},{7,6},{8,9},{9,8},{10,11... | collective-permute-start | bytes 196616 | tf_op jit(solution)/shard_map/ppermute | solution.py:323
  37.8 9.6 %copy-start = (f32[2048,512]{1,0:T(8,128)S(1)}, f32[2048,512]{1,0:T(8,128)}, u32[]{:S(2)}) copy-start(f32[2048,512]{1,0:T(8,128)} %look.3) | copy-start | bytes 12582916
  37.8 9.6 %copy-start.3 = (f32[256,256]{1,0:T(8,128)S(1)}, f32[256,256]{1,0:T(8,128)}, u32[]{:S(2)}) copy-start(f32[256,256]{1,0:T(8,128)} %lower.1) | copy-start | bytes 786436
  37.8 9.6 %collective-permute-start.15 = (f32[80,512]{1,0:T(8,128)S(1)}, f32[80,512]{1,0:T(8,128)S(1)}, u32[]{:S(2)}, u32[]{:S(2)}) collective-permute-start(f32[80,512]{1,0:T(8,128)S(1)} %get-tuple-element.33), channel_id=1, source_target_pairs={{0,12},{4,8},{8,4},{12,0},{16,28},{20,24},{24,20},{28,16},{1,13},{... | collective-permute-start | bytes 491528 | tf_op jit(solution)/shard_map/ppermute | solution.py:265
  40.3 7.1 %collective-permute-start.14 = (f32[80,512]{1,0:T(8,128)S(1)}, f32[80,512]{1,0:T(8,128)S(1)}, u32[]{:S(2)}, u32[]{:S(2)}) collective-permute-start(f32[80,512]{1,0:T(8,128)S(1)} %get-tuple-element.50), channel_id=1, source_target_pairs={{0,8},{4,12},{8,0},{12,4},{16,24},{20,28},{24,16},{28,20},{1,9},{5... | collective-permute-start | bytes 491528 | tf_op jit(solution)/shard_map/ppermute | solution.py:265
  40.4 7.0 %collective-permute-start.13 = (f32[80,512]{1,0:T(8,128)S(1)}, f32[80,512]{1,0:T(8,128)S(1)}, u32[]{:S(2)}, u32[]{:S(2)}) collective-permute-start(f32[80,512]{1,0:T(8,128)S(1)} %get-tuple-element.51), channel_id=1, source_target_pairs={{0,4},{4,0},{8,12},{12,8},{16,20},{20,16},{24,28},{28,24},{1,5},{5... | collective-permute-start | bytes 491528 | tf_op jit(solution)/shard_map/ppermute | solution.py:265

commit v6 on v5

--- a/solution.py
+++ b/solution.py
@@ -116,43 +116,32 @@
     return split2(jnp.where(keep, upper[...], 0.0))
 
 
-def factor_kernel(order, pivots, pivot_row, *rest):
-    blocks, (upper, upper_own, fac_hi, fac_lo, own_out, owned_list, whole) = (
+def factor_kernel(order, pivot_row, *rest):
+    blocks, (upper, upper_own, fac_hi, fac_lo, own_out, whole) = (
         rest[: len(order)],
         rest[len(order) :],
     )
     cw, rows_dev = blocks[0].shape
     nb = upper.shape[0]
-    wide = nb + GROUP_ROWS
     col = lax.axis_index("col")
     first = lax.axis_index("row") * rows_dev
     target = pivot_row[...] - first
     tri = triangle(upper)
     own = split2(upper_own[...])
-    steps = rows_dev // nb
-    count = jnp.int32(0)
-    for b in range(steps):
+    for b in range(rows_dev // nb):
         lanes = pl.ds(b * nb, nb)
         for k, block in zip(order, blocks):
             whole[b % 2, pl.ds(pl.multiple_of((col ^ k) * cw, 8), cw), :] = block[:, lanes]
-        for p in range(b * nb // steps, (b + 1) * nb // steps):
-            there = pivots[p] - first
-            owned_list[count] = there + (p << 16)
-            count = count + (there.astype(jnp.uint32) < jnp.uint32(rows_dev)).astype(I32)
         data = whole[b % 2]
         place = lax.broadcasted_iota(I32, (nb, nb), 0) + b * nb
         hit = jnp.max(jnp.where(place == target, 1.0, 0.0), axis=1, keepdims=True)
         fac = jnp.where(hit > 0.5, 0.0, mm3(split2(data.T), tri))
         fac_hi[lanes, :], fac_lo[lanes, :] = split2(fac)
         own_out[:, lanes] = mm3(own, split2(data))
-    last = owned_list[jnp.maximum(count - 1, 0)]
-    for i in range(GROUP_ROWS):
-        owned_list[count + i] = last
-    owned_list[wide] = count
-
-
-def head_kernel(order, pivot_row, *rest):
-    heads, (upper, upper_own, own_in, top_hi, top_lo, own_out, top) = (
+
+
+def head_kernel(order, pivots, pivot_row, *rest):
+    heads, (upper, upper_own, own_in, top_hi, top_lo, own_out, owned_list, top) = (
         rest[: len(order)],
         rest[len(order) :],
     )
@@ -165,12 +154,24 @@
     top_hi[...], top_lo[...] = split2(mm3(split2(data.T), triangle(upper)))
     parts = split3(mm3(split2(upper_own[...]), split2(data)))
     left = jnp.concatenate([*parts, jnp.ones((16, nb), BF16)])
-    target = pivot_row[...] - lax.axis_index("row") * rows_dev
-    for b in range(rows_dev // nb):
+    first = lax.axis_index("row") * rows_dev
+    target = pivot_row[...] - first
+    wide = nb + GROUP_ROWS
+    steps = rows_dev // nb
+    count = jnp.int32(0)
+    for b in range(steps):
+        for p in range(b * nb // steps, (b + 1) * nb // steps):
+            there = pivots[p] - first
+            owned_list[count] = there + (p << 16)
+            count = count + (there.astype(jnp.uint32) < jnp.uint32(rows_dev)).astype(I32)
         part = pl.ds(b * nb, nb)
         moved = mm(left, one_hot(target, b * nb, nb), ((1,), (1,)))
         new = (moved[:cw] + moved[cw : 2 * cw]) + moved[2 * cw : 3 * cw]
         own_out[:, part] = jnp.where(moved[3 * cw : 3 * cw + 1] > 0.5, new, own_in[:, part])
+    last = owned_list[jnp.maximum(count - 1, 0)]
+    for i in range(GROUP_ROWS):
+        owned_list[count + i] = last
+    owned_list[wide] = count
 
 
 def final_kernel(owned_list, look, fac_hi, fac_lo, top_hi, top_lo, lower, pivot_row, *rest):
@@ -326,27 +327,28 @@
     blocks = [blocks[k] for k in order]
     upper_own = lax.dynamic_slice_in_dim(jnp.triu(upper_inv), col * cw, cw, 1).T
     own_shape = jax.ShapeDtypeStruct((cw, rows_dev), F32)
-    fac_hi, fac_lo, own_raw, owned_list = pl.pallas_call(
+    fac_hi, fac_lo, own_raw = pl.pallas_call(
         functools.partial(factor_kernel, order),
         out_shape=[jax.ShapeDtypeStruct((rows_dev, nb), BF16)] * 2
-        + [own_shape, jax.ShapeDtypeStruct((nb + 2 * GROUP_ROWS,), I32)],
-        in_specs=[SMEM] + [VMEM] * (n_col + 3),
-        out_specs=[VMEM] * 3 + [SMEM],
+        + [own_shape],
+        in_specs=[VMEM] * (n_col + 3),
+        out_specs=[VMEM] * 3,
         scratch_shapes=[pltpu.VMEM((2, nb, nb), F32)],
         cost_estimate=pl.CostEstimate(flops=10**9, bytes_accessed=4 * 10**6, transcendentals=0),
         compiler_params=pltpu.CompilerParams(vmem_limit_bytes=FACTOR_VMEM),
         name="factor",
-    )(pivots, pivot_row, *blocks, upper_inv, upper_own)
-    top_hi, top_lo, panel_out = pl.pallas_call(
+    )(pivot_row, *blocks, upper_inv, upper_own)
+    top_hi, top_lo, panel_out, owned_list = pl.pallas_call(
         functools.partial(head_kernel, order),
-        out_shape=[jax.ShapeDtypeStruct((nb, nb), BF16)] * 2 + [own_shape],
-        in_specs=[VMEM] * (4 + n_col),
-        out_specs=[VMEM] * 3,
+        out_shape=[jax.ShapeDtypeStruct((nb, nb), BF16)] * 2
+        + [own_shape, jax.ShapeDtypeStruct((nb + 2 * GROUP_ROWS,), I32)],
+        in_specs=[SMEM] + [VMEM] * (4 + n_col),
+        out_specs=[VMEM] * 3 + [SMEM],
         scratch_shapes=[pltpu.VMEM((nb, nb), F32)],
         cost_estimate=pl.CostEstimate(flops=10**9, bytes_accessed=4 * 10**6, transcendentals=0),
         compiler_params=pltpu.CompilerParams(vmem_limit_bytes=FACTOR_VMEM),
         name="headfix",
-    )(pivot_row, *heads.values(), upper_inv, upper_own, own_raw)
+    )(pivots, pivot_row, *heads.values(), upper_inv, upper_own, own_raw)
 
     n_in = 8 + 2 * GROUP
     updated, panel_out, sketch_t = pl.pallas_call(

time: 52.7 us -> 51.9 us (0.985)
  Pallas kernels: 13.9 us -> 13 us
    pallas_call x1, Pallas kernels: 3.58 us -> 1.94 us  [on_device(): pl.pallas_call(functools.partial(factor_kernel, order), out_shape=[jax.Sh...]
    pallas_call x1, Pallas kernels: 1.57 us -> 2.34 us  [on_device(): pl.pallas_call(functools.partial(head_kernel, order), out_shape=[jax.Shap...]
  transfers between devices with their start and end apart: 16 -> 16, of which waited for: 6 -> 6; matrix products, arithmetic and copies ran while one was open for 9% -> 10% of each run, Pallas kernels for 17% -> 16%
where the time goes in v6:
time: 51.9 us; the launch traced here: 51.5 us
  starting transfers between devices  19.9 us (38%)
  Pallas kernels  13 us (25%)
  waiting for transfers between devices  11 us (21%)
  other arithmetic  4.04 us (8%)
  local copies, waits for them, and re-layouts  2.67 us (5%)
  between operations  0.89 us (2%)
    ppermute x3, starting transfers between devices, on_device(): sent = lax.ppermute(head, 'row', [(i, i + bit) for i in range(bit)])  7.86 us
    ppermute x7, starting transfers between devices, across(): return lax.ppermute(v, 'row', [(i, i ^ s) for i in range(n_row)])  7.74 us
    ppermute x7, waiting for transfers between devices, across(): return lax.ppermute(v, 'row', [(i, i ^ s) for i in range(n_row)])  5.65 us
    pallas_call x1, Pallas kernels, on_device(): pl.pallas_call(final_kernel, out_shape=[jax.ShapeDtypeStruct((rows_dev, l...  4.93 us
    pallas_call x1, Pallas kernels, on_device(): pl.pallas_call(pick_kernel, out_shape=[message] * GROUP + [jax.ShapeDtype...  3.82 us
    ppermute x3, starting transfers between devices, on_device(): blocks[k ^ bit] = lax.ppermute(blocks[k], 'col', pairs)  3.11 us
    ppermute x3, waiting for transfers between devices, on_device(): sent = lax.ppermute(head, 'row', [(i, i + bit) for i in range(bit)])  3.07 us
    unnamed x15, local copies, waits for them, and re-layouts  2.49 us
  transfers between devices with their start and end apart: 16, of which 6 were waited for; matrix products, arithmetic and copies ran while one was open for 10% of the time, Pallas kernels for 16%

profile of v6, /device:TPU:0, one launch (start us, length us, event | category | flops | bytes accessed | tf_op | source)
XLA Modules:
  0.0 51.5 jit_solution(15035265446877104453)
XLA Ops:
  0.6 0.6 %collective-permute-start.7 = (f32[64,2048]{1,0:T(8,128)}, f32[64,2048]{1,0:T(8,128)S(1)}, u32[]{:S(2)}, u32[]{:S(2)}) collective-permute-start(f32[64,2048]{1,0:T(8,128)} %bitcast.6), channel_id=1, source_target_pairs={{0,1},{1,0},{2,3},{3,2},{4,5},{5,4},{6,7},{7,6},{8,9},{9,8},{10,11... | collective-permute-start | bytes 1572872 | tf_op jit(solution)/shard_map/ppermute | solution.py:312
  1.2 2.6 %collective-permute-start.6 = (f32[64,2048]{1,0:T(8,128)}, f32[64,2048]{1,0:T(8,128)S(1)}, u32[]{:S(2)}, u32[]{:S(2)}) collective-permute-start(f32[64,2048]{1,0:T(8,128)} %bitcast.7), channel_id=1, source_target_pairs={{0,2},{1,3},{2,0},{3,1},{4,6},{5,7},{6,4},{7,5},{8,10},{9,11},{10,... | collective-permute-start | bytes 1572872 | tf_op jit(solution)/shard_map/ppermute | solution.py:312
  3.8 1.1 %copy-done.1 = f32[2048,64]{0,1:T(8,128)S(1)} copy-done((f32[2048,64]{0,1:T(8,128)S(1)}, f32[2048,64]{0,1:T(8,128)}, u32[]{:S(2)}) %copy-start.1) | copy-done | bytes 524312
  4.8 0.7 %copy-done.5 = s32[256]{0:T(256)S(1)} copy-done((s32[256]{0:T(256)S(1)}, s32[256]{0:T(256)}, u32[]{:S(2)}) %copy-start.5) | copy-done | bytes 1048
  5.5 3.8 %pick.1 = (f32[80,512]{1,0:T(8,128)S(1)}, f32[80,512]{1,0:T(8,128)S(1)}, f32[80,512]{1,0:T(8,128)S(1)}, f32[80,512]{1,0:T(8,128)S(1)}, f32[64,256]{1,0:T(8,128)S(1)}) custom-call(s32[256]{0:T(256)S(1)} %copy-done.5, f32[2048,512]{1,0:T(8,128)} %look.3, f32[64,2048]{1,0:T(8,128)S(1)} %bitcast.8, f32[256,2048]{1,0:T(8,128)} %sketch_map.1, s32[1,256]{1,0:T(1,128)S(1)} %bitcast.10), custom_call_target="tpu_custom_call" | custom-call | flops 1000000000 | bytes 4000000 | tf_op jit(solution)/shard_map/pick/pallas_call | solution.py:269
  9.3 3.4 %collective-permute-start = (f32[64,256]{1,0:T(8,128)S(1)}, f32[64,256]{1,0:T(8,128)S(1)}, u32[]{:S(2)}, u32[]{:S(2)}) collective-permute-start(f32[64,256]{1,0:T(8,128)S(1)} %get-tuple-element.18), channel_id=1, source_target_pairs={{0,4},{1,5},{2,6},{3,7}} | collective-permute-start | bytes 196616 | tf_op jit(solution)/shard_map/ppermute | solution.py:316
  12.8 0.1 collective-permute-start.9
  12.9 0.3 collective-permute-start.10
  13.2 0.1 dynamic_slice.7
  13.3 0.6 %fusion.2 = (pred[80]{0:T(512)(128)(4,1)S(1)}, pred[80]{0:T(512)(128)(4,1)}, pred[80]{0:T(512)(128)(4,1)S(1)}, pred[80]{0:T(512)(128)(4,1)S(1)}, pred[80]{0:T(51...) fusion(s32[64]{0:T(128)S(1)} %dynamic_slice.7, ...), kind=kLoop, calls=%fused_computation.33 | loop fusion | flops 2000 | bytes 1396 | tf_op jit(solution)/shard_map/or | solution.py:291
  13.9 0.1 constant_dynamic-slice_fusion
  14.0 0.7 %copy.11 = f32[256,64]{0,1:T(8,128)} copy(f32[256,64]{1,0:T(8,128)S(1)} %constant_dynamic-slice_fusion) | data formatting | bytes 131072
  14.7 0.5 %collective-permute-done = f32[64,256]{1,0:T(8,128)S(1)} collective-permute-done((f32[64,256]{1,0:T(8,128)S(1)}, f32[64,256]{1,0:T(8,128)S(1)}, u32[]{:S(2)}, u32[]{:S(2)}) %collective-permute-start) | collective-permute-done | bytes 65568 | tf_op jit(solution)/shard_map/ppermute | solution.py:316
  15.3 3.1 %collective-permute-start.1 = (f32[64,256]{1,0:T(8,128)S(1)}, f32[64,256]{1,0:T(8,128)S(1)}, u32[]{:S(2)}, u32[]{:S(2)}) collective-permute-start(f32[64,256]{1,0:T(8,128)S(1)} %broadcast_select_fusion.6), channel_id=1, source_target_pairs={{0,8},{4,12},{1,9},{5,13},{2,10},{6,14},{3,11},{7,15}} | collective-permute-start | bytes 196616 | tf_op jit(solution)/shard_map/ppermute | solution.py:316
  18.4 1.9 %collective-permute-done.1 = f32[64,256]{1,0:T(8,128)S(1)} collective-permute-done((f32[64,256]{1,0:T(8,128)S(1)}, f32[64,256]{1,0:T(8,128)S(1)}, u32[]{:S(2)}, u32[]{:S(2)}) %collective-permute-start.1) | collective-permute-done | bytes 65568 | tf_op jit(solution)/shard_map/ppermute | solution.py:316
  20.3 3.7 %collective-permute-start.11 = (f32[80,512]{1,0:T(8,128)S(1)}, f32[80,512]{1,0:T(8,128)S(1)}, u32[]{:S(2)}, u32[]{:S(2)}) collective-permute-start(f32[80,512]{1,0:T(8,128)S(1)} %get-tuple-element.28.rest_3_), channel_id=1, source_target_pairs={{0,12},{4,8},{8,4},{12,0},{16,28},{20,24},{24,20},{28,16},{1,13},{... | collective-permute-start | bytes 491528 | tf_op jit(solution)/shard_map/ppermute | solution.py:266
  24.1 1.3 %collective-permute-start.2 = (f32[64,256]{1,0:T(8,128)S(1)}, f32[64,256]{1,0:T(8,128)S(1)}, u32[]{:S(2)}, u32[]{:S(2)}) collective-permute-start(f32[64,256]{1,0:T(8,128)S(1)} %broadcast_select_fusion.7), channel_id=1, source_target_pairs={{0,16},{4,20},{8,24},{12,28},{1,17},{5,21},{9,25},{13,29},{2,18},{... | collective-permute-start | bytes 196616 | tf_op jit(solution)/shard_map/ppermute | solution.py:316
  25.4 2.3 %collective-permute-done.11 = f32[80,512]{1,0:T(8,128)S(1)} collective-permute-done((f32[80,512]{1,0:T(8,128)S(1)}, f32[80,512]{1,0:T(8,128)S(1)}, u32[]{:S(2)}, u32[]{:S(2)}) %collective-permute-start.11) | collective-permute-done | bytes 163872 | tf_op jit(solution)/shard_map/ppermute | solution.py:266
  27.7 0.8 %broadcast_select_fusion.3 = (f32[80,512]{1,0:T(8,128)}, f32[80,512]{1,0:T(8,128)S(1)}, f32[80,512]{1,0:T(8,128)S(1)}) fusion(pred[80]{0:T(512)(128)(4,1)S(1)} %compare_or_fusion, f32[80,512]{1,0:T(8,128)S(1)} %collective-permute-done.11, f32[80,512]{1,0:T(8,128)S(1)} %collective-permute-done.10, f32[80,512]{1,0:T(8,128)S(1)} %collective-permute-done.9, ...), kind=kLoop, calls=%fused_computation.6 | loop fusion | flops 450560 | bytes 1147283 | tf_op jit(solution)/shard_map/jit(_where)/select_n | solution.py:298
  28.5 0.7 %collective-permute-done.2 = f32[64,256]{1,0:T(8,128)S(1)} collective-permute-done((f32[64,256]{1,0:T(8,128)S(1)}, f32[64,256]{1,0:T(8,128)S(1)}, u32[]{:S(2)}, u32[]{:S(2)}) %collective-permute-start.2) | collective-permute-done | bytes 65568 | tf_op jit(solution)/shard_map/ppermute | solution.py:316
  29.2 0.6 %collective-permute-start.3 = (f32[64,256]{1,0:T(8,128)S(1)}, f32[64,256]{1,0:T(8,128)S(1)}, u32[]{:S(2)}, u32[]{:S(2)}) collective-permute-start(f32[64,256]{1,0:T(8,128)S(1)} %broadcast_select_fusion.8.rest_0_), channel_id=1, source_target_pairs={{0,2},{1,3},{2,0},{3,1},{4,6},{5,7},{6,4},{7,5},{8,10},{9,11},{10,... | collective-permute-start | bytes 196616 | tf_op jit(solution)/shard_map/ppermute | solution.py:324
  29.8 0.9 %select_bitcast_fusion.rest_5_ = f32[64,256]{1,0:T(8,128)S(1)} fusion(f32[256,64]{0,1:T(8,128)} %copy.11, s32[]{:T(128)S(6)} %select_n.130, s32[256]{0:T(256)S(1)} %iota_add_fusion), kind=kLoop, calls=%fused_computation.10 | loop fusion | flops 49152 | bytes 132100 | tf_op jit(solution)/shard_map/transpose | solution.py:328
  30.6 0.6 %collective-permute-start.4 = (f32[64,256]{1,0:T(8,128)S(1)}, f32[64,256]{1,0:T(8,128)S(1)}, u32[]{:S(2)}, u32[]{:S(2)}) collective-permute-start(f32[64,256]{1,0:T(8,128)S(1)} %broadcast_select_fusion.8.rest_0_), channel_id=1, source_target_pairs={{0,1},{1,0},{2,3},{3,2},{4,5},{5,4},{6,7},{7,6},{8,9},{9,8},{10,11... | collective-permute-start | bytes 196616 | tf_op jit(solution)/shard_map/ppermute | solution.py:324
  31.2 2.3 %collective-permute-done.3.rest_1_ = f32[64,256]{1,0:T(8,128)S(1)} collective-permute-done((f32[64,256]{1,0:T(8,128)S(1)}, f32[64,256]{1,0:T(8,128)S(1)}, u32[]{:S(2)}, u32[]{:S(2)}) %collective-permute-start.3) | collective-permute-done | bytes 65568 | tf_op jit(solution)/shard_map/ppermute | solution.py:324
  33.5 3.3 %collective-permute-done.12 = f32[80,512]{1,0:T(8,128)} collective-permute-done((f32[80,512]{1,0:T(8,128)}, f32[80,512]{1,0:T(8,128)}, u32[]{:S(2)}, u32[]{:S(2)}) %collective-permute-start.12) | collective-permute-done | bytes 163872 | tf_op jit(solution)/shard_map/ppermute | solution.py:266
  36.8 1.0 %broadcast_select_fusion = (f32[80,512]{1,0:T(8,128)S(1)}, f32[80,512]{1,0:T(8,128)S(1)}, f32[80,512]{1,0:T(8,128)S(1)}) fusion(pred[80]{0:T(512)(128)(4,1)S(1)} %get-tuple-element.54, f32[80,512]{1,0:T(8,128)} %collective-permute-done.12, pred[80]{0:T(512)(128)(4,1)S(1)} %get-tuple-element.59, f32[80,512]{1,0:T(8,128)S(1)} %get-tuple-element.41, ...), kind=kLoop, calls=%fused_computation.3 | loop fusion | flops 204800 | bytes 983281 | tf_op jit(solution)/shard_map/jit(_where)/select_n | solution.py:304
  37.8 1.7 %collective-permute-start.15 = (f32[80,512]{1,0:T(8,128)S(1)}, f32[80,512]{1,0:T(8,128)S(1)}, u32[]{:S(2)}, u32[]{:S(2)}) collective-permute-start(f32[80,512]{1,0:T(8,128)S(1)} %get-tuple-element.33), channel_id=1, source_target_pairs={{0,12},{4,8},{8,4},{12,0},{16,28},{20,24},{24,20},{28,16},{1,13},{... | collective-permute-start | bytes 491528 | tf_op jit(solution)/shard_map/ppermute | solution.py:266
  39.5 0.8 %broadcast_select_fusion.1 = (f32[80,512]{1,0:T(8,128)S(1)}, f32[80,512]{1,0:T(8,128)S(1)}, f32[80,512]{1,0:T(8,128)S(1)}) fusion(f32[80,512]{1,0:T(8,128)S(1)} %get-tuple-element.35, f32[80,512]{1,0:T(8,128)S(1)} %get-tuple-element.34, pred[80]{0:T(512)(128)(4,1)} %get-tuple-element.58, pred[80]{0:T(512)(128)(4,1)} %get-tuple-element.56, ...), kind=kLoop, calls=%fused_computation.4 | loop fusion | flops 122880 | bytes 819440 | tf_op jit(solution)/shard_map/jit(_where)/select_n | solution.py:304
  40.4 1.8 %collective-permute-start.13 = (f32[80,512]{1,0:T(8,128)S(1)}, f32[80,512]{1,0:T(8,128)S(1)}, u32[]{:S(2)}, u32[]{:S(2)}) collective-permute-start(f32[80,512]{1,0:T(8,128)S(1)} %get-tuple-element.51), channel_id=1, source_target_pairs={{0,4},{4,0},{8,12},{12,8},{16,20},{20,16},{24,28},{28,24},{1,5},{5... | collective-permute-start | bytes 491528 | tf_op jit(solution)/shard_map/ppermute | solution.py:266
  42.3 1.9 %factor.1 = (bf16[2048,256]{1,0:T(8,128)(2,1)S(1)}, bf16[2048,256]{1,0:T(8,128)(2,1)S(1)}, f32[64,2048]{1,0:T(8,128)S(1)}) custom-call(s32[1,256]{1,0:T(1,128)S(1)} %bitcast.11, f32[64,2048]{1,0:T(8,128)S(1)} %bitcast.9, f32[64,2048]{1,0:T(8,128)S(1)} %collective-permute-done.6.rest_1_, f32[64,2048]{1,0:T(8,128)S(1)} %collective-permute-done.7.rest_2_, ...), custom_call_target="tpu_custom_call" | custom-call | flops 1000000000 | bytes 4000000 | tf_op jit(solution)/shard_map/factor/pallas_call | solution.py:330
  44.2 2.3 %headfix.1 = (bf16[256,256]{1,0:T(8,128)(2,1)S(1)}, bf16[256,256]{1,0:T(8,128)(2,1)S(1)}, f32[64,2048]{1,0:T(8,128)}, s32[272]{0:T(512)S(1)}) custom-call(s32[256]{0:T(256)S(1)} %copy-done.6, s32[1,256]{1,0:T(1,128)S(1)} %bitcast.12, f32[64,256]{1,0:T(8,128)S(1)} %broadcast_select_fusion.8.rest_0_, f32[64,256]{1,0:T(8,128)S(1)} %collective-permute-done.3.rest_1_, ...), custom_call_target="tpu_custom_call" | custom-call | flops 1000000000 | bytes 4000000 | tf_op jit(solution)/shard_map/headfix/pallas_call | solution.py:341
  46.6 4.9 %final.1 = (f32[2048,512]{1,0:T(8,128)}, f32[64,2048]{1,0:T(8,128)}, f32[64,256]{1,0:T(8,128)}) custom-call(s32[272]{0:T(512)S(1)} %get-tuple-element.20.owned_list, f32[2048,512]{1,0:T(8,128)S(1)} %copy-done, bf16[2048,256]{1,0:T(8,128)(2,1)S(1)} %get-tuple-element.21.fac_hi, ...), custom_call_target="tpu_custom_call", output_to_operand_aliasing={{1}: (16, {})} | custom-call | flops 2000000000 | bytes 12000000 | tf_op jit(solution)/shard_map/final/pallas_call | solution.py:354
  (32 shorter events, 0.2 us)
Async XLA Ops:
  0.6 12.6 %copy-start.6 = (s32[256]{0:T(256)S(1)}, s32[256]{0:T(256)}, u32[]{:S(2)}) copy-start(s32[256]{0:T(256)} %pivots.3) | copy-start | bytes 3076
  0.6 39.7 %collective-permute-start.7 = (f32[64,2048]{1,0:T(8,128)}, f32[64,2048]{1,0:T(8,128)S(1)}, u32[]{:S(2)}, u32[]{:S(2)}) collective-permute-start(f32[64,2048]{1,0:T(8,128)} %bitcast.6), channel_id=1, source_target_pairs={{0,1},{1,0},{2,3},{3,2},{4,5},{5,4},{6,7},{7,6},{8,9},{9,8},{10,11... | collective-permute-start | bytes 1572872 | tf_op jit(solution)/shard_map/ppermute | solution.py:312
  1.2 28.6 %collective-permute-start.6 = (f32[64,2048]{1,0:T(8,128)}, f32[64,2048]{1,0:T(8,128)S(1)}, u32[]{:S(2)}, u32[]{:S(2)}) collective-permute-start(f32[64,2048]{1,0:T(8,128)} %bitcast.7), channel_id=1, source_target_pairs={{0,2},{1,3},{2,0},{3,1},{4,6},{5,7},{6,4},{7,5},{8,10},{9,11},{10,... | collective-permute-start | bytes 1572872 | tf_op jit(solution)/shard_map/ppermute | solution.py:312
  3.8 1.1 %copy-start.1 = (f32[2048,64]{0,1:T(8,128)S(1)}, f32[2048,64]{0,1:T(8,128)}, u32[]{:S(2)}) copy-start(f32[2048,64]{0,1:T(8,128)} %param.6) | copy-start | bytes 1572868
  4.8 0.7 %copy-start.5 = (s32[256]{0:T(256)S(1)}, s32[256]{0:T(256)}, u32[]{:S(2)}) copy-start(s32[256]{0:T(256)} %pivots.3) | copy-start | bytes 3076
  5.5 8.4 %copy-start.4 = (f32[256,256]{1,0:T(8,128)S(1)}, f32[256,256]{1,0:T(8,128)}, u32[]{:S(2)}) copy-start(f32[256,256]{1,0:T(8,128)} %rest_4_.3) | copy-start | bytes 786436
  5.5 36.7 %copy-start.2 = (f32[2048,64]{0,1:T(8,128)S(1)}, f32[2048,64]{0,1:T(8,128)}, u32[]{:S(2)}) copy-start(f32[2048,64]{0,1:T(8,128)} %param.6) | copy-start | bytes 1572868
  9.3 5.9 %collective-permute-start = (f32[64,256]{1,0:T(8,128)S(1)}, f32[64,256]{1,0:T(8,128)S(1)}, u32[]{:S(2)}, u32[]{:S(2)}) collective-permute-start(f32[64,256]{1,0:T(8,128)S(1)} %get-tuple-element.18), channel_id=1, source_target_pairs={{0,4},{1,5},{2,6},{3,7}} | collective-permute-start | bytes 196616 | tf_op jit(solution)/shard_map/ppermute | solution.py:316
  12.8 11.3 %collective-permute-start.9 = (f32[80,512]{1,0:T(8,128)S(1)}, f32[80,512]{1,0:T(8,128)S(1)}, u32[]{:S(2)}, u32[]{:S(2)}) collective-permute-start(f32[80,512]{1,0:T(8,128)S(1)} %get-tuple-element.26.rest_1_), channel_id=1, source_target_pairs={{0,4},{4,0},{8,12},{12,8},{16,20},{20,16},{24,28},{28,24},{1,5},{5... | collective-permute-start | bytes 491528 | tf_op jit(solution)/shard_map/ppermute | solution.py:266
  12.9 12.5 %collective-permute-start.10 = (f32[80,512]{1,0:T(8,128)S(1)}, f32[80,512]{1,0:T(8,128)S(1)}, u32[]{:S(2)}, u32[]{:S(2)}) collective-permute-start(f32[80,512]{1,0:T(8,128)S(1)} %get-tuple-element.27.rest_2_), channel_id=1, source_target_pairs={{0,8},{4,12},{8,0},{12,4},{16,24},{20,28},{24,16},{28,20},{1,9},{5... | collective-permute-start | bytes 491528 | tf_op jit(solution)/shard_map/ppermute | solution.py:266
  15.3 5.0 %collective-permute-start.1 = (f32[64,256]{1,0:T(8,128)S(1)}, f32[64,256]{1,0:T(8,128)S(1)}, u32[]{:S(2)}, u32[]{:S(2)}) collective-permute-start(f32[64,256]{1,0:T(8,128)S(1)} %broadcast_select_fusion.6), channel_id=1, source_target_pairs={{0,8},{4,12},{1,9},{5,13},{2,10},{6,14},{3,11},{7,15}} | collective-permute-start | bytes 196616 | tf_op jit(solution)/shard_map/ppermute | solution.py:316
  20.3 7.4 %collective-permute-start.11 = (f32[80,512]{1,0:T(8,128)S(1)}, f32[80,512]{1,0:T(8,128)S(1)}, u32[]{:S(2)}, u32[]{:S(2)}) collective-permute-start(f32[80,512]{1,0:T(8,128)S(1)} %get-tuple-element.28.rest_3_), channel_id=1, source_target_pairs={{0,12},{4,8},{8,4},{12,0},{16,28},{20,24},{24,20},{28,16},{1,13},{... | collective-permute-start | bytes 491528 | tf_op jit(solution)/shard_map/ppermute | solution.py:266
  24.1 5.1 %collective-permute-start.2 = (f32[64,256]{1,0:T(8,128)S(1)}, f32[64,256]{1,0:T(8,128)S(1)}, u32[]{:S(2)}, u32[]{:S(2)}) collective-permute-start(f32[64,256]{1,0:T(8,128)S(1)} %broadcast_select_fusion.7), channel_id=1, source_target_pairs={{0,16},{4,20},{8,24},{12,28},{1,17},{5,21},{9,25},{13,29},{2,18},{... | collective-permute-start | bytes 196616 | tf_op jit(solution)/shard_map/ppermute | solution.py:316
  28.5 8.3 %collective-permute-start.12 = (f32[80,512]{1,0:T(8,128)}, f32[80,512]{1,0:T(8,128)}, u32[]{:S(2)}, u32[]{:S(2)}) collective-permute-start(f32[80,512]{1,0:T(8,128)} %get-tuple-element.39), channel_id=1, source_target_pairs={{0,16},{4,20},{8,24},{12,28},{16,0},{20,4},{24,8},{28,12},{1,17},{... | collective-permute-start | bytes 491528 | tf_op jit(solution)/shard_map/ppermute | solution.py:266
  29.2 4.3 %collective-permute-start.3 = (f32[64,256]{1,0:T(8,128)S(1)}, f32[64,256]{1,0:T(8,128)S(1)}, u32[]{:S(2)}, u32[]{:S(2)}) collective-permute-start(f32[64,256]{1,0:T(8,128)S(1)} %broadcast_select_fusion.8.rest_0_), channel_id=1, source_target_pairs={{0,2},{1,3},{2,0},{3,1},{4,6},{5,7},{6,4},{7,5},{8,10},{9,11},{10,... | collective-permute-start | bytes 196616 | tf_op jit(solution)/shard_map/ppermute | solution.py:324
  29.8 10.6 %collective-permute-start.8 = (f32[64,2048]{1,0:T(8,128)S(1)}, f32[64,2048]{1,0:T(8,128)S(1)}, u32[]{:S(2)}, u32[]{:S(2)}) collective-permute-start(f32[64,2048]{1,0:T(8,128)S(1)} %collective-permute-done.6.rest_1_), channel_id=1, source_target_pairs={{0,1},{1,0},{2,3},{3,2},{4,5},{5,4},{6,7},{7,6},{8,9},{9,8},{10,11... | collective-permute-start | bytes 1572872 | tf_op jit(solution)/shard_map/ppermute | solution.py:312
  30.6 13.6 %collective-permute-start.4 = (f32[64,256]{1,0:T(8,128)S(1)}, f32[64,256]{1,0:T(8,128)S(1)}, u32[]{:S(2)}, u32[]{:S(2)}) collective-permute-start(f32[64,256]{1,0:T(8,128)S(1)} %broadcast_select_fusion.8.rest_0_), channel_id=1, source_target_pairs={{0,1},{1,0},{2,3},{3,2},{4,5},{5,4},{6,7},{7,6},{8,9},{9,8},{10,11... | collective-permute-start | bytes 196616 | tf_op jit(solution)/shard_map/ppermute | solution.py:324
  33.5 10.7 %collective-permute-start.5 = (f32[64,256]{1,0:T(8,128)S(1)}, f32[64,256]{1,0:T(8,128)S(1)}, u32[]{:S(2)}, u32[]{:S(2)}) collective-permute-start(f32[64,256]{1,0:T(8,128)S(1)} %collective-permute-done.3.rest_1_), channel_id=1, source_target_pairs={{0,1},{1,0},{2,3},{3,2},{4,5},{5,4},{6,7},{7,6},{8,9},{9,8},{10,11... | collective-permute-start | bytes 196616 | tf_op jit(solution)/shard_map/ppermute | solution.py:324
  37.8 8.8 %copy-start = (f32[2048,512]{1,0:T(8,128)S(1)}, f32[2048,512]{1,0:T(8,128)}, u32[]{:S(2)}) copy-start(f32[2048,512]{1,0:T(8,128)} %look.3) | copy-start | bytes 12582916
  37.8 8.8 %copy-start.3 = (f32[256,256]{1,0:T(8,128)S(1)}, f32[256,256]{1,0:T(8,128)}, u32[]{:S(2)}) copy-start(f32[256,256]{1,0:T(8,128)} %lower.1) | copy-start | bytes 786436
  37.8 8.7 %collective-permute-start.15 = (f32[80,512]{1,0:T(8,128)S(1)}, f32[80,512]{1,0:T(8,128)S(1)}, u32[]{:S(2)}, u32[]{:S(2)}) collective-permute-start(f32[80,512]{1,0:T(8,128)S(1)} %get-tuple-element.33), channel_id=1, source_target_pairs={{0,12},{4,8},{8,4},{12,0},{16,28},{20,24},{24,20},{28,16},{1,13},{... | collective-permute-start | bytes 491528 | tf_op jit(solution)/shard_map/ppermute | solution.py:266
  40.3 6.3 %collective-permute-start.14 = (f32[80,512]{1,0:T(8,128)S(1)}, f32[80,512]{1,0:T(8,128)S(1)}, u32[]{:S(2)}, u32[]{:S(2)}) collective-permute-start(f32[80,512]{1,0:T(8,128)S(1)} %get-tuple-element.50), channel_id=1, source_target_pairs={{0,8},{4,12},{8,0},{12,4},{16,24},{20,28},{24,16},{28,20},{1,9},{5... | collective-permute-start | bytes 491528 | tf_op jit(solution)/shard_map/ppermute | solution.py:266
  40.4 6.2 %collective-permute-start.13 = (f32[80,512]{1,0:T(8,128)S(1)}, f32[80,512]{1,0:T(8,128)S(1)}, u32[]{:S(2)}, u32[]{:S(2)}) collective-permute-start(f32[80,512]{1,0:T(8,128)S(1)} %get-tuple-element.51), channel_id=1, source_target_pairs={{0,4},{4,0},{8,12},{12,8},{16,20},{20,16},{24,28},{28,24},{1,5},{5... | collective-permute-start | bytes 491528 | tf_op jit(solution)/shard_map/ppermute | solution.py:266
